TPU v7x, 128 devices: a whole 4x4x4 slice. The times are simulated.
128 devices in a mesh: dp: 64 (over y, z_lo, x, core), seq: 2 (over z_hi).
Axes of the slice: x: 4, y: 4, z: 4 (z_hi: 2, z_lo: 2; z = z_hi * 2 + z_lo), core: 2. Of those that a mesh axis runs over, the one named last changes fastest.
Arguments:
- hidden_in: bfloat16 [65536, 2048], P(('dp', 'seq')), may hold values from -6 to 6
- norm_gain: float32 [2048], replicated, may hold values from 0.1 to 1.9
- w_qk: bfloat16 [2048, 3072], P(('dp', 'seq')), may hold values from -1 to 1
- w_v: bfloat16 [2048, 1024], P(('dp', 'seq')), may hold values from -0.125 to 0.125
- w_o: bfloat16 [2048, 2048], P(('dp', 'seq')), may hold values from -0.125 to 0.125
- prompt_pages: int32 [64], replicated, may hold values from 1 to 17, 512 in all
- last_fill: int32 [64], replicated, may hold values from 1 to 128
- page_slots: int32 [512], P('dp'), may hold values from 0 to 7, as said below
Outputs:
- attended: bfloat16 [65536, 2048], P(('dp', 'seq'))
- key_cache: bfloat16 [512, 128, 1024], P(('dp', 'seq'))
- value_cache: bfloat16 [512, 128, 1024], P(('dp', 'seq'))
Inputs may be any that keep to these rules, and one draw needn't show every extreme that they name: `prompt_pages`: the prompts' pages lie end to end from position 0 and add up to 512. `page_slots`: each aligned run of 8 entries is a permutation of 0 to 7.
All inputs are finite; a program needn't handle non-finite values.
Results may differ from a plain program's by a relative error of at most 0.01.
The roundings to bfloat16 on the way count: a program that leaves them out, or rounds other values in their place, can miss the bound.
Values may be sent and summed in bfloat16 or wider, within the bound.
No kernel may reach another device: no remote copies, remote signals or barrier semaphores. Data moves between devices by JAX's collectives and lax.ppermute only.
A program may use at most 192 MiB of HBM per device.

v0:
```python
import functools
import math

import jax
import jax.numpy as jnp
from jax import lax
from jax.experimental import pallas as pl
from jax.experimental.pallas import tpu as pltpu
from jax.sharding import Mesh, PartitionSpec as P


AXES = ("y", "zl", "x", "c", "zh")
SIZES = (4, 2, 4, 2, 2)
QUAD = ("c", "zh")
DEPTH = 2048
TOK = 512
PAGE = 128
QTOK = 4 * TOK
QPAGES = QTOK // PAGE
CHUNK = 256
THETA = 1000000.0
EPS = 1e-05
NEG = -1e30
BF = jnp.bfloat16
INSIDE = pl.BlockSpec(memory_space=pltpu.VMEM)
F32 = jnp.float32


def swap(block, axis):
    return lax.ppermute(block, axis, [(0, 1), (1, 0)])


def shift(block, axis, distance):
    return lax.ppermute(block, axis, [(i, (i + distance) % 4) for i in range(4)])


def to_role(block, flip):
    return lax.ppermute(block, QUAD, [(i, i ^ flip) for i in range(4)])


def ring_pieces(block, axis):
    pieces = [block]
    for distance in (1, 2, 3):
        pieces.append(shift(block, axis, distance))
    return pieces


def slices_kernel(here, qk_ref, v_ref, o_ref, out_ref):
    for role in range(4):
        for copy in (role, role + 4):
            out_ref[copy, :, :512] = qk_ref[:, 512 * role : 512 * role + 512]
            first = 2048 + 256 * role
            out_ref[copy, :, 512:768] = qk_ref[:, first : first + 256]
            out_ref[copy, :, 768:1024] = v_ref[:, 256 * role : 256 * role + 256]
            first = 1024 * (role // 2)
            out_ref[copy, :, 1024:] = o_ref[:, first : first + 1024]


def split_kernel(here, level_ref, kv_ref, rest_ref):
    kv_ref[...] = level_ref[:, :, 512:1024]
    rest_ref[:, :, :512] = level_ref[:, :, :512]
    rest_ref[:, :, 512:] = level_ref[:, :, 1024:]


def arrange_kernel(here, *refs):
    pieces, outs = refs[:4], refs[4:]
    for k in range(4):
        place = lax.rem(here[2] + 4 - k, 4)
        first = 0
        for out_ref in outs:
            width = out_ref.shape[3]
            out_ref[:, place] = pieces[k][:, :, first : first + width]
            first += width


def tick_kernel(in_ref, out_ref):
    for i in range(51):
        out_ref[i] = in_ref[i]


def tick(meta):
    scalars = pl.BlockSpec(memory_space=pltpu.SMEM)
    return pl.pallas_call(
        tick_kernel,
        in_specs=[scalars],
        out_specs=scalars,
        out_shape=jax.ShapeDtypeStruct((51,), jnp.int32),
        name="tick",
    )(meta)


def small(kernel, here, operands, shapes):
    return pl.pallas_call(
        kernel,
        grid_spec=pltpu.PrefetchScalarGridSpec(
            num_scalar_prefetch=1,
            grid=(),
            in_specs=[INSIDE] * len(operands),
            out_specs=[INSIDE] * len(shapes),
        ),
        out_shape=[jax.ShapeDtypeStruct(shape, BF) for shape in shapes],
        compiler_params=pltpu.CompilerParams(vmem_limit_bytes=20 << 20),
    )(here, *operands)


def after(block, *others):
    return lax.optimization_barrier((block, *others))[0]


def normalize(hidden_in, norm_gain):
    values = hidden_in.astype(F32)
    scale = lax.rsqrt(jnp.mean(values * values, axis=-1, keepdims=True) + EPS)
    return (values * scale * norm_gain[None, :]).astype(BF)


def page_tables(prompt_pages, last_fill, first_page):
    count = prompt_pages.shape[0]
    order = jnp.arange(count, dtype=jnp.int32)
    ends = jnp.sum(
        jnp.where(order[None, :] <= order[:, None], prompt_pages[None, :], 0), axis=1
    )
    pages = first_page + jnp.arange(QPAGES, dtype=jnp.int32)
    before = ends[None, :] <= pages[:, None]
    start = jnp.max(jnp.where(before, ends[None, :], 0), axis=1)
    closing = ends[None, :] == pages[:, None] + 1
    short = jnp.sum(jnp.where(closing, PAGE - last_fill[None, :], 0), axis=1)
    return pages - start, PAGE - short


def rotation_tables(offset):
    row = jnp.arange(PAGE, dtype=jnp.int32)
    position = (offset[:, None] * PAGE + row[None, :]).reshape(QTOK)
    half = 64
    freq = jnp.power(THETA, -2.0 * jnp.arange(half, dtype=F32) / 128)
    angle = position.astype(F32)[:, None] * freq[None, :]
    cosine, sine = jnp.cos(angle), jnp.sin(angle)
    return (
        jnp.concatenate([cosine, cosine], axis=-1),
        jnp.concatenate([-sine, sine], axis=-1),
    )


def project_kernel(store, meta, *refs):
    x_refs, parts, tables, out_refs = refs[:2], refs[2:6], refs[6:8], refs[8:]
    step = pl.program_id(0)
    cosine = tables[0][...]
    sine = tables[1][...]

    def turned(block):
        return (block * cosine + pltpu.roll(block, 64, 1) * sine).astype(BF)

    def body(x_ref):
        result = jnp.zeros((x_ref.shape[0], 512), F32)
        for i in range(4):
            start = pl.multiple_of(lax.rem(meta[49] + 4 - i, 4) * 512, 512)
            result += jnp.dot(
                x_ref[:, pl.ds(start, 512)],
                parts[i][...].reshape(512, 512),
                preferred_element_type=F32,
            )
        store(result, turned, *out_refs)

    @pl.when(step < 2)
    def _():
        body(x_refs[0])

    @pl.when(step >= 2)
    def _():
        body(x_refs[1])


def store_queries(result, turned, q_ref):
    for head in range(4):
        lanes = slice(128 * head, 128 * head + 128)
        q_ref[:, lanes] = turned(result[:, lanes])


def store_keys(result, turned, kvt_ref, v_ref):
    for head in range(2):
        kvt_ref[head] = turned(result[:, 128 * head : 128 * head + 128])
        value = result[:, 256 + 128 * head : 384 + 128 * head]
        v_ref[head] = value.astype(BF)
        for page in range(result.shape[0] // PAGE):
            rows = slice(PAGE * page, PAGE * page + PAGE)
            kvt_ref[2 + head, rows, :] = jnp.transpose(value[rows]).astype(BF)


def project(meta, sides, parts, tables, pair, kind):
    tile = 256

    def table(i, m):
        return (jnp.bitwise_xor(m[0], 2 * (i // 2) + pair) * 2 + i % 2, 0)

    if kind == "q":
        store = store_queries
        out_specs = [pl.BlockSpec((tile, 512), lambda i, m: (i, 0))]
        out_shape = [jax.ShapeDtypeStruct((2 * TOK, 512), BF)]
    else:
        store = store_keys
        out_specs = [
            pl.BlockSpec((4, tile, 128), lambda i, m: (0, i, 0)),
            pl.BlockSpec((2, tile, 128), lambda i, m: (0, i, 0)),
        ]
        out_shape = [
            jax.ShapeDtypeStruct((4, 2 * TOK, 128), BF),
            jax.ShapeDtypeStruct((2, 2 * TOK, 128), BF),
        ]
    return pl.pallas_call(
        functools.partial(project_kernel, store),
        grid_spec=pltpu.PrefetchScalarGridSpec(
            num_scalar_prefetch=1,
            grid=(4,),
            in_specs=[
                pl.BlockSpec((tile, DEPTH), lambda i, m: (jnp.minimum(i, 1), 0)),
                pl.BlockSpec((tile, DEPTH), lambda i, m: (jnp.maximum(i - 2, 0), 0)),
            ]
            + [INSIDE] * 4
            + [pl.BlockSpec((tile, 128), table)] * 2,
            out_specs=out_specs,
        ),
        out_shape=out_shape,
        compiler_params=pltpu.CompilerParams(vmem_limit_bytes=40 << 20),
        cost_estimate=pl.CostEstimate(
            flops=4 * TOK * DEPTH * 512, transcendentals=0, bytes_accessed=8 << 20
        ),
    )(meta, *sides, *parts, *tables)


def attend_kernel(pair, meta, *refs):
    q_ref, own, halo, out_ref, kvt, saved, bias = (
        refs[0], refs[1:3], refs[3:5], *refs[5:]
    )
    role = meta[0]
    for p in range(4):
        block = jnp.bitwise_xor(role, 2 * (p % 2) + p // 2)
        source = slice((p % 2) * TOK, (p % 2) * TOK + TOK)
        for at, side in ((0, halo), (4, own)):
            rows = pl.ds(pl.multiple_of((block + at) * TOK, TOK), TOK)
            kvt[:, rows, :] = side[p // 2][:, source, :]
    kvt[:, pl.ds(2 * QTOK, CHUNK), :] = jnp.zeros((4, CHUNK, 128), BF)
    gap = lax.broadcasted_iota(jnp.int32, (CHUNK, 256), 0) - (
        lax.broadcasted_iota(jnp.int32, (CHUNK, 256), 1) % PAGE
    )
    for i in range(2):
        bias[i] = jnp.where(gap <= i * PAGE, 0.0, NEG)
    factor = (1.0 / math.sqrt(128)) * math.log2(math.e)
    tall = lax.broadcasted_iota(jnp.int32, (PAGE, 128), 0)

    def one_page(index, carry):
        rows = pl.ds(pl.multiple_of(index * PAGE, PAGE), PAGE)
        page = jnp.bitwise_xor(role, 2 * (index // 4) + pair) * 4 + index % 4
        offset = meta[1 + page]
        live = meta[17 + page]
        low = QPAGES + page - offset
        full = offset // 2
        stack = [
            jnp.concatenate(
                [
                    q_ref[rows, 256 * h : 256 * h + 128],
                    q_ref[rows, 256 * h + 128 : 256 * h + 256],
                ],
                axis=0,
            )
            for h in range(2)
        ]

        def scan(chunk, tops, count, masked):
            base = pl.multiple_of((low + 2 * chunk) * PAGE, PAGE)
            result = []
            for h in range(2):
                scores = lax.dot_general(
                    kvt[h, pl.ds(base, count * CHUNK), :],
                    stack[h],
                    (((1,), (1,)), ((), ())),
                    preferred_element_type=F32,
                )
                if masked:
                    scores = scores + bias[offset % 2]
                for i in range(count):
                    saved[h, chunk + i] = scores[CHUNK * i : CHUNK * i + CHUNK]
                peak = jnp.max(scores.reshape(count * CHUNK // 8, 8, 256), axis=0)
                result.append(jnp.maximum(tops[h], peak))
            return tuple(result)

        tops = (jnp.full((8, 256), NEG, F32),) * 2
        tops = lax.fori_loop(
            0, full // 2, lambda i, t: scan(2 * i, t, 2, False), tops
        )
        tops = lax.fori_loop(
            full // 2 * 2, full, lambda i, t: scan(i, t, 1, False), tops
        )
        tops = scan(full, tops, 1, True)
        tops = [jnp.max(top, axis=0, keepdims=True) for top in tops]

        def fold(chunk, state, count):
            result = []
            for h in range(2):
                total, acc = state[h]
                parts, weights = [], []
                for i in range(count):
                    expo = jnp.exp2((saved[h, chunk + i] - tops[h]) * factor)
                    total = total + jnp.sum(expo.reshape(CHUNK // 8, 8, 256), axis=0)
                    weights.append(expo.astype(BF))
                for i in range(2 * count):
                    at = pl.multiple_of((low + 2 * chunk + i) * PAGE, PAGE)
                    parts.append(kvt[2 + h, pl.ds(at, PAGE), :])
                acc = acc + jnp.dot(
                    jnp.concatenate(parts, axis=1),
                    jnp.concatenate(weights, axis=0),
                    preferred_element_type=F32,
                )
                result.append((total, acc))
            return tuple(result)

        state = ((jnp.zeros((8, 256), F32), jnp.zeros((128, 256), F32)),) * 2
        count = full + 1
        state = lax.fori_loop(0, count // 2, lambda i, s: fold(2 * i, s, 2), state)
        state = lax.fori_loop(
            count // 2 * 2, count, lambda i, s: fold(i, s, 1), state
        )
        for h in range(2):
            total, acc = state[h]
            value = acc / jnp.sum(total, axis=0, keepdims=True)
            value = jnp.transpose(value)
            for g in range(2):
                part = value[128 * g : 128 * g + 128]
                part = jnp.where(tall < live, part, 0.0)
                at_lane = 256 * h + 128 * g
                out_ref[rows, at_lane : at_lane + 128] = part.astype(BF)
        return carry

    lax.fori_loop(0, 8, one_page, 0)


def attend(meta, queries, own, halo, pair):
    return pl.pallas_call(
        functools.partial(attend_kernel, pair),
        grid_spec=pltpu.PrefetchScalarGridSpec(
            num_scalar_prefetch=1,
            grid=(),
            in_specs=[INSIDE] * 5,
            out_specs=INSIDE,
            scratch_shapes=[
                pltpu.VMEM((4, 2 * QTOK + CHUNK, 128), BF),
                pltpu.VMEM((2, 9, CHUNK, 256), F32),
                pltpu.VMEM((2, CHUNK, 256), F32),
            ],
        ),
        out_shape=jax.ShapeDtypeStruct((2 * TOK, 512), BF),
        compiler_params=pltpu.CompilerParams(vmem_limit_bytes=40 << 20),
        cost_estimate=pl.CostEstimate(
            flops=4 << 30, transcendentals=4 << 20, bytes_accessed=6 << 20
        ),
    )(meta, queries, *own, *halo)


def pack_kernel(meta, *refs):
    keys, values, out_refs, kv = refs[:2], refs[2:4], refs[4:8], refs[8]
    role = meta[0]
    for p in range(4):
        block = jnp.bitwise_xor(role, 2 * (p % 2) + p // 2)
        rows = pl.ds(pl.multiple_of(block * TOK, TOK), TOK)
        source = slice((p % 2) * TOK, (p % 2) * TOK + TOK)
        kv[:2, rows, :] = keys[p // 2][:2, source, :]
        kv[2:, rows, :] = values[p // 2][:, source, :]
    tall = lax.broadcasted_iota(jnp.int32, (PAGE, 128), 0)
    for p in range(4):
        target = jnp.bitwise_xor(role, p)
        for slot in range(4):
            page = meta[33 + target * 4 + slot]
            live = meta[17 + page]
            rows = pl.ds(pl.multiple_of(page * PAGE, PAGE), PAGE)
            for part in range(4):
                block = jnp.where(tall < live, kv[part, rows, :].astype(F32), 0.0)
                lanes = slice(128 * part, 128 * part + 128)
                out_refs[p][PAGE * slot : PAGE * slot + PAGE, lanes] = block.astype(BF)


def pack(meta, keys, values):
    return pl.pallas_call(
        pack_kernel,
        grid_spec=pltpu.PrefetchScalarGridSpec(
            num_scalar_prefetch=1,
            grid=(),
            in_specs=[INSIDE] * 4,
            out_specs=[INSIDE] * 4,
            scratch_shapes=[pltpu.VMEM((4, QTOK, 128), BF)],
        ),
        out_shape=[jax.ShapeDtypeStruct((TOK, 512), BF)] * 4,
        compiler_params=pltpu.CompilerParams(vmem_limit_bytes=30 << 20),
        name="pack_pages",
    )(meta, *keys, *values)


def unpack_kernel(meta, *refs):
    in_refs, key_ref, value_ref = refs[:4], refs[4], refs[5]
    step = pl.program_id(0)
    for p in range(4):

        @pl.when(step == p)
        def _(p=p):
            key_ref[...] = in_refs[p][:, :256]
            value_ref[...] = in_refs[p][:, 256:]


def unpack(meta, received):
    whole = pl.BlockSpec((TOK, 512), lambda i, m: (0, 0))
    column = pl.BlockSpec((TOK, 256), lambda i, m: (0, jnp.bitwise_xor(m[0], i)))
    return pl.pallas_call(
        unpack_kernel,
        grid_spec=pltpu.PrefetchScalarGridSpec(
            num_scalar_prefetch=1,
            grid=(4,),
            in_specs=[whole] * 4,
            out_specs=[column] * 2,
        ),
        out_shape=[jax.ShapeDtypeStruct((TOK, 1024), BF)] * 2,
        compiler_params=pltpu.CompilerParams(vmem_limit_bytes=30 << 20),
        name="unpack_pages",
    )(meta, *received)


def output_kernel(meta, *refs):
    in_refs, weights, out_ref = refs[:4], refs[4:6], refs[6]
    step = pl.program_id(0)
    for half in range(2):

        @pl.when(step == half)
        def _(half=half):
            total = jnp.zeros((TOK, 1024), F32)
            for p in range(4):
                block = jnp.bitwise_xor(meta[0], p)
                total += jnp.dot(
                    in_refs[p][...],
                    weights[half][lax.rem(meta[49] + 4 - block, 4)].reshape(512, 1024),
                    preferred_element_type=F32,
                )
            out_ref[...] = total.astype(BF)


def output(meta, received, own_half, other_half):
    whole = pl.BlockSpec((TOK, 512), lambda i, m: (0, 0))
    return pl.pallas_call(
        output_kernel,
        grid_spec=pltpu.PrefetchScalarGridSpec(
            num_scalar_prefetch=1,
            grid=(2,),
            in_specs=[whole] * 4 + [INSIDE] * 2,
            out_specs=pl.BlockSpec(
                (TOK, 1024), lambda i, m: (0, jnp.bitwise_xor(m[0] // 2, i))
            ),
        ),
        out_shape=jax.ShapeDtypeStruct((TOK, DEPTH), BF),
        compiler_params=pltpu.CompilerParams(vmem_limit_bytes=48 << 20),
        name="output_rows",
    )(meta, *received, own_half, other_half)


def page_sources(page_slots, core):
    other = swap(page_slots, "c")
    first = jnp.where(core == 0, page_slots, other)
    second = jnp.where(core == 0, other, page_slots)
    slots = jnp.stack([first, second])
    wanted = jnp.arange(8, dtype=jnp.int32)
    hit = slots[:, None, :] == wanted[None, :, None]
    found = jnp.sum(jnp.where(hit, wanted[None, None, :], 0), axis=2)
    return (found + jnp.array([[0], [8]], jnp.int32)).reshape(16)


def previous_quad(block):
    names = ("y", "zl", "x", "c", "zh")
    route = [(i, i + 4) for i in range(124)]
    return lax.ppermute(block, names, route)


def shards(hidden_in, norm_gain, w_qk, w_v, w_o, prompt_pages, last_fill, page_slots):
    core = lax.axis_index("c")
    role = core * 2 + lax.axis_index("zh")
    y, x = lax.axis_index("y"), lax.axis_index("x")
    quad = (y * 2 + lax.axis_index("zl")) * 4 + x

    here = jnp.stack([role, y, x]).astype(jnp.int32)

    slices = small(slices_kernel, here, (w_qk, w_v, w_o), [(8, 16, 2048)])[0]
    level = lax.all_to_all(
        slices, ("zl", "c", "zh"), split_axis=0, concat_axis=0, tiled=True
    ).reshape(2, 64, 2048)
    kv_level, rest = small(split_kernel, here, (level,), [(2, 64, 512), (2, 64, 1536)])
    kv_row = small(
        arrange_kernel, here, ring_pieces(kv_level, "x"), [(2, 4, 64, 512)]
    )[0]
    kv_parts = ring_pieces(kv_row, "y")
    q_row, o_row = small(
        arrange_kernel,
        here,
        ring_pieces(after(rest, kv_row), "x"),
        [(2, 4, 64, 512), (2, 4, 64, 1024)],
    )
    q_parts = ring_pieces(q_row, "y")
    o_parts = ring_pieces(o_row, "y")

    normed = normalize(after(hidden_in, slices), norm_gain)
    beside = swap(normed, "c")
    across = swap(after(normed, level), "zh")
    diagonal = swap(across, "c")

    offset, live = page_tables(prompt_pages, last_fill, quad * QPAGES)
    sources = page_sources(page_slots, core)
    meta = jnp.concatenate(
        [role[None], offset, live, sources, y[None], x[None]]
    ).astype(jnp.int32)
    tables = rotation_tables(offset)

    sides = ((normed, beside), (across, diagonal))
    keys, values, halo, queries = [], [], [], []
    for pair in range(2):
        kvt, v = project(meta, sides[pair], kv_parts, tables, pair, "kv")
        keys.append(kvt)
        values.append(v)
        halo.append(previous_quad(kvt))
    later = after(tick(meta), *keys)
    for pair in range(2):
        queries += project(later, sides[pair], q_parts, tables, pair, "q")
    packed = pack(meta, keys, values)
    pages = [packed[0]]
    for flip in (1, 2, 3):
        pages.append(to_role(packed[flip], flip))

    far = attend(meta, queries[1], keys, halo, 1)
    far = swap(far, "zh")
    near = attend(meta, queries[0], keys, halo, 0)
    own_half = jnp.stack(o_parts)
    other_half = swap(own_half, "c")
    received = [near, far, swap(near[TOK:], "c"), swap(far[TOK:], "c")]
    attended = output(meta, received, own_half, other_half)
    key_cache, value_cache = unpack(meta, pages)
    return (
        attended,
        key_cache.reshape(4, PAGE, 1024),
        value_cache.reshape(4, PAGE, 1024),
    )


def solution(mesh):
    fine = Mesh(mesh.devices.reshape(SIZES), AXES)
    rows = P(AXES, None)
    in_specs = (rows, P(), rows, rows, rows, P(), P(), P(("y", "zl", "x", "c")))
    out_specs = (rows, P(AXES, None, None), P(AXES, None, None))
    return jax.shard_map(
        shards, mesh=fine, in_specs=in_specs, out_specs=out_specs, check_vma=False
    )
```

profile of v0, /device:TPU:33, one launch (start us, length us, event | category | flops | bytes accessed | tf_op | source)
XLA Modules:
  0.0 299.1 jit_solution(12423026638073092838)
XLA Ops:
  4.6 5.7 %all-to-all-start = ((bf16[8,16,2048]{2,1,0:T(8,128)(2,1)}), bf16[8,16,2048]{2,1,0:T(8,128)(2,1)S(1)}, u32[]{:S(2)}, u32[]{:S(2)}) async-start(bf16[8,16,2048]{2,1,0:T(8,128)(2,1)} %shard_map.112), calls=%async_computation | async-start | bytes 1048576 | tf_op jit(solution)/shard_map/all_to_all | solution.py:485
  15.0 3.3 %all-to-all-done = bf16[8,16,2048]{2,1,0:T(8,128)(2,1)S(1)} async-done(((bf16[8,16,2048]{2,1,0:T(8,128)(2,1)}), bf16[8,16,2048]{2,1,0:T(8,128)(2,1)S(1)}, u32[]{:S(2)}, u32[]{:S(2)}) %all-to-all-start) | async-done | bytes 524320 | tf_op jit(solution)/shard_map/all_to_all | solution.py:485
  27.5 3.8 %collective-permute-done.3.refs_2_ = bf16[2,64,512]{2,1,0:T(8,128)(2,1)S(1)} collective-permute-done((bf16[2,64,512]{2,1,0:T(8,128)(2,1)S(1)}, bf16[2,64,512]{2,1,0:T(8,128)(2,1)S(1)}, u32[]{:S(2)}, u32[]{:S(2)}) %collective-permute-start.3) | collective-permute-done | bytes 131104 | tf_op jit(solution)/shard_map/ppermute | solution.py:34
  36.3 6.7 %collective-permute-done.10.refs_1_ = bf16[2,64,1536]{2,1,0:T(8,128)(2,1)S(1)} collective-permute-done((bf16[2,64,1536]{2,1,0:T(8,128)(2,1)S(1)}, bf16[2,64,1536]{2,1,0:T(8,128)(2,1)S(1)}, u32[]{:S(2)}, u32[]{:S(2)}) %collective-permute-start.10) | collective-permute-done | bytes 393248 | tf_op jit(solution)/shard_map/ppermute | solution.py:34
  42.9 9.0 %collective-permute-done.11.refs_2_ = bf16[2,64,1536]{2,1,0:T(8,128)(2,1)S(1)} collective-permute-done((bf16[2,64,1536]{2,1,0:T(8,128)(2,1)S(1)}, bf16[2,64,1536]{2,1,0:T(8,128)(2,1)S(1)}, u32[]{:S(2)}, u32[]{:S(2)}) %collective-permute-start.11) | collective-permute-done | bytes 393248 | tf_op jit(solution)/shard_map/ppermute | solution.py:34
  57.6 9.9 %collective-permute-done.8.refs_0_ = bf16[512,2048]{1,0:T(8,128)(2,1)} collective-permute-done((bf16[512,2048]{1,0:T(8,128)(2,1)}, bf16[512,2048]{1,0:T(8,128)(2,1)}, u32[]{:S(2)}, u32[]{:S(2)}) %collective-permute-start.8) | collective-permute-done | bytes 2097184 | tf_op jit(solution)/shard_map/ppermute | solution.py:30
  68.1 3.7 %fusion.3 = (f32[2048,64]{1,0:T(8,128)S(1)}, f32[2048,64]{1,0:T(8,128)S(1)}, f32[2048,64]{1,0:T(8,128)S(1)}) fusion(f32[64]{0:T(128)S(1)} %multiply_power_fusion, f32[2048]{0:T(1024)S(1)} %convert_bitcast_fusion), kind=kLoop, calls=%fused_computation.10 | loop fusion | flops 262144 | bytes 1581312 | tf_op jit(solution)/shard_map/neg | solution.py:139
  72.5 6.3 %collective-permute-done.23 = bf16[2,4,64,1024]{3,2,1,0:T(8,128)(2,1)} collective-permute-done((bf16[2,4,64,1024]{3,2,1,0:T(8,128)(2,1)}, bf16[2,4,64,1024]{3,2,1,0:T(8,128)(2,1)}, u32[]{:S(2)}, u32[]{:S(2)}) %collective-permute-start.23) | collective-permute-done | bytes 1048608 | tf_op jit(solution)/shard_map/ppermute | solution.py:34
  81.4 21.4 %collective-permute-start = (s32[8]{0:T(128)S(1)}, s32[8]{0:T(128)S(1)}, u32[]{:S(2)}, u32[]{:S(2)}) collective-permute-start(s32[8]{0:T(128)S(1)} %copy-done.16), channel_id=1, source_target_pairs={{0,2},{2,0},{1,3},{3,1},{4,6},{6,4},{5,7},{7,5},{8,10},{10,8},{9,1... | collective-permute-start | bytes 104 | tf_op jit(solution)/shard_map/ppermute | solution.py:30
  106.0 3.8 %pad_maximum_fusion.refs_4_ = bf16[4,2,4,64,1024]{4,3,2,1,0:T(8,128)(2,1)} fusion(bf16[1,2,4,64,1024]{4,3,2,1,0:T(8,128)(2,1)} %bitcast.10, bf16[1,2,4,64,1024]{4,3,2,1,0:T(8,128)(2,1)} %bitcast.9, bf16[1,2,4,64,1024]{4,3,2,1,0:T(8,128)(2,1)} %bitcast.8, bf16[1,2,4,64,1024]{4,3,2,1,0:T(8,128)(2,1)} %bitcast.7), kind=kLoop, calls=%fused_computation.5 | loop fusion | flops 6291456 | bytes 8388608 | tf_op jit(solution)/shard_map/stack | solution.py:532
  111.8 5.0 %collective-permute-done.5.refs_3_ = bf16[2,4,64,512]{3,2,1,0:T(8,128)(2,1)} collective-permute-done((bf16[2,4,64,512]{3,2,1,0:T(8,128)(2,1)S(1)}, bf16[2,4,64,512]{3,2,1,0:T(8,128)(2,1)}, u32[]{:S(2)}, u32[]{:S(2)}) %collective-permute-start.5) | collective-permute-done | bytes 524320 | tf_op jit(solution)/shard_map/ppermute | solution.py:34
  117.2 8.7 %collective-permute-done.6.refs_4_ = bf16[2,4,64,512]{3,2,1,0:T(8,128)(2,1)} collective-permute-done((bf16[2,4,64,512]{3,2,1,0:T(8,128)(2,1)S(1)}, bf16[2,4,64,512]{3,2,1,0:T(8,128)(2,1)}, u32[]{:S(2)}, u32[]{:S(2)}) %collective-permute-start.6) | collective-permute-done | bytes 524320 | tf_op jit(solution)/shard_map/ppermute | solution.py:34
  126.5 10.2 %collective-permute-done.7.refs_5_ = bf16[2,4,64,512]{3,2,1,0:T(8,128)(2,1)} collective-permute-done((bf16[2,4,64,512]{3,2,1,0:T(8,128)(2,1)S(1)}, bf16[2,4,64,512]{3,2,1,0:T(8,128)(2,1)}, u32[]{:S(2)}, u32[]{:S(2)}) %collective-permute-start.7) | collective-permute-done | bytes 524320 | tf_op jit(solution)/shard_map/ppermute | solution.py:34
  136.7 7.3 %shard_map.115 = (bf16[4,1024,128]{2,1,0:T(8,128)(2,1)}, bf16[2,1024,128]{2,1,0:T(8,128)(2,1)S(1)}) custom-call(s32[51]{0:T(128)S(1)} %concatenate.9.in_ref.meta, bf16[512,2048]{1,0:T(8,128)(2,1)} %fusion.2.refs_0_, bf16[512,2048]{1,0:T(8,128)(2,1)} %collective-permute-done.1.refs_1_, bf16[2,4,64,512]{3,2,1,0:T(8,128)(2,1)S(1)} %shard_map.114.refs_2_, ...), custom_call_target="tpu_custom_call" | custom-call | flops 2147483648 | bytes 8388608 | tf_op jit(solution)/shard_map/pallas_call | solution.py:208
  146.9 7.3 %shard_map.116 = (bf16[4,1024,128]{2,1,0:T(8,128)(2,1)}, bf16[2,1024,128]{2,1,0:T(8,128)(2,1)S(1)}) custom-call(s32[51]{0:T(128)S(1)} %concatenate.9.in_ref.meta, bf16[512,2048]{1,0:T(8,128)(2,1)} %collective-permute-done.8.refs_0_, bf16[512,2048]{1,0:T(8,128)(2,1)} %collective-permute-done.9.refs_1_, bf16[2,4,64,512]{3,2,1,0:T(8,128)(2,1)S(1)} %shard_map.114.refs_2_, ...), custom_call_target="tpu_custom_call" | custom-call | flops 2147483648 | bytes 8388608 | tf_op jit(solution)/shard_map/pallas_call | solution.py:208
  155.0 3.6 %collective-permute-start.17 = (bf16[4,1024,128]{2,1,0:T(8,128)(2,1)}, bf16[4,1024,128]{2,1,0:T(8,128)(2,1)}, u32[]{:S(2)}, u32[]{:S(2)}) collective-permute-start(bf16[4,1024,128]{2,1,0:T(8,128)(2,1)} %get-tuple-element.25.refs_2_.refs_1_), channel_id=1, source_target_pairs={{0,4},{1,5},{2,6},{3,7},{4,8},{5,9},{6,10},{7,11},{8,12},{9,13},{1... | collective-permute-start | bytes 3145736 | tf_op jit(solution)/shard_map/ppermute | solution.py:473
  164.7 47.0 %collective-permute-done.14.refs_4_ = bf16[2,4,64,512]{3,2,1,0:T(8,128)(2,1)S(1)} collective-permute-done((bf16[2,4,64,512]{3,2,1,0:T(8,128)(2,1)S(1)}, bf16[2,4,64,512]{3,2,1,0:T(8,128)(2,1)S(1)}, u32[]{:S(2)}, u32[]{:S(2)}) %collective-permute-start.14) | collective-permute-done | bytes 524320 | tf_op jit(solution)/shard_map/ppermute | solution.py:34
  215.1 6.1 %shard_map.120.refs_0_ = bf16[1024,512]{1,0:T(8,128)(2,1)S(1)} custom-call(s32[51]{0:T(128)S(1)} %copy-done.14, bf16[512,2048]{1,0:T(8,128)(2,1)} %collective-permute-done.8.refs_0_, bf16[512,2048]{1,0:T(8,128)(2,1)} %collective-permute-done.9.refs_1_, bf16[2,4,64,512]{3,2,1,0:T(8,128)(2,1)S(1)} %get-tuple-element.29.refs_2_, ...), custom_call_target="tpu_custom_call" | custom-call | flops 2147483648 | bytes 8388608 | tf_op jit(solution)/shard_map/pallas_call | solution.py:208
  221.4 16.5 %shard_map.121 = bf16[1024,512]{1,0:T(8,128)(2,1)S(1)} custom-call(s32[51]{0:T(128)S(1)} %copy-done.13, bf16[1024,512]{1,0:T(8,128)(2,1)S(1)} %shard_map.120.refs_0_, bf16[4,1024,128]{2,1,0:T(8,128)(2,1)} %get-tuple-element.23.refs_1_.refs_0_, bf16[4,1024,128]{2,1,0:T(8,128)(2,1)} %get-tuple-element.25.refs_2_.refs_1_, ...), custom_call_target="tpu_custom_call" | custom-call | flops 4294967296 | bytes 6291456 | tf_op jit(solution)/shard_map/pallas_call | solution.py:336
  244.8 6.1 %shard_map.118.refs_0_ = bf16[1024,512]{1,0:T(8,128)(2,1)S(1)} custom-call(s32[51]{0:T(128)S(1)} %copy-done.14, bf16[512,2048]{1,0:T(8,128)(2,1)} %fusion.2.refs_0_, bf16[512,2048]{1,0:T(8,128)(2,1)} %collective-permute-done.1.refs_1_, bf16[2,4,64,512]{3,2,1,0:T(8,128)(2,1)S(1)} %get-tuple-element.29.refs_2_, bf16[2,4,64,512]{3,2,1,0:T(8,128)(2,1)S(1)} %copy-done.1, ...), custom_call_target="tpu_custom_call" | custom-call | flops 2147483648 | bytes 8388608 | tf_op jit(solution)/shard_map/pallas_call | solution.py:208
  250.9 14.9 %shard_map.119.refs_0_ = bf16[1024,512]{1,0:T(8,128)(2,1)S(1)} custom-call(s32[51]{0:T(128)S(1)} %copy-done.13, bf16[1024,512]{1,0:T(8,128)(2,1)S(1)} %shard_map.118.refs_0_, bf16[4,1024,128]{2,1,0:T(8,128)(2,1)} %get-tuple-element.23.refs_1_.refs_0_, bf16[4,1024,128]{2,1,0:T(8,128)(2,1)} %get-tuple-element.25.refs_2_.refs_1_, ...), custom_call_target="tpu_custom_call" | custom-call | flops 4294967296 | bytes 6291456 | tf_op jit(solution)/shard_map/pallas_call | solution.py:336
  266.2 8.7 %collective-permute-done.25.refs_1_ = bf16[512,512]{1,0:T(8,128)(2,1)S(1)} collective-permute-done((bf16[512,512]{1,0:T(8,128)(2,1)S(1)}, bf16[512,512]{1,0:T(8,128)(2,1)S(1)}, u32[]{:S(2)}, u32[]{:S(2)}) %collective-permute-start.25) | collective-permute-done | bytes 524320 | tf_op jit(solution)/shard_map/ppermute | solution.py:38
  277.3 9.6 %collective-permute-done.27.refs_3_ = bf16[512,512]{1,0:T(8,128)(2,1)S(1)} collective-permute-done((bf16[512,512]{1,0:T(8,128)(2,1)S(1)}, bf16[512,512]{1,0:T(8,128)(2,1)S(1)}, u32[]{:S(2)}, u32[]{:S(2)}) %collective-permute-start.27) | collective-permute-done | bytes 524320 | tf_op jit(solution)/shard_map/ppermute | solution.py:38
  289.3 9.8 %output_rows.1 = bf16[512,2048]{1,0:T(8,128)(2,1)} custom-call(s32[51]{0:T(128)S(1)} %copy-done.13, bf16[1024,512]{1,0:T(8,128)(2,1)S(1)} %shard_map.119.refs_0_, bf16[1024,512]{1,0:T(8,128)(2,1)S(1)} %collective-permute-done.18.refs_1_, bf16[512,512]{1,0:T(8,128)(2,1)S(1)} %collective-permute-done.19.refs_2_, ...), custom_call_target="tpu_custom_call" | custom-call | tf_op jit(solution)/shard_map/output_rows/pallas_call | solution.py:443
  (111 shorter events, 63.7 us)
Async XLA Ops:
  18.3 49.3 %collective-permute-start.8 = (bf16[512,2048]{1,0:T(8,128)(2,1)}, bf16[512,2048]{1,0:T(8,128)(2,1)}, u32[]{:S(2)}, u32[]{:S(2)}) collective-permute-start(bf16[512,2048]{1,0:T(8,128)(2,1)} %fusion.2.refs_0_), channel_id=1, source_target_pairs={{0,1},{1,0},{2,3},{3,2},{4,5},{5,4},{6,7},{7,6},{8,9},{9,8},{10,11... | collective-permute-start | bytes 6291464 | tf_op jit(solution)/shard_map/ppermute | solution.py:30
  19.2 117.6 %collective-permute-start.1 = (bf16[512,2048]{1,0:T(8,128)(2,1)}, bf16[512,2048]{1,0:T(8,128)(2,1)}, u32[]{:S(2)}, u32[]{:S(2)}) collective-permute-start(bf16[512,2048]{1,0:T(8,128)(2,1)} %fusion.2.refs_0_), channel_id=1, source_target_pairs={{0,2},{2,0},{1,3},{3,1},{4,6},{6,4},{5,7},{7,5},{8,10},{10,8},{9,1... | collective-permute-start | bytes 6291464 | tf_op jit(solution)/shard_map/ppermute | solution.py:30
  32.8 19.2 %collective-permute-start.11 = (bf16[2,64,1536]{2,1,0:T(8,128)(2,1)S(1)}, bf16[2,64,1536]{2,1,0:T(8,128)(2,1)S(1)}, u32[]{:S(2)}, u32[]{:S(2)}) collective-permute-start(bf16[2,64,1536]{2,1,0:T(8,128)(2,1)S(1)} %get-tuple-element.28.refs_0_), channel_id=1, source_target_pairs={{0,8},{4,12},{8,0},{12,4},{1,9},{5,13},{9,1},{13,5},{2,10},{6,14},... | collective-permute-start | bytes 1179656 | tf_op jit(solution)/shard_map/ppermute | solution.py:34
  35.1 17.0 %collective-permute-start.12 = (bf16[2,64,1536]{2,1,0:T(8,128)(2,1)S(1)}, bf16[2,64,1536]{2,1,0:T(8,128)(2,1)S(1)}, u32[]{:S(2)}, u32[]{:S(2)}) collective-permute-start(bf16[2,64,1536]{2,1,0:T(8,128)(2,1)S(1)} %get-tuple-element.28.refs_0_), channel_id=1, source_target_pairs={{0,12},{4,0},{8,4},{12,8},{1,13},{5,1},{9,5},{13,9},{2,14},{6,2},{... | collective-permute-start | bytes 1179656 | tf_op jit(solution)/shard_map/ppermute | solution.py:34
  53.8 25.1 %collective-permute-start.23 = (bf16[2,4,64,1024]{3,2,1,0:T(8,128)(2,1)}, bf16[2,4,64,1024]{3,2,1,0:T(8,128)(2,1)}, u32[]{:S(2)}, u32[]{:S(2)}) collective-permute-start(bf16[2,4,64,1024]{3,2,1,0:T(8,128)(2,1)} %get-tuple-element.30), channel_id=1, source_target_pairs={{0,96},{32,0},{64,32},{96,64},{1,97},{33,1},{65,33},{97,65},{2,98}... | collective-permute-start | bytes 3145736 | tf_op jit(solution)/shard_map/ppermute | solution.py:34
  56.5 24.9 %collective-permute-start.22 = (bf16[2,4,64,1024]{3,2,1,0:T(8,128)(2,1)}, bf16[2,4,64,1024]{3,2,1,0:T(8,128)(2,1)}, u32[]{:S(2)}, u32[]{:S(2)}) collective-permute-start(bf16[2,4,64,1024]{3,2,1,0:T(8,128)(2,1)} %get-tuple-element.30), channel_id=1, source_target_pairs={{0,64},{32,96},{64,0},{96,32},{1,65},{33,97},{65,1},{97,33},{2,66}... | collective-permute-start | bytes 3145736 | tf_op jit(solution)/shard_map/ppermute | solution.py:34
  56.9 49.0 %collective-permute-start.21 = (bf16[2,4,64,1024]{3,2,1,0:T(8,128)(2,1)}, bf16[2,4,64,1024]{3,2,1,0:T(8,128)(2,1)}, u32[]{:S(2)}, u32[]{:S(2)}) collective-permute-start(bf16[2,4,64,1024]{3,2,1,0:T(8,128)(2,1)} %get-tuple-element.30), channel_id=1, source_target_pairs={{0,32},{32,64},{64,96},{96,0},{1,33},{33,65},{65,97},{97,1},{2,34}... | collective-permute-start | bytes 3145736 | tf_op jit(solution)/shard_map/ppermute | solution.py:34
  67.5 79.4 %collective-permute-start.9 = (bf16[512,2048]{1,0:T(8,128)(2,1)}, bf16[512,2048]{1,0:T(8,128)(2,1)}, u32[]{:S(2)}, u32[]{:S(2)}) collective-permute-start(bf16[512,2048]{1,0:T(8,128)(2,1)} %collective-permute-done.8.refs_0_), channel_id=1, source_target_pairs={{0,2},{2,0},{1,3},{3,1},{4,6},{6,4},{5,7},{7,5},{8,10},{10,8},{9,1... | collective-permute-start | bytes 6291464 | tf_op jit(solution)/shard_map/ppermute | solution.py:30
  78.8 38.0 %collective-permute-start.5 = (bf16[2,4,64,512]{3,2,1,0:T(8,128)(2,1)S(1)}, bf16[2,4,64,512]{3,2,1,0:T(8,128)(2,1)}, u32[]{:S(2)}, u32[]{:S(2)}) collective-permute-start(bf16[2,4,64,512]{3,2,1,0:T(8,128)(2,1)S(1)} %shard_map.114.refs_2_), channel_id=1, source_target_pairs={{0,32},{32,64},{64,96},{96,0},{1,33},{33,65},{65,97},{97,1},{2,34}... | collective-permute-start | bytes 1572872 | tf_op jit(solution)/shard_map/ppermute | solution.py:34
  81.4 29.0 %collective-permute-start = (s32[8]{0:T(128)S(1)}, s32[8]{0:T(128)S(1)}, u32[]{:S(2)}, u32[]{:S(2)}) collective-permute-start(s32[8]{0:T(128)S(1)} %copy-done.16), channel_id=1, source_target_pairs={{0,2},{2,0},{1,3},{3,1},{4,6},{6,4},{5,7},{7,5},{8,10},{10,8},{9,1... | collective-permute-start | bytes 104 | tf_op jit(solution)/shard_map/ppermute | solution.py:30
  109.8 179.5 %collective-permute-start.24 = (bf16[4,2,4,64,1024]{4,3,2,1,0:T(8,128)(2,1)}, bf16[4,2,4,64,1024]{4,3,2,1,0:T(8,128)(2,1)}, u32[]{:S(2)}, u32[]{:S(2)}) collective-permute-start(bf16[4,2,4,64,1024]{4,3,2,1,0:T(8,128)(2,1)} %pad_maximum_fusion.refs_4_), channel_id=1, source_target_pairs={{0,2},{2,0},{1,3},{3,1},{4,6},{6,4},{5,7},{7,5},{8,10},{10,8},{9,1... | collective-permute-start | bytes 12582920 | tf_op jit(solution)/shard_map/ppermute | solution.py:30
  110.3 15.5 %collective-permute-start.6 = (bf16[2,4,64,512]{3,2,1,0:T(8,128)(2,1)S(1)}, bf16[2,4,64,512]{3,2,1,0:T(8,128)(2,1)}, u32[]{:S(2)}, u32[]{:S(2)}) collective-permute-start(bf16[2,4,64,512]{3,2,1,0:T(8,128)(2,1)S(1)} %shard_map.114.refs_2_), channel_id=1, source_target_pairs={{0,64},{32,96},{64,0},{96,32},{1,65},{33,97},{65,1},{97,33},{2,66}... | collective-permute-start | bytes 1572872 | tf_op jit(solution)/shard_map/ppermute | solution.py:34
  116.8 19.9 %collective-permute-start.7 = (bf16[2,4,64,512]{3,2,1,0:T(8,128)(2,1)S(1)}, bf16[2,4,64,512]{3,2,1,0:T(8,128)(2,1)}, u32[]{:S(2)}, u32[]{:S(2)}) collective-permute-start(bf16[2,4,64,512]{3,2,1,0:T(8,128)(2,1)S(1)} %shard_map.114.refs_2_), channel_id=1, source_target_pairs={{0,96},{32,0},{64,32},{96,64},{1,97},{33,1},{65,33},{97,65},{2,98}... | collective-permute-start | bytes 1572872 | tf_op jit(solution)/shard_map/ppermute | solution.py:34
  125.9 34.4 %collective-permute-start.13 = (bf16[2,4,64,512]{3,2,1,0:T(8,128)(2,1)S(1)}, bf16[2,4,64,512]{3,2,1,0:T(8,128)(2,1)S(1)}, u32[]{:S(2)}, u32[]{:S(2)}) collective-permute-start(bf16[2,4,64,512]{3,2,1,0:T(8,128)(2,1)S(1)} %get-tuple-element.29.refs_2_), channel_id=1, source_target_pairs={{0,32},{32,64},{64,96},{96,0},{1,33},{33,65},{65,97},{97,1},{2,34}... | collective-permute-start | bytes 1572872 | tf_op jit(solution)/shard_map/ppermute | solution.py:34
  144.8 76.5 %collective-permute-start.16 = (bf16[4,1024,128]{2,1,0:T(8,128)(2,1)}, bf16[4,1024,128]{2,1,0:T(8,128)(2,1)}, u32[]{:S(2)}, u32[]{:S(2)}) collective-permute-start(bf16[4,1024,128]{2,1,0:T(8,128)(2,1)} %get-tuple-element.23.refs_1_.refs_0_), channel_id=1, source_target_pairs={{0,4},{1,5},{2,6},{3,7},{4,8},{5,9},{6,10},{7,11},{8,12},{9,13},{1... | collective-permute-start | bytes 3145736 | tf_op jit(solution)/shard_map/ppermute | solution.py:473
  155.0 66.3 %collective-permute-start.17 = (bf16[4,1024,128]{2,1,0:T(8,128)(2,1)}, bf16[4,1024,128]{2,1,0:T(8,128)(2,1)}, u32[]{:S(2)}, u32[]{:S(2)}) collective-permute-start(bf16[4,1024,128]{2,1,0:T(8,128)(2,1)} %get-tuple-element.25.refs_2_.refs_1_), channel_id=1, source_target_pairs={{0,4},{1,5},{2,6},{3,7},{4,8},{5,9},{6,10},{7,11},{8,12},{9,13},{1... | collective-permute-start | bytes 3145736 | tf_op jit(solution)/shard_map/ppermute | solution.py:473
  158.6 53.0 %collective-permute-start.14 = (bf16[2,4,64,512]{3,2,1,0:T(8,128)(2,1)S(1)}, bf16[2,4,64,512]{3,2,1,0:T(8,128)(2,1)S(1)}, u32[]{:S(2)}, u32[]{:S(2)}) collective-permute-start(bf16[2,4,64,512]{3,2,1,0:T(8,128)(2,1)S(1)} %get-tuple-element.29.refs_2_), channel_id=1, source_target_pairs={{0,64},{32,96},{64,0},{96,32},{1,65},{33,97},{65,1},{97,33},{2,66}... | collective-permute-start | bytes 1572872 | tf_op jit(solution)/shard_map/ppermute | solution.py:34
  161.1 51.3 %collective-permute-start.15 = (bf16[2,4,64,512]{3,2,1,0:T(8,128)(2,1)S(1)}, bf16[2,4,64,512]{3,2,1,0:T(8,128)(2,1)}, u32[]{:S(2)}, u32[]{:S(2)}) collective-permute-start(bf16[2,4,64,512]{3,2,1,0:T(8,128)(2,1)S(1)} %get-tuple-element.29.refs_2_), channel_id=1, source_target_pairs={{0,96},{32,0},{64,32},{96,64},{1,97},{33,1},{65,33},{97,65},{2,98}... | collective-permute-start | bytes 1572872 | tf_op jit(solution)/shard_map/ppermute | solution.py:34
  237.9 28.0 %collective-permute-start.18 = (bf16[1024,512]{1,0:T(8,128)(2,1)S(1)}, bf16[1024,512]{1,0:T(8,128)(2,1)S(1)}, u32[]{:S(2)}, u32[]{:S(2)}) collective-permute-start(bf16[1024,512]{1,0:T(8,128)(2,1)S(1)} %shard_map.121), channel_id=1, source_target_pairs={{0,1},{1,0},{2,3},{3,2},{4,5},{5,4},{6,7},{7,6},{8,9},{9,8},{10,11... | collective-permute-start | bytes 3145736 | tf_op jit(solution)/shard_map/ppermute | solution.py:30
  240.7 34.2 %collective-permute-start.25 = (bf16[512,512]{1,0:T(8,128)(2,1)S(1)}, bf16[512,512]{1,0:T(8,128)(2,1)S(1)}, u32[]{:S(2)}, u32[]{:S(2)}) collective-permute-start(bf16[512,512]{1,0:T(8,128)(2,1)S(1)} %get-tuple-element.34), channel_id=1, source_target_pairs={{0,1},{1,0},{2,3},{3,2},{4,5},{5,4},{6,7},{7,6},{8,9},{9,8},{10,11... | collective-permute-start | bytes 1572872 | tf_op jit(solution)/shard_map/ppermute | solution.py:38
  243.7 33.6 %collective-permute-start.26 = (bf16[512,512]{1,0:T(8,128)(2,1)S(1)}, bf16[512,512]{1,0:T(8,128)(2,1)S(1)}, u32[]{:S(2)}, u32[]{:S(2)}) collective-permute-start(bf16[512,512]{1,0:T(8,128)(2,1)S(1)} %get-tuple-element.35), channel_id=1, source_target_pairs={{0,2},{1,3},{2,0},{3,1},{4,6},{5,7},{6,4},{7,5},{8,10},{9,11},{10,... | collective-permute-start | bytes 1572872 | tf_op jit(solution)/shard_map/ppermute | solution.py:38
  244.8 42.1 %collective-permute-start.27 = (bf16[512,512]{1,0:T(8,128)(2,1)S(1)}, bf16[512,512]{1,0:T(8,128)(2,1)S(1)}, u32[]{:S(2)}, u32[]{:S(2)}) collective-permute-start(bf16[512,512]{1,0:T(8,128)(2,1)S(1)} %get-tuple-element.36), channel_id=1, source_target_pairs={{0,3},{1,2},{2,1},{3,0},{4,7},{5,6},{6,5},{7,4},{8,11},{9,10},{10,... | collective-permute-start | bytes 1572872 | tf_op jit(solution)/shard_map/ppermute | solution.py:38
  265.9 23.4 %collective-permute-start.19 = (bf16[512,512]{1,0:T(8,128)(2,1)S(1)}, bf16[512,512]{1,0:T(8,128)(2,1)S(1)}, u32[]{:S(2)}, u32[]{:S(2)}) collective-permute-start(bf16[512,512]{1,0:T(8,128)(2,1)S(1)} %slice.8), channel_id=1, source_target_pairs={{0,2},{2,0},{1,3},{3,1},{4,6},{6,4},{5,7},{7,5},{8,10},{10,8},{9,1... | collective-permute-start | bytes 1572872 | tf_op jit(solution)/shard_map/ppermute | solution.py:30
  274.9 14.3 %collective-permute-start.20 = (bf16[512,512]{1,0:T(8,128)(2,1)S(1)}, bf16[512,512]{1,0:T(8,128)(2,1)S(1)}, u32[]{:S(2)}, u32[]{:S(2)}) collective-permute-start(bf16[512,512]{1,0:T(8,128)(2,1)S(1)} %slice.9), channel_id=1, source_target_pairs={{0,2},{2,0},{1,3},{3,1},{4,6},{6,4},{5,7},{7,5},{8,10},{10,8},{9,1... | collective-permute-start | bytes 1572872 | tf_op jit(solution)/shard_map/ppermute | solution.py:30
  (24 other events, 272.9 us)
where the time goes:
time: 300 us; the launch traced here: 299 us
  waiting for transfers between devices  135 us (45%)
  Pallas kernels  78.7 us (26%)
  starting transfers between devices  61.9 us (21%)
  other arithmetic  13.5 us (4%)
  local copies, waits for them, and re-layouts  8.65 us (3%)
    ppermute x15, waiting for transfers between devices, shift(): lax.ppermute(block, axis, [(i, (i + distance) % 4) for i in range(4)])  104 us
    pallas_call x2, Pallas kernels, attend(): pl.pallas_call(functools.partial(attend_kernel, pair), grid_spec=pltpu.Pr...  31.4 us
    ppermute x8, starting transfers between devices, swap(): return lax.ppermute(block, axis, [(0, 1), (1, 0)])  27.5 us
    pallas_call x4, Pallas kernels, project(): pl.pallas_call(functools.partial(project_kernel, store), grid_spec=pltpu....  26.9 us
    ppermute x15, starting transfers between devices, shift(): lax.ppermute(block, axis, [(i, (i + distance) % 4) for i in range(4)])  19 us
    ppermute x3, waiting for transfers between devices, to_role(): return lax.ppermute(block, QUAD, [(i, i ^ flip) for i in range(4)])  18.3 us
    ppermute x8, waiting for transfers between devices, swap(): return lax.ppermute(block, axis, [(0, 1), (1, 0)])  9.9 us
    pallas_call x1, Pallas kernels, output(): pl.pallas_call(output_kernel, grid_spec=pltpu.PrefetchScalarGridSpec(num_...  9.8 us
  transfers between devices with their start and end apart: 29, of which 16 were waited for; matrix products, arithmetic and copies ran while one was open for 5% of the time, Pallas kernels for 23%

commit v1 on v0

--- a/solution.py
+++ b/solution.py
@@ -45,6 +45,13 @@
     return pieces
 
 
+def ring_chain(block, axis):
+    pieces = [block]
+    for _ in range(3):
+        pieces.append(shift(pieces[-1], axis, -1))
+    return pieces
+
+
 def slices_kernel(here, qk_ref, v_ref, o_ref, out_ref):
     for role in range(4):
         for copy in (role, role + 4):
@@ -71,6 +78,11 @@
             width = out_ref.shape[3]
             out_ref[:, place] = pieces[k][:, :, first : first + width]
             first += width
+
+
+def column_kernel(here, *refs):
+    for k in range(4):
+        refs[4][lax.rem(here[1] + 4 - k, 4)] = refs[k][...]
 
 
 def tick_kernel(in_ref, out_ref):
@@ -142,6 +154,8 @@
 
 def project_kernel(store, meta, *refs):
     x_refs, parts, tables, out_refs = refs[:2], refs[2:6], refs[6:8], refs[8:]
+    if store is store_keys:
+        out_refs, weight = out_refs[:-1], out_refs[-1]
     step = pl.program_id(0)
     cosine = tables[0][...]
     sine = tables[1][...]
@@ -149,15 +163,29 @@
     def turned(block):
         return (block * cosine + pltpu.roll(block, 64, 1) * sine).astype(BF)
 
+    if store is store_keys:
+
+        @pl.when(step == 0)
+        def _():
+            for i in range(4):
+                weight[:, :, lax.rem(meta[50] + 4 - i, 4)] = parts[i][...]
+
     def body(x_ref):
-        result = jnp.zeros((x_ref.shape[0], 512), F32)
-        for i in range(4):
-            start = pl.multiple_of(lax.rem(meta[49] + 4 - i, 4) * 512, 512)
-            result += jnp.dot(
-                x_ref[:, pl.ds(start, 512)],
-                parts[i][...].reshape(512, 512),
+        if store is store_keys:
+            result = jnp.dot(
+                x_ref[...],
+                weight[...].reshape(DEPTH, 512),
                 preferred_element_type=F32,
             )
+        else:
+            result = jnp.zeros((x_ref.shape[0], 512), F32)
+            for i in range(4):
+                start = pl.multiple_of(lax.rem(meta[49] + 4 - i, 4) * 512, 512)
+                result += jnp.dot(
+                    x_ref[:, pl.ds(start, 512)],
+                    parts[i][...].reshape(512, 512),
+                    preferred_element_type=F32,
+                )
         store(result, turned, *out_refs)
 
     @pl.when(step < 2)
@@ -193,10 +221,12 @@
 
     if kind == "q":
         store = store_queries
+        scratch = []
         out_specs = [pl.BlockSpec((tile, 512), lambda i, m: (i, 0))]
         out_shape = [jax.ShapeDtypeStruct((2 * TOK, 512), BF)]
     else:
         store = store_keys
+        scratch = [pltpu.VMEM((4, 2, 4, 64, 512), BF)]
         out_specs = [
             pl.BlockSpec((4, tile, 128), lambda i, m: (0, i, 0)),
             pl.BlockSpec((2, tile, 128), lambda i, m: (0, i, 0)),
@@ -217,6 +247,7 @@
             + [INSIDE] * 4
             + [pl.BlockSpec((tile, 128), table)] * 2,
             out_specs=out_specs,
+            scratch_shapes=scratch,
         ),
         out_shape=out_shape,
         compiler_params=pltpu.CompilerParams(vmem_limit_bytes=40 << 20),
@@ -420,40 +451,79 @@
     )(meta, *received)
 
 
-def output_kernel(meta, *refs):
-    in_refs, weights, out_ref = refs[:4], refs[4:6], refs[6]
+def fill_rows(meta, parts, weight, parity):
+    for half in range(2):
+        for d in range(4):
+            flip = jnp.bitwise_xor(lax.rem(meta[49] + d, 4), meta[0])
+
+            @pl.when(lax.rem(flip, 2) == parity)
+            def _(half=half, d=d, flip=flip):
+                weight[half, flip // 2] = parts[4 * half + d][...].reshape(512, 1024)
+
+
+def pair_product(in_refs, weight, half):
+    return jnp.dot(
+        in_refs[0][:TOK], weight[half, 0], preferred_element_type=F32
+    ) + jnp.dot(in_refs[1][...], weight[half, 1], preferred_element_type=F32)
+
+
+def near_kernel(meta, *refs):
+    in_refs, parts, out_ref, weight = refs[:2], refs[2:10], refs[10], refs[11]
+    fill_rows(meta, parts, weight, 0)
+    for half in range(2):
+        out_ref[half] = pair_product(in_refs, weight, half)
+
+
+def far_kernel(meta, *refs):
+    in_refs, parts, partial, out_ref, weight = (
+        refs[:2], refs[2:10], refs[10], refs[11], refs[12]
+    )
     step = pl.program_id(0)
+
+    @pl.when(step == 0)
+    def _():
+        fill_rows(meta, parts, weight, 1)
+
     for half in range(2):
 
         @pl.when(step == half)
         def _(half=half):
-            total = jnp.zeros((TOK, 1024), F32)
-            for p in range(4):
-                block = jnp.bitwise_xor(meta[0], p)
-                total += jnp.dot(
-                    in_refs[p][...],
-                    weights[half][lax.rem(meta[49] + 4 - block, 4)].reshape(512, 1024),
-                    preferred_element_type=F32,
-                )
+            total = partial[half] + pair_product(in_refs, weight, half)
             out_ref[...] = total.astype(BF)
 
 
-def output(meta, received, own_half, other_half):
-    whole = pl.BlockSpec((TOK, 512), lambda i, m: (0, 0))
-    return pl.pallas_call(
-        output_kernel,
+def output_near(meta, pair, parts):
+    return pl.pallas_call(
+        near_kernel,
+        grid_spec=pltpu.PrefetchScalarGridSpec(
+            num_scalar_prefetch=1,
+            grid=(),
+            in_specs=[INSIDE] * 10,
+            out_specs=INSIDE,
+            scratch_shapes=[pltpu.VMEM((2, 2, 512, 1024), BF)],
+        ),
+        out_shape=jax.ShapeDtypeStruct((2, TOK, 1024), F32),
+        compiler_params=pltpu.CompilerParams(vmem_limit_bytes=32 << 20),
+        name="output_near",
+    )(meta, *pair, *parts)
+
+
+def output_far(meta, pair, parts, partial):
+    return pl.pallas_call(
+        far_kernel,
         grid_spec=pltpu.PrefetchScalarGridSpec(
             num_scalar_prefetch=1,
             grid=(2,),
-            in_specs=[whole] * 4 + [INSIDE] * 2,
+            in_specs=[INSIDE] * 11,
             out_specs=pl.BlockSpec(
                 (TOK, 1024), lambda i, m: (0, jnp.bitwise_xor(m[0] // 2, i))
             ),
+            scratch_shapes=[pltpu.VMEM((2, 2, 512, 1024), BF)],
         ),
         out_shape=jax.ShapeDtypeStruct((TOK, DEPTH), BF),
-        compiler_params=pltpu.CompilerParams(vmem_limit_bytes=48 << 20),
-        name="output_rows",
-    )(meta, *received, own_half, other_half)
+        compiler_params=pltpu.CompilerParams(vmem_limit_bytes=32 << 20),
+        name="output_far",
+    )(meta, *pair, *parts, partial)
 
 
 def page_sources(page_slots, core):
@@ -487,9 +557,9 @@
     ).reshape(2, 64, 2048)
     kv_level, rest = small(split_kernel, here, (level,), [(2, 64, 512), (2, 64, 1536)])
     kv_row = small(
-        arrange_kernel, here, ring_pieces(kv_level, "x"), [(2, 4, 64, 512)]
+        column_kernel, here, ring_pieces(kv_level, "y"), [(4, 2, 64, 512)]
     )[0]
-    kv_parts = ring_pieces(kv_row, "y")
+    kv_parts = ring_pieces(kv_row, "x")
     q_row, o_row = small(
         arrange_kernel,
         here,
@@ -497,7 +567,7 @@
         [(2, 4, 64, 512), (2, 4, 64, 1024)],
     )
     q_parts = ring_pieces(q_row, "y")
-    o_parts = ring_pieces(o_row, "y")
+    o_parts = ring_chain(o_row, "y")
 
     normed = normalize(after(hidden_in, slices), norm_gain)
     beside = swap(normed, "c")
@@ -529,10 +599,12 @@
     far = attend(meta, queries[1], keys, halo, 1)
     far = swap(far, "zh")
     near = attend(meta, queries[0], keys, halo, 0)
-    own_half = jnp.stack(o_parts)
-    other_half = swap(own_half, "c")
-    received = [near, far, swap(near[TOK:], "c"), swap(far[TOK:], "c")]
-    attended = output(meta, received, own_half, other_half)
+    o_parts = list(o_parts)
+    for i in range(4):
+        o_parts.append(swap(o_parts[i], "c"))
+    partial = output_near(meta, (near, swap(near[TOK:], "c")), o_parts)
+    diagonal_far = swap(far[TOK:], "c")
+    attended = output_far(meta, (far, diagonal_far), o_parts, partial)
     key_cache, value_cache = unpack(meta, pages)
     return (
         attended,

time: 300 us -> 285 us (0.950)
  the two profiles are of different devices: /device:TPU:33 before, /device:TPU:57 now
where the time goes in v1:
time: 285 us
  waiting for transfers between devices  102 us (36%)
  Pallas kernels  83.4 us (29%)
  starting transfers between devices  79 us (28%)
  other arithmetic  12.4 us (4%)
  local copies, waits for them, and re-layouts  6.91 us (2%)
    ppermute x15, starting transfers between devices, shift(): lax.ppermute(block, axis, [(i, (i + distance) % 4) for i in range(4)])  48.4 us
    ppermute x15, waiting for transfers between devices, shift(): lax.ppermute(block, axis, [(i, (i + distance) % 4) for i in range(4)])  36.4 us
    pallas_call x2, Pallas kernels, attend(): pl.pallas_call(functools.partial(attend_kernel, pair), grid_spec=pltpu.Pr...  34 us
    ppermute x11, waiting for transfers between devices, swap(): return lax.ppermute(block, axis, [(0, 1), (1, 0)])  31.1 us
    ppermute x3, waiting for transfers between devices, to_role(): return lax.ppermute(block, QUAD, [(i, i ^ flip) for i in range(4)])  30.5 us
    pallas_call x4, Pallas kernels, project(): pl.pallas_call(functools.partial(project_kernel, store), grid_spec=pltpu....  27.2 us
    ppermute x11, starting transfers between devices, swap(): return lax.ppermute(block, axis, [(0, 1), (1, 0)])  13.8 us
    ppermute x2, starting transfers between devices, previous_quad(): return lax.ppermute(block, names, route)  7.29 us
  transfers between devices with their start and end apart: 32, of which 11 were waited for; matrix products, arithmetic and copies ran while one was open for 4% of the time, Pallas kernels for 27%

profile of v1, /device:TPU:57, one launch (start us, length us, event | category | flops | bytes accessed | tf_op | source)
XLA Modules:
  0.0 284.7 jit_solution(12160557927733095109)
XLA Ops:
  4.6 5.7 %all-to-all-start = ((bf16[8,16,2048]{2,1,0:T(8,128)(2,1)}), bf16[8,16,2048]{2,1,0:T(8,128)(2,1)S(1)}, u32[]{:S(2)}, u32[]{:S(2)}) async-start(bf16[8,16,2048]{2,1,0:T(8,128)(2,1)} %shard_map.112), calls=%async_computation | async-start | bytes 1048576 | tf_op jit(solution)/shard_map/all_to_all | solution.py:555
  14.3 4.0 %all-to-all-done = bf16[8,16,2048]{2,1,0:T(8,128)(2,1)S(1)} async-done(((bf16[8,16,2048]{2,1,0:T(8,128)(2,1)}), bf16[8,16,2048]{2,1,0:T(8,128)(2,1)S(1)}, u32[]{:S(2)}, u32[]{:S(2)}) %all-to-all-start) | async-done | bytes 524320 | tf_op jit(solution)/shard_map/all_to_all | solution.py:555
  23.7 2.8 collective-permute-done.2.refs_1_
  27.9 3.1 %collective-permute-done.4.refs_3_ = bf16[2,64,512]{2,1,0:T(8,128)(2,1)S(1)} collective-permute-done((bf16[2,64,512]{2,1,0:T(8,128)(2,1)S(1)}, bf16[2,64,512]{2,1,0:T(8,128)(2,1)S(1)}, u32[]{:S(2)}, u32[]{:S(2)}) %collective-permute-start.4) | collective-permute-done | bytes 131104 | tf_op jit(solution)/shard_map/ppermute | solution.py:34
  36.5 31.0 %collective-permute-done.8.refs_0_ = bf16[512,2048]{1,0:T(8,128)(2,1)} collective-permute-done((bf16[512,2048]{1,0:T(8,128)(2,1)}, bf16[512,2048]{1,0:T(8,128)(2,1)}, u32[]{:S(2)}, u32[]{:S(2)}) %collective-permute-start.8) | collective-permute-done | bytes 2097184 | tf_op jit(solution)/shard_map/ppermute | solution.py:30
  68.1 5.5 %fusion.3 = (f32[2048,64]{1,0:T(8,128)}, f32[2048,64]{1,0:T(8,128)}, f32[2048,64]{1,0:T(8,128)S(1)}) fusion(f32[64]{0:T(128)S(1)} %multiply_power_fusion, f32[2048]{0:T(1024)S(1)} %convert_bitcast_fusion), kind=kLoop, calls=%fused_computation.9 | loop fusion | flops 262144 | bytes 1581312 | tf_op jit(solution)/shard_map/neg | solution.py:151
  81.9 6.7 %collective-permute-done.5.refs_3_ = bf16[4,2,64,512]{3,2,1,0:T(8,128)(2,1)} collective-permute-done((bf16[4,2,64,512]{3,2,1,0:T(8,128)(2,1)S(1)}, bf16[4,2,64,512]{3,2,1,0:T(8,128)(2,1)}, u32[]{:S(2)}, u32[]{:S(2)}) %collective-permute-start.5) | collective-permute-done | bytes 524320 | tf_op jit(solution)/shard_map/ppermute | solution.py:34
  90.2 10.5 %collective-permute-done.6.refs_4_ = bf16[4,2,64,512]{3,2,1,0:T(8,128)(2,1)} collective-permute-done((bf16[4,2,64,512]{3,2,1,0:T(8,128)(2,1)S(1)}, bf16[4,2,64,512]{3,2,1,0:T(8,128)(2,1)}, u32[]{:S(2)}, u32[]{:S(2)}) %collective-permute-start.6) | collective-permute-done | bytes 524320 | tf_op jit(solution)/shard_map/ppermute | solution.py:34
  103.9 7.4 %shard_map.115 = (bf16[4,1024,128]{2,1,0:T(8,128)(2,1)}, bf16[2,1024,128]{2,1,0:T(8,128)(2,1)S(1)}) custom-call(s32[51]{0:T(128)S(1)} %concatenate.9.in_ref.meta, bf16[512,2048]{1,0:T(8,128)(2,1)} %fusion.2.refs_0_, bf16[512,2048]{1,0:T(8,128)(2,1)} %collective-permute-done.1.refs_1_, bf16[4,2,64,512]{3,2,1,0:T(8,128)(2,1)S(1)} %shard_map.114.refs_2_, ...), custom_call_target="tpu_custom_call" | custom-call | flops 2147483648 | bytes 8388608 | tf_op jit(solution)/shard_map/pallas_call | solution.py:238
  112.1 5.4 %collective-permute-start.16 = (bf16[4,1024,128]{2,1,0:T(8,128)(2,1)}, bf16[4,1024,128]{2,1,0:T(8,128)(2,1)}, u32[]{:S(2)}, u32[]{:S(2)}) collective-permute-start(bf16[4,1024,128]{2,1,0:T(8,128)(2,1)} %get-tuple-element.23.refs_1_.refs_0_), channel_id=1, source_target_pairs={{0,4},{1,5},{2,6},{3,7},{4,8},{5,9},{6,10},{7,11},{8,12},{9,13},{1... | collective-permute-start | bytes 3145736 | tf_op jit(solution)/shard_map/ppermute | solution.py:543
  117.5 7.4 %shard_map.116 = (bf16[4,1024,128]{2,1,0:T(8,128)(2,1)}, bf16[2,1024,128]{2,1,0:T(8,128)(2,1)S(1)}) custom-call(s32[51]{0:T(128)S(1)} %concatenate.9.in_ref.meta, bf16[512,2048]{1,0:T(8,128)(2,1)} %collective-permute-done.8.refs_0_, bf16[512,2048]{1,0:T(8,128)(2,1)} %collective-permute-done.9.refs_1_, bf16[4,2,64,512]{3,2,1,0:T(8,128)(2,1)S(1)} %shard_map.114.refs_2_, ...), custom_call_target="tpu_custom_call" | custom-call | flops 2147483648 | bytes 8388608 | tf_op jit(solution)/shard_map/pallas_call | solution.py:238
  132.7 8.8 %collective-permute-done.14.refs_4_ = bf16[2,4,64,512]{3,2,1,0:T(8,128)(2,1)S(1)} collective-permute-done((bf16[2,4,64,512]{3,2,1,0:T(8,128)(2,1)S(1)}, bf16[2,4,64,512]{3,2,1,0:T(8,128)(2,1)S(1)}, u32[]{:S(2)}, u32[]{:S(2)}) %collective-permute-start.14) | collective-permute-done | bytes 524320 | tf_op jit(solution)/shard_map/ppermute | solution.py:34
  141.5 3.9 %collective-permute-start.23 = (bf16[2,4,64,1024]{3,2,1,0:T(8,128)(2,1)}, bf16[2,4,64,1024]{3,2,1,0:T(8,128)(2,1)S(1)}, u32[]{:S(2)}, u32[]{:S(2)}) collective-permute-start(bf16[2,4,64,1024]{3,2,1,0:T(8,128)(2,1)} %get-tuple-element.30.refs_2_), channel_id=1, source_target_pairs={{0,2},{2,0},{1,3},{3,1},{4,6},{6,4},{5,7},{7,5},{8,10},{10,8},{9,1... | collective-permute-start | bytes 3145736 | tf_op jit(solution)/shard_map/ppermute | solution.py:30
  145.5 32.8 %collective-permute-start.22 = (bf16[2,4,64,1024]{3,2,1,0:T(8,128)(2,1)}, bf16[2,4,64,1024]{3,2,1,0:T(8,128)(2,1)S(1)}, u32[]{:S(2)}, u32[]{:S(2)}) collective-permute-start(bf16[2,4,64,1024]{3,2,1,0:T(8,128)(2,1)} %collective-permute-done.21.refs_4_), channel_id=1, source_target_pairs={{0,96},{32,0},{64,32},{96,64},{1,97},{33,1},{65,33},{97,65},{2,98}... | collective-permute-start | bytes 3145736 | tf_op jit(solution)/shard_map/ppermute | solution.py:34
  180.0 6.1 %shard_map.118.refs_0_ = bf16[1024,512]{1,0:T(8,128)(2,1)S(1)} custom-call(s32[51]{0:T(128)S(1)} %copy-done.12, bf16[512,2048]{1,0:T(8,128)(2,1)} %collective-permute-done.8.refs_0_, bf16[512,2048]{1,0:T(8,128)(2,1)} %collective-permute-done.9.refs_1_, bf16[2,4,64,512]{3,2,1,0:T(8,128)(2,1)S(1)} %get-tuple-element.29.refs_2_, ...), custom_call_target="tpu_custom_call" | custom-call | flops 2147483648 | bytes 8388608 | tf_op jit(solution)/shard_map/pallas_call | solution.py:238
  186.2 14.9 %shard_map.119 = bf16[1024,512]{1,0:T(8,128)(2,1)S(1)} custom-call(s32[51]{0:T(128)S(1)} %copy-done.11, bf16[1024,512]{1,0:T(8,128)(2,1)S(1)} %shard_map.118.refs_0_, bf16[4,1024,128]{2,1,0:T(8,128)(2,1)} %get-tuple-element.23.refs_1_.refs_0_, bf16[4,1024,128]{2,1,0:T(8,128)(2,1)} %get-tuple-element.25.refs_2_.refs_1_, ...), custom_call_target="tpu_custom_call" | custom-call | flops 4294967296 | bytes 6291456 | tf_op jit(solution)/shard_map/pallas_call | solution.py:367
  201.1 5.2 %collective-permute-start.18 = (bf16[1024,512]{1,0:T(8,128)(2,1)S(1)}, bf16[1024,512]{1,0:T(8,128)(2,1)S(1)}, u32[]{:S(2)}, u32[]{:S(2)}) collective-permute-start(bf16[1024,512]{1,0:T(8,128)(2,1)S(1)} %shard_map.119), channel_id=1, source_target_pairs={{0,1},{1,0},{2,3},{3,2},{4,5},{5,4},{6,7},{7,6},{8,9},{9,8},{10,11... | collective-permute-start | bytes 3145736 | tf_op jit(solution)/shard_map/ppermute | solution.py:30
  206.3 2.7 pack_pages.1
  210.2 30.5 %collective-permute-done.28.refs_1_ = bf16[512,512]{1,0:T(8,128)(2,1)S(1)} collective-permute-done((bf16[512,512]{1,0:T(8,128)(2,1)S(1)}, bf16[512,512]{1,0:T(8,128)(2,1)S(1)}, u32[]{:S(2)}, u32[]{:S(2)}) %collective-permute-start.28) | collective-permute-done | bytes 524320 | tf_op jit(solution)/shard_map/ppermute | solution.py:38
  241.6 2.9 %collective-permute-start.30 = (bf16[512,512]{1,0:T(8,128)(2,1)S(1)}, bf16[512,512]{1,0:T(8,128)(2,1)S(1)}, u32[]{:S(2)}, u32[]{:S(2)}) collective-permute-start(bf16[512,512]{1,0:T(8,128)(2,1)S(1)} %get-tuple-element.36), channel_id=1, source_target_pairs={{0,3},{1,2},{2,1},{3,0},{4,7},{5,6},{6,5},{7,4},{8,11},{9,10},{10,... | collective-permute-start | bytes 1572872 | tf_op jit(solution)/shard_map/ppermute | solution.py:38
  244.5 6.1 %shard_map.120.refs_0_ = bf16[1024,512]{1,0:T(8,128)(2,1)S(1)} custom-call(s32[51]{0:T(128)S(1)} %copy-done.12, bf16[512,2048]{1,0:T(8,128)(2,1)} %fusion.2.refs_0_, bf16[512,2048]{1,0:T(8,128)(2,1)} %collective-permute-done.1.refs_1_, bf16[2,4,64,512]{3,2,1,0:T(8,128)(2,1)S(1)} %get-tuple-element.29.refs_2_, bf16[2,4,64,512]{3,2,1,0:T(8,128)(2,1)S(1)} %copy-done.2, ...), custom_call_target="tpu_custom_call" | custom-call | flops 2147483648 | bytes 8388608 | tf_op jit(solution)/shard_map/pallas_call | solution.py:238
  250.6 19.1 %shard_map.121.refs_0_ = bf16[1024,512]{1,0:T(8,128)(2,1)S(1)} custom-call(s32[51]{0:T(128)S(1)} %copy-done.11, bf16[1024,512]{1,0:T(8,128)(2,1)S(1)} %shard_map.120.refs_0_, bf16[4,1024,128]{2,1,0:T(8,128)(2,1)} %get-tuple-element.23.refs_1_.refs_0_, bf16[4,1024,128]{2,1,0:T(8,128)(2,1)} %get-tuple-element.25.refs_2_.refs_1_, ...), custom_call_target="tpu_custom_call" | custom-call | flops 4294967296 | bytes 6291456 | tf_op jit(solution)/shard_map/pallas_call | solution.py:367
  272.9 5.3 %output_near.1.refs_10_ = f32[2,512,1024]{2,1,0:T(8,128)S(1)} custom-call(s32[51]{0:T(128)S(1)} %copy-done.11, bf16[1024,512]{1,0:T(8,128)(2,1)S(1)} %shard_map.121.refs_0_, bf16[512,512]{1,0:T(8,128)(2,1)S(1)} %collective-permute-done.27.refs_1_, bf16[2,4,64,1024]{3,2,1,0:T(8,128)(2,1)} %get-tuple-element.30.refs_2_, ...), custom_call_target="tpu_custom_call" | custom-call | tf_op jit(solution)/shard_map/output_near/pallas_call | solution.py:496
  278.3 6.4 %output_far.1 = bf16[512,2048]{1,0:T(8,128)(2,1)} custom-call(s32[51]{0:T(128)S(1)} %copy-done.11, bf16[1024,512]{1,0:T(8,128)(2,1)S(1)} %collective-permute-done.18.refs_0_, bf16[512,512]{1,0:T(8,128)(2,1)S(1)} %collective-permute-done.19.refs_1_, bf16[2,4,64,1024]{3,2,1,0:T(8,128)(2,1)} %get-tuple-element.30.refs_2_, ...), custom_call_target="tpu_custom_call" | custom-call | tf_op jit(solution)/shard_map/output_far/pallas_call | solution.py:512
  (115 shorter events, 49.3 us)
Async XLA Ops:
  18.2 49.3 %collective-permute-start.8 = (bf16[512,2048]{1,0:T(8,128)(2,1)}, bf16[512,2048]{1,0:T(8,128)(2,1)}, u32[]{:S(2)}, u32[]{:S(2)}) collective-permute-start(bf16[512,2048]{1,0:T(8,128)(2,1)} %fusion.2.refs_0_), channel_id=1, source_target_pairs={{0,1},{1,0},{2,3},{3,2},{4,5},{5,4},{6,7},{7,6},{8,9},{9,8},{10,11... | collective-permute-start | bytes 6291464 | tf_op jit(solution)/shard_map/ppermute | solution.py:30
  19.1 84.7 %collective-permute-start.1 = (bf16[512,2048]{1,0:T(8,128)(2,1)}, bf16[512,2048]{1,0:T(8,128)(2,1)}, u32[]{:S(2)}, u32[]{:S(2)}) collective-permute-start(bf16[512,2048]{1,0:T(8,128)(2,1)} %fusion.2.refs_0_), channel_id=1, source_target_pairs={{0,2},{2,0},{1,3},{3,1},{4,6},{6,4},{5,7},{7,5},{8,10},{10,8},{9,1... | collective-permute-start | bytes 6291464 | tf_op jit(solution)/shard_map/ppermute | solution.py:30
  31.6 42.4 %collective-permute-start.10 = (bf16[2,64,1536]{2,1,0:T(8,128)(2,1)S(1)}, bf16[2,64,1536]{2,1,0:T(8,128)(2,1)S(1)}, u32[]{:S(2)}, u32[]{:S(2)}) collective-permute-start(bf16[2,64,1536]{2,1,0:T(8,128)(2,1)S(1)} %get-tuple-element.28.refs_0_), channel_id=1, source_target_pairs={{0,4},{4,8},{8,12},{12,0},{1,5},{5,9},{9,13},{13,1},{2,6},{6,10},{... | collective-permute-start | bytes 1179656 | tf_op jit(solution)/shard_map/ppermute | solution.py:34
  32.9 41.2 %collective-permute-start.11 = (bf16[2,64,1536]{2,1,0:T(8,128)(2,1)S(1)}, bf16[2,64,1536]{2,1,0:T(8,128)(2,1)S(1)}, u32[]{:S(2)}, u32[]{:S(2)}) collective-permute-start(bf16[2,64,1536]{2,1,0:T(8,128)(2,1)S(1)} %get-tuple-element.28.refs_0_), channel_id=1, source_target_pairs={{0,8},{4,12},{8,0},{12,4},{1,9},{5,13},{9,1},{13,5},{2,10},{6,14},... | collective-permute-start | bytes 1179656 | tf_op jit(solution)/shard_map/ppermute | solution.py:34
  35.3 40.1 %collective-permute-start.12 = (bf16[2,64,1536]{2,1,0:T(8,128)(2,1)S(1)}, bf16[2,64,1536]{2,1,0:T(8,128)(2,1)S(1)}, u32[]{:S(2)}, u32[]{:S(2)}) collective-permute-start(bf16[2,64,1536]{2,1,0:T(8,128)(2,1)S(1)} %get-tuple-element.28.refs_0_), channel_id=1, source_target_pairs={{0,12},{4,0},{8,4},{12,8},{1,13},{5,1},{9,5},{13,9},{2,14},{6,2},{... | collective-permute-start | bytes 1179656 | tf_op jit(solution)/shard_map/ppermute | solution.py:34
  67.5 50.0 %collective-permute-start.9 = (bf16[512,2048]{1,0:T(8,128)(2,1)}, bf16[512,2048]{1,0:T(8,128)(2,1)}, u32[]{:S(2)}, u32[]{:S(2)}) collective-permute-start(bf16[512,2048]{1,0:T(8,128)(2,1)} %collective-permute-done.8.refs_0_), channel_id=1, source_target_pairs={{0,2},{2,0},{1,3},{3,1},{4,6},{6,4},{5,7},{7,5},{8,10},{10,8},{9,1... | collective-permute-start | bytes 6291464 | tf_op jit(solution)/shard_map/ppermute | solution.py:30
  74.1 14.4 %collective-permute-start.5 = (bf16[4,2,64,512]{3,2,1,0:T(8,128)(2,1)S(1)}, bf16[4,2,64,512]{3,2,1,0:T(8,128)(2,1)}, u32[]{:S(2)}, u32[]{:S(2)}) collective-permute-start(bf16[4,2,64,512]{3,2,1,0:T(8,128)(2,1)S(1)} %shard_map.114.refs_2_), channel_id=1, source_target_pairs={{0,4},{4,8},{8,12},{12,0},{1,5},{5,9},{9,13},{13,1},{2,6},{6,10},{... | collective-permute-start | bytes 1572872 | tf_op jit(solution)/shard_map/ppermute | solution.py:34
  77.0 25.5 %collective-permute-start.20 = (bf16[2,4,64,1024]{3,2,1,0:T(8,128)(2,1)}, bf16[2,4,64,1024]{3,2,1,0:T(8,128)(2,1)}, u32[]{:S(2)}, u32[]{:S(2)}) collective-permute-start(bf16[2,4,64,1024]{3,2,1,0:T(8,128)(2,1)} %get-tuple-element.30.refs_2_), channel_id=1, source_target_pairs={{0,96},{32,0},{64,32},{96,64},{1,97},{33,1},{65,33},{97,65},{2,98}... | collective-permute-start | bytes 3145736 | tf_op jit(solution)/shard_map/ppermute | solution.py:34
  79.3 21.4 %collective-permute-start.6 = (bf16[4,2,64,512]{3,2,1,0:T(8,128)(2,1)S(1)}, bf16[4,2,64,512]{3,2,1,0:T(8,128)(2,1)}, u32[]{:S(2)}, u32[]{:S(2)}) collective-permute-start(bf16[4,2,64,512]{3,2,1,0:T(8,128)(2,1)S(1)} %shard_map.114.refs_2_), channel_id=1, source_target_pairs={{0,8},{4,12},{8,0},{12,4},{1,9},{5,13},{9,1},{13,5},{2,10},{6,14},... | collective-permute-start | bytes 1572872 | tf_op jit(solution)/shard_map/ppermute | solution.py:34
  88.5 15.3 %collective-permute-start.7 = (bf16[4,2,64,512]{3,2,1,0:T(8,128)(2,1)S(1)}, bf16[4,2,64,512]{3,2,1,0:T(8,128)(2,1)}, u32[]{:S(2)}, u32[]{:S(2)}) collective-permute-start(bf16[4,2,64,512]{3,2,1,0:T(8,128)(2,1)S(1)} %shard_map.114.refs_2_), channel_id=1, source_target_pairs={{0,12},{4,0},{8,4},{12,8},{1,13},{5,1},{9,5},{13,9},{2,14},{6,2},{... | collective-permute-start | bytes 1572872 | tf_op jit(solution)/shard_map/ppermute | solution.py:34
  100.8 27.7 %collective-permute-start.13 = (bf16[2,4,64,512]{3,2,1,0:T(8,128)(2,1)S(1)}, bf16[2,4,64,512]{3,2,1,0:T(8,128)(2,1)S(1)}, u32[]{:S(2)}, u32[]{:S(2)}) collective-permute-start(bf16[2,4,64,512]{3,2,1,0:T(8,128)(2,1)S(1)} %get-tuple-element.29.refs_2_), channel_id=1, source_target_pairs={{0,32},{32,64},{64,96},{96,0},{1,33},{33,65},{65,97},{97,1},{2,34}... | collective-permute-start | bytes 1572872 | tf_op jit(solution)/shard_map/ppermute | solution.py:34
  102.5 42.9 %collective-permute-start.21 = (bf16[2,4,64,1024]{3,2,1,0:T(8,128)(2,1)}, bf16[2,4,64,1024]{3,2,1,0:T(8,128)(2,1)}, u32[]{:S(2)}, u32[]{:S(2)}) collective-permute-start(bf16[2,4,64,1024]{3,2,1,0:T(8,128)(2,1)} %collective-permute-done.20.refs_3_), channel_id=1, source_target_pairs={{0,96},{32,0},{64,32},{96,64},{1,97},{33,1},{65,33},{97,65},{2,98}... | collective-permute-start | bytes 3145736 | tf_op jit(solution)/shard_map/ppermute | solution.py:34
  112.1 74.1 %collective-permute-start.16 = (bf16[4,1024,128]{2,1,0:T(8,128)(2,1)}, bf16[4,1024,128]{2,1,0:T(8,128)(2,1)}, u32[]{:S(2)}, u32[]{:S(2)}) collective-permute-start(bf16[4,1024,128]{2,1,0:T(8,128)(2,1)} %get-tuple-element.23.refs_1_.refs_0_), channel_id=1, source_target_pairs={{0,4},{1,5},{2,6},{3,7},{4,8},{5,9},{6,10},{7,11},{8,12},{9,13},{1... | collective-permute-start | bytes 3145736 | tf_op jit(solution)/shard_map/ppermute | solution.py:543
  125.7 60.4 %collective-permute-start.17 = (bf16[4,1024,128]{2,1,0:T(8,128)(2,1)}, bf16[4,1024,128]{2,1,0:T(8,128)(2,1)}, u32[]{:S(2)}, u32[]{:S(2)}) collective-permute-start(bf16[4,1024,128]{2,1,0:T(8,128)(2,1)} %get-tuple-element.25.refs_2_.refs_1_), channel_id=1, source_target_pairs={{0,4},{1,5},{2,6},{3,7},{4,8},{5,9},{6,10},{7,11},{8,12},{9,13},{1... | collective-permute-start | bytes 3145736 | tf_op jit(solution)/shard_map/ppermute | solution.py:543
  129.2 49.0 %collective-permute-start.15 = (bf16[2,4,64,512]{3,2,1,0:T(8,128)(2,1)S(1)}, bf16[2,4,64,512]{3,2,1,0:T(8,128)(2,1)}, u32[]{:S(2)}, u32[]{:S(2)}) collective-permute-start(bf16[2,4,64,512]{3,2,1,0:T(8,128)(2,1)S(1)} %get-tuple-element.29.refs_2_), channel_id=1, source_target_pairs={{0,96},{32,0},{64,32},{96,64},{1,97},{33,1},{65,33},{97,65},{2,98}... | collective-permute-start | bytes 1572872 | tf_op jit(solution)/shard_map/ppermute | solution.py:34
  141.5 68.2 %collective-permute-start.23 = (bf16[2,4,64,1024]{3,2,1,0:T(8,128)(2,1)}, bf16[2,4,64,1024]{3,2,1,0:T(8,128)(2,1)S(1)}, u32[]{:S(2)}, u32[]{:S(2)}) collective-permute-start(bf16[2,4,64,1024]{3,2,1,0:T(8,128)(2,1)} %get-tuple-element.30.refs_2_), channel_id=1, source_target_pairs={{0,2},{2,0},{1,3},{3,1},{4,6},{6,4},{5,7},{7,5},{8,10},{10,8},{9,1... | collective-permute-start | bytes 3145736 | tf_op jit(solution)/shard_map/ppermute | solution.py:30
  145.5 64.3 %collective-permute-start.22 = (bf16[2,4,64,1024]{3,2,1,0:T(8,128)(2,1)}, bf16[2,4,64,1024]{3,2,1,0:T(8,128)(2,1)S(1)}, u32[]{:S(2)}, u32[]{:S(2)}) collective-permute-start(bf16[2,4,64,1024]{3,2,1,0:T(8,128)(2,1)} %collective-permute-done.21.refs_4_), channel_id=1, source_target_pairs={{0,96},{32,0},{64,32},{96,64},{1,97},{33,1},{65,33},{97,65},{2,98}... | collective-permute-start | bytes 3145736 | tf_op jit(solution)/shard_map/ppermute | solution.py:34
  201.1 40.5 %collective-permute-start.18 = (bf16[1024,512]{1,0:T(8,128)(2,1)S(1)}, bf16[1024,512]{1,0:T(8,128)(2,1)S(1)}, u32[]{:S(2)}, u32[]{:S(2)}) collective-permute-start(bf16[1024,512]{1,0:T(8,128)(2,1)S(1)} %shard_map.119), channel_id=1, source_target_pairs={{0,1},{1,0},{2,3},{3,2},{4,5},{5,4},{6,7},{7,6},{8,9},{9,8},{10,11... | collective-permute-start | bytes 3145736 | tf_op jit(solution)/shard_map/ppermute | solution.py:30
  209.0 31.8 %collective-permute-start.28 = (bf16[512,512]{1,0:T(8,128)(2,1)S(1)}, bf16[512,512]{1,0:T(8,128)(2,1)S(1)}, u32[]{:S(2)}, u32[]{:S(2)}) collective-permute-start(bf16[512,512]{1,0:T(8,128)(2,1)S(1)} %get-tuple-element.34), channel_id=1, source_target_pairs={{0,1},{1,0},{2,3},{3,2},{4,5},{5,4},{6,7},{7,6},{8,9},{9,8},{10,11... | collective-permute-start | bytes 1572872 | tf_op jit(solution)/shard_map/ppermute | solution.py:38
  209.1 63.8 %collective-permute-start.24 = (bf16[2,4,64,1024]{3,2,1,0:T(8,128)(2,1)}, bf16[2,4,64,1024]{3,2,1,0:T(8,128)(2,1)S(1)}, u32[]{:S(2)}, u32[]{:S(2)}) collective-permute-start(bf16[2,4,64,1024]{3,2,1,0:T(8,128)(2,1)} %collective-permute-done.20.refs_3_), channel_id=1, source_target_pairs={{0,2},{2,0},{1,3},{3,1},{4,6},{6,4},{5,7},{7,5},{8,10},{10,8},{9,1... | collective-permute-start | bytes 3145736 | tf_op jit(solution)/shard_map/ppermute | solution.py:30
  209.7 63.2 %collective-permute-start.25 = (bf16[2,4,64,1024]{3,2,1,0:T(8,128)(2,1)}, bf16[2,4,64,1024]{3,2,1,0:T(8,128)(2,1)S(1)}, u32[]{:S(2)}, u32[]{:S(2)}) collective-permute-start(bf16[2,4,64,1024]{3,2,1,0:T(8,128)(2,1)} %collective-permute-done.21.refs_4_), channel_id=1, source_target_pairs={{0,2},{2,0},{1,3},{3,1},{4,6},{6,4},{5,7},{7,5},{8,10},{10,8},{9,1... | collective-permute-start | bytes 3145736 | tf_op jit(solution)/shard_map/ppermute | solution.py:30
  209.8 63.1 %collective-permute-start.26 = (bf16[2,4,64,1024]{3,2,1,0:T(8,128)(2,1)S(1)}, bf16[2,4,64,1024]{3,2,1,0:T(8,128)(2,1)S(1)}, u32[]{:S(2)}, u32[]{:S(2)}) collective-permute-start(bf16[2,4,64,1024]{3,2,1,0:T(8,128)(2,1)S(1)} %collective-permute-done.22.refs_5_), channel_id=1, source_target_pairs={{0,2},{2,0},{1,3},{3,1},{4,6},{6,4},{5,7},{7,5},{8,10},{10,8},{9,1... | collective-permute-start | bytes 3145736 | tf_op jit(solution)/shard_map/ppermute | solution.py:30
  240.8 29.0 %collective-permute-start.29 = (bf16[512,512]{1,0:T(8,128)(2,1)S(1)}, bf16[512,512]{1,0:T(8,128)(2,1)S(1)}, u32[]{:S(2)}, u32[]{:S(2)}) collective-permute-start(bf16[512,512]{1,0:T(8,128)(2,1)S(1)} %get-tuple-element.35), channel_id=1, source_target_pairs={{0,2},{1,3},{2,0},{3,1},{4,6},{5,7},{6,4},{7,5},{8,10},{9,11},{10,... | collective-permute-start | bytes 1572872 | tf_op jit(solution)/shard_map/ppermute | solution.py:38
  241.6 28.8 %collective-permute-start.30 = (bf16[512,512]{1,0:T(8,128)(2,1)S(1)}, bf16[512,512]{1,0:T(8,128)(2,1)S(1)}, u32[]{:S(2)}, u32[]{:S(2)}) collective-permute-start(bf16[512,512]{1,0:T(8,128)(2,1)S(1)} %get-tuple-element.36), channel_id=1, source_target_pairs={{0,3},{1,2},{2,1},{3,0},{4,7},{5,6},{6,5},{7,4},{8,11},{9,10},{10,... | collective-permute-start | bytes 1572872 | tf_op jit(solution)/shard_map/ppermute | solution.py:38
  (26 other events, 314.8 us)

commit v2 on v1

--- a/solution.py
+++ b/solution.py
@@ -63,10 +63,10 @@
             out_ref[copy, :, 1024:] = o_ref[:, first : first + 1024]
 
 
-def split_kernel(here, level_ref, kv_ref, rest_ref):
+def split_kernel(here, level_ref, kv_ref, q_ref, o_ref):
     kv_ref[...] = level_ref[:, :, 512:1024]
-    rest_ref[:, :, :512] = level_ref[:, :, :512]
-    rest_ref[:, :, 512:] = level_ref[:, :, 1024:]
+    q_ref[...] = level_ref[:, :, :512]
+    o_ref[...] = level_ref[:, :, 1024:]
 
 
 def arrange_kernel(here, *refs):
@@ -188,11 +188,11 @@
                 )
         store(result, turned, *out_refs)
 
-    @pl.when(step < 2)
+    @pl.when(step == 0)
     def _():
         body(x_refs[0])
 
-    @pl.when(step >= 2)
+    @pl.when(step == 1)
     def _():
         body(x_refs[1])
 
@@ -214,10 +214,10 @@
 
 
 def project(meta, sides, parts, tables, pair, kind):
-    tile = 256
+    tile = TOK
 
     def table(i, m):
-        return (jnp.bitwise_xor(m[0], 2 * (i // 2) + pair) * 2 + i % 2, 0)
+        return (jnp.bitwise_xor(m[0], 2 * i + pair), 0)
 
     if kind == "q":
         store = store_queries
@@ -239,11 +239,8 @@
         functools.partial(project_kernel, store),
         grid_spec=pltpu.PrefetchScalarGridSpec(
             num_scalar_prefetch=1,
-            grid=(4,),
-            in_specs=[
-                pl.BlockSpec((tile, DEPTH), lambda i, m: (jnp.minimum(i, 1), 0)),
-                pl.BlockSpec((tile, DEPTH), lambda i, m: (jnp.maximum(i - 2, 0), 0)),
-            ]
+            grid=(2,),
+            in_specs=[pl.BlockSpec((tile, DEPTH), lambda i, m: (0, 0))] * 2
             + [INSIDE] * 4
             + [pl.BlockSpec((tile, 128), table)] * 2,
             out_specs=out_specs,
@@ -555,18 +552,18 @@
     level = lax.all_to_all(
         slices, ("zl", "c", "zh"), split_axis=0, concat_axis=0, tiled=True
     ).reshape(2, 64, 2048)
-    kv_level, rest = small(split_kernel, here, (level,), [(2, 64, 512), (2, 64, 1536)])
+    kv_level, q_level, o_level = small(
+        split_kernel, here, (level,), [(2, 64, 512), (2, 64, 512), (2, 64, 1024)]
+    )
     kv_row = small(
         column_kernel, here, ring_pieces(kv_level, "y"), [(4, 2, 64, 512)]
     )[0]
     kv_parts = ring_pieces(kv_row, "x")
-    q_row, o_row = small(
-        arrange_kernel,
-        here,
-        ring_pieces(after(rest, kv_row), "x"),
-        [(2, 4, 64, 512), (2, 4, 64, 1024)],
-    )
+    q_row = small(arrange_kernel, here, ring_pieces(q_level, "x"), [(2, 4, 64, 512)])[0]
     q_parts = ring_pieces(q_row, "y")
+    o_row = small(
+        arrange_kernel, here, ring_pieces(o_level, "x"), [(2, 4, 64, 1024)]
+    )[0]
     o_parts = ring_chain(o_row, "y")
 
     normed = normalize(after(hidden_in, slices), norm_gain)
@@ -583,14 +580,13 @@
 
     sides = ((normed, beside), (across, diagonal))
     keys, values, halo, queries = [], [], [], []
+    metas = (meta, tick(meta))
     for pair in range(2):
-        kvt, v = project(meta, sides[pair], kv_parts, tables, pair, "kv")
+        kvt, v = project(metas[pair], sides[pair], kv_parts, tables, pair, "kv")
         keys.append(kvt)
         values.append(v)
         halo.append(previous_quad(kvt))
-    later = after(tick(meta), *keys)
-    for pair in range(2):
-        queries += project(later, sides[pair], q_parts, tables, pair, "q")
+        queries += project(meta, sides[pair], q_parts, tables, pair, "q")
     packed = pack(meta, keys, values)
     pages = [packed[0]]
     for flip in (1, 2, 3):

time: 285 us -> 277 us (0.972)
  Pallas kernels: 83.4 us -> 75.5 us
  starting transfers between devices: 79 us -> 82.1 us
    pallas_call x2, Pallas kernels: 34 us -> 29.6 us  [attend(): pl.pallas_call(functools.partial(attend_kernel, pair), grid_spec=pltpu.Pr...]
    unnamed x36 -> x34, local copies, waits for them, and re-layouts: 6.67 us -> 3.23 us
    ppermute x2, starting transfers between devices: 7.29 us -> 10.5 us  [previous_quad(): return lax.ppermute(block, names, route)]
    ppermute x11, waiting for transfers between devices: 31.1 us -> 34.1 us  [swap(): return lax.ppermute(block, axis, [(0, 1), (1, 0)])]
    ppermute x15 -> x18, waiting for transfers between devices: 36.4 us -> 34.5 us  [shift(): lax.ppermute(block, axis, [(i, (i + distance) % 4) for i in range(4)])]
    ppermute x15 -> x18, starting transfers between devices: 48.4 us -> 48.4 us  [shift(): lax.ppermute(block, axis, [(i, (i + distance) % 4) for i in range(4)])]
  transfers between devices with their start and end apart: 32 -> 35, of which waited for: 11 -> 12; matrix products, arithmetic and copies ran while one was open for 4% -> 4% of each run, Pallas kernels for 27% -> 25%
where the time goes in v2:
time: 277 us
  waiting for transfers between devices  104 us (38%)
  starting transfers between devices  82.1 us (30%)
  Pallas kernels  75.5 us (27%)
  other arithmetic  9.55 us (3%)
  local copies, waits for them, and re-layouts  4.67 us (2%)
    ppermute x18, starting transfers between devices, shift(): lax.ppermute(block, axis, [(i, (i + distance) % 4) for i in range(4)])  48.4 us
    ppermute x18, waiting for transfers between devices, shift(): lax.ppermute(block, axis, [(i, (i + distance) % 4) for i in range(4)])  34.5 us
    ppermute x11, waiting for transfers between devices, swap(): return lax.ppermute(block, axis, [(0, 1), (1, 0)])  34.1 us
    ppermute x3, waiting for transfers between devices, to_role(): return lax.ppermute(block, QUAD, [(i, i ^ flip) for i in range(4)])  31.4 us
    pallas_call x2, Pallas kernels, attend(): pl.pallas_call(functools.partial(attend_kernel, pair), grid_spec=pltpu.Pr...  29.6 us
    pallas_call x4, Pallas kernels, project(): pl.pallas_call(functools.partial(project_kernel, store), grid_spec=pltpu....  24.7 us
    ppermute x11, starting transfers between devices, swap(): return lax.ppermute(block, axis, [(0, 1), (1, 0)])  13.6 us
    ppermute x2, starting transfers between devices, previous_quad(): return lax.ppermute(block, names, route)  10.5 us
  transfers between devices with their start and end apart: 35, of which 12 were waited for; matrix products, arithmetic and copies ran while one was open for 4% of the time, Pallas kernels for 25%

profile of v2, /device:TPU:57, one launch (start us, length us, event | category | flops | bytes accessed | tf_op | source)
XLA Modules:
  0.0 276.8 jit_solution(15274605729075479021)
XLA Ops:
  4.6 5.7 %all-to-all-start = ((bf16[8,16,2048]{2,1,0:T(8,128)(2,1)}), bf16[8,16,2048]{2,1,0:T(8,128)(2,1)S(1)}, u32[]{:S(2)}, u32[]{:S(2)}) async-start(bf16[8,16,2048]{2,1,0:T(8,128)(2,1)} %shard_map.112), calls=%async_computation | async-start | bytes 1048576 | tf_op jit(solution)/shard_map/all_to_all | solution.py:552
  14.3 4.0 %all-to-all-done = bf16[8,16,2048]{2,1,0:T(8,128)(2,1)S(1)} async-done(((bf16[8,16,2048]{2,1,0:T(8,128)(2,1)}), bf16[8,16,2048]{2,1,0:T(8,128)(2,1)S(1)}, u32[]{:S(2)}, u32[]{:S(2)}) %all-to-all-start) | async-done | bytes 524320 | tf_op jit(solution)/shard_map/all_to_all | solution.py:552
  23.7 2.8 %collective-permute-done.10.refs_1_ = bf16[2,64,512]{2,1,0:T(8,128)(2,1)S(1)} collective-permute-done((bf16[2,64,512]{2,1,0:T(8,128)(2,1)S(1)}, bf16[2,64,512]{2,1,0:T(8,128)(2,1)S(1)}, u32[]{:S(2)}, u32[]{:S(2)}) %collective-permute-start.10) | collective-permute-done | bytes 131104 | tf_op jit(solution)/shard_map/ppermute | solution.py:34
  33.4 34.0 %collective-permute-done.1.refs_0_ = bf16[512,2048]{1,0:T(8,128)(2,1)} collective-permute-done((bf16[512,2048]{1,0:T(8,128)(2,1)}, bf16[512,2048]{1,0:T(8,128)(2,1)}, u32[]{:S(2)}, u32[]{:S(2)}) %collective-permute-start.1) | collective-permute-done | bytes 2097184 | tf_op jit(solution)/shard_map/ppermute | solution.py:30
  68.1 3.7 %fusion.3 = (f32[2048,64]{1,0:T(8,128)S(1)}, f32[2048,64]{1,0:T(8,128)S(1)}, f32[2048,64]{1,0:T(8,128)S(1)}) fusion(f32[64]{0:T(128)S(1)} %multiply_power_fusion, f32[2048]{0:T(1024)S(1)} %convert_bitcast_fusion), kind=kLoop, calls=%fused_computation.9 | loop fusion | flops 262144 | bytes 1581312 | tf_op jit(solution)/shard_map/neg | solution.py:151
  79.2 2.8 %collective-permute-done.4.refs_2_ = bf16[2,64,512]{2,1,0:T(8,128)(2,1)S(1)} collective-permute-done((bf16[2,64,512]{2,1,0:T(8,128)(2,1)S(1)}, bf16[2,64,512]{2,1,0:T(8,128)(2,1)S(1)}, u32[]{:S(2)}, u32[]{:S(2)}) %collective-permute-start.4) | collective-permute-done | bytes 131104 | tf_op jit(solution)/shard_map/ppermute | solution.py:34
  83.5 2.8 %collective-permute-done.5.refs_3_ = bf16[2,64,512]{2,1,0:T(8,128)(2,1)} collective-permute-done((bf16[2,64,512]{2,1,0:T(8,128)(2,1)S(1)}, bf16[2,64,512]{2,1,0:T(8,128)(2,1)}, u32[]{:S(2)}, u32[]{:S(2)}) %collective-permute-start.5) | collective-permute-done | bytes 131104 | tf_op jit(solution)/shard_map/ppermute | solution.py:34
  88.2 5.0 %collective-permute-done.13.refs_3_ = bf16[4,2,64,512]{3,2,1,0:T(8,128)(2,1)} collective-permute-done((bf16[4,2,64,512]{3,2,1,0:T(8,128)(2,1)}, bf16[4,2,64,512]{3,2,1,0:T(8,128)(2,1)}, u32[]{:S(2)}, u32[]{:S(2)}) %collective-permute-start.13) | collective-permute-done | bytes 524320 | tf_op jit(solution)/shard_map/ppermute | solution.py:34
  97.8 6.7 %collective-permute-done.14.refs_4_ = bf16[4,2,64,512]{3,2,1,0:T(8,128)(2,1)} collective-permute-done((bf16[4,2,64,512]{3,2,1,0:T(8,128)(2,1)}, bf16[4,2,64,512]{3,2,1,0:T(8,128)(2,1)}, u32[]{:S(2)}, u32[]{:S(2)}) %collective-permute-start.14) | collective-permute-done | bytes 524320 | tf_op jit(solution)/shard_map/ppermute | solution.py:34
  107.8 6.5 %shard_map.117 = (bf16[4,1024,128]{2,1,0:T(8,128)(2,1)S(1)}, bf16[2,1024,128]{2,1,0:T(8,128)(2,1)S(1)}) custom-call(s32[51]{0:T(128)S(1)} %copy-done.4, bf16[512,2048]{1,0:T(8,128)(2,1)} %fusion.2.refs_0_, bf16[512,2048]{1,0:T(8,128)(2,1)} %collective-permute-done.9.refs_1_, bf16[4,2,64,512]{3,2,1,0:T(8,128)(2,1)} %shard_map.116.refs_2_, ...), custom_call_target="tpu_custom_call" | custom-call | flops 2147483648 | bytes 8388608 | tf_op jit(solution)/shard_map/pallas_call | solution.py:238
  114.3 8.6 %collective-permute-start.16 = (bf16[4,1024,128]{2,1,0:T(8,128)(2,1)S(1)}, bf16[4,1024,128]{2,1,0:T(8,128)(2,1)S(1)}, u32[]{:S(2)}, u32[]{:S(2)}) collective-permute-start(bf16[4,1024,128]{2,1,0:T(8,128)(2,1)S(1)} %get-tuple-element.22.refs_1_.refs_0_), channel_id=1, source_target_pairs={{0,4},{1,5},{2,6},{3,7},{4,8},{5,9},{6,10},{7,11},{8,12},{9,13},{1... | collective-permute-start | bytes 3145736 | tf_op jit(solution)/shard_map/ppermute | solution.py:540
  123.0 6.6 %shard_map.118 = (bf16[4,1024,128]{2,1,0:T(8,128)(2,1)S(1)}, bf16[2,1024,128]{2,1,0:T(8,128)(2,1)S(1)}) custom-call(s32[51]{0:T(128)S(1)} %copy-done.7, bf16[512,2048]{1,0:T(8,128)(2,1)} %collective-permute-done.1.refs_0_, bf16[512,2048]{1,0:T(8,128)(2,1)} %collective-permute-done.2.refs_1_, bf16[4,2,64,512]{3,2,1,0:T(8,128)(2,1)} %shard_map.116.refs_2_, ...), custom_call_target="tpu_custom_call" | custom-call | flops 2147483648 | bytes 8388608 | tf_op jit(solution)/shard_map/pallas_call | solution.py:238
  132.6 12.7 %collective-permute-done.7.refs_4_ = bf16[2,4,64,512]{3,2,1,0:T(8,128)(2,1)S(1)} collective-permute-done((bf16[2,4,64,512]{3,2,1,0:T(8,128)(2,1)S(1)}, bf16[2,4,64,512]{3,2,1,0:T(8,128)(2,1)S(1)}, u32[]{:S(2)}, u32[]{:S(2)}) %collective-permute-start.7) | collective-permute-done | bytes 524320 | tf_op jit(solution)/shard_map/ppermute | solution.py:34
  145.3 4.0 %collective-permute-start.26 = (bf16[2,4,64,1024]{3,2,1,0:T(8,128)(2,1)S(1)}, bf16[2,4,64,1024]{3,2,1,0:T(8,128)(2,1)S(1)}, u32[]{:S(2)}, u32[]{:S(2)}) collective-permute-start(bf16[2,4,64,1024]{3,2,1,0:T(8,128)(2,1)S(1)} %shard_map.120.refs_2_), channel_id=1, source_target_pairs={{0,2},{2,0},{1,3},{3,1},{4,6},{6,4},{5,7},{7,5},{8,10},{10,8},{9,1... | collective-permute-start | bytes 3145736 | tf_op jit(solution)/shard_map/ppermute | solution.py:30
  149.3 29.7 %collective-permute-start.25 = (bf16[2,4,64,1024]{3,2,1,0:T(8,128)(2,1)S(1)}, bf16[2,4,64,1024]{3,2,1,0:T(8,128)(2,1)S(1)}, u32[]{:S(2)}, u32[]{:S(2)}) collective-permute-start(bf16[2,4,64,1024]{3,2,1,0:T(8,128)(2,1)S(1)} %collective-permute-done.24.refs_4_), channel_id=1, source_target_pairs={{0,96},{32,0},{64,32},{96,64},{1,97},{33,1},{65,33},{97,65},{2,98}... | collective-permute-start | bytes 3145736 | tf_op jit(solution)/shard_map/ppermute | solution.py:34
  179.0 5.8 %shard_map.115.refs_0_ = bf16[1024,512]{1,0:T(8,128)(2,1)S(1)} custom-call(s32[51]{0:T(128)S(1)} %copy-done.4, bf16[512,2048]{1,0:T(8,128)(2,1)} %collective-permute-done.1.refs_0_, bf16[512,2048]{1,0:T(8,128)(2,1)} %collective-permute-done.2.refs_1_, bf16[2,4,64,512]{3,2,1,0:T(8,128)(2,1)S(1)} %shard_map.114.refs_2_, ...), custom_call_target="tpu_custom_call" | custom-call | flops 2147483648 | bytes 8388608 | tf_op jit(solution)/shard_map/pallas_call | solution.py:238
  184.9 12.7 %shard_map.119 = bf16[1024,512]{1,0:T(8,128)(2,1)S(1)} custom-call(s32[51]{0:T(128)S(1)} %copy-done.4, bf16[1024,512]{1,0:T(8,128)(2,1)S(1)} %shard_map.115.refs_0_, bf16[4,1024,128]{2,1,0:T(8,128)(2,1)S(1)} %get-tuple-element.22.refs_1_.refs_0_, bf16[4,1024,128]{2,1,0:T(8,128)(2,1)S(1)} %get-tuple-element.23.refs_2_.refs_1_, ...), custom_call_target="tpu_custom_call" | custom-call | flops 4294967296 | bytes 6291456 | tf_op jit(solution)/shard_map/pallas_call | solution.py:364
  197.6 4.6 %collective-permute-start.18 = (bf16[1024,512]{1,0:T(8,128)(2,1)S(1)}, bf16[1024,512]{1,0:T(8,128)(2,1)S(1)}, u32[]{:S(2)}, u32[]{:S(2)}) collective-permute-start(bf16[1024,512]{1,0:T(8,128)(2,1)S(1)} %shard_map.119), channel_id=1, source_target_pairs={{0,1},{1,0},{2,3},{3,2},{4,5},{5,4},{6,7},{7,6},{8,9},{9,8},{10,11... | collective-permute-start | bytes 3145736 | tf_op jit(solution)/shard_map/ppermute | solution.py:30
  205.3 31.4 %collective-permute-done.31.refs_1_ = bf16[512,512]{1,0:T(8,128)(2,1)S(1)} collective-permute-done((bf16[512,512]{1,0:T(8,128)(2,1)S(1)}, bf16[512,512]{1,0:T(8,128)(2,1)S(1)}, u32[]{:S(2)}, u32[]{:S(2)}) %collective-permute-start.31) | collective-permute-done | bytes 524320 | tf_op jit(solution)/shard_map/ppermute | solution.py:38
  237.6 2.9 %collective-permute-start.33 = (bf16[512,512]{1,0:T(8,128)(2,1)S(1)}, bf16[512,512]{1,0:T(8,128)(2,1)S(1)}, u32[]{:S(2)}, u32[]{:S(2)}) collective-permute-start(bf16[512,512]{1,0:T(8,128)(2,1)S(1)} %get-tuple-element.30), channel_id=1, source_target_pairs={{0,3},{1,2},{2,1},{3,0},{4,7},{5,6},{6,5},{7,4},{8,11},{9,10},{10,... | collective-permute-start | bytes 1572872 | tf_op jit(solution)/shard_map/ppermute | solution.py:38
  240.6 5.8 %shard_map.121.refs_0_ = bf16[1024,512]{1,0:T(8,128)(2,1)S(1)} custom-call(s32[51]{0:T(128)S(1)} %copy-done.5, bf16[512,2048]{1,0:T(8,128)(2,1)} %fusion.2.refs_0_, bf16[512,2048]{1,0:T(8,128)(2,1)} %collective-permute-done.9.refs_1_, bf16[2,4,64,512]{3,2,1,0:T(8,128)(2,1)S(1)} %shard_map.114.refs_2_, ...), custom_call_target="tpu_custom_call" | custom-call | flops 2147483648 | bytes 8388608 | tf_op jit(solution)/shard_map/pallas_call | solution.py:238
  246.4 16.9 %shard_map.122.refs_0_ = bf16[1024,512]{1,0:T(8,128)(2,1)S(1)} custom-call(s32[51]{0:T(128)S(1)} %copy-done.5, bf16[1024,512]{1,0:T(8,128)(2,1)S(1)} %shard_map.121.refs_0_, bf16[4,1024,128]{2,1,0:T(8,128)(2,1)S(1)} %get-tuple-element.22.refs_1_.refs_0_, bf16[4,1024,128]{2,1,0:T(8,128)(2,1)S(1)} %copy-done.1, bf16[4,1024,128]{2,1,0:T(8,128)(2,1)S(1)} %copy-done.9, ...), custom_call_target="tpu_custom_call" | custom-call | flops 4294967296 | bytes 6291456 | tf_op jit(solution)/shard_map/pallas_call | solution.py:364
  266.5 4.5 %output_near.1.refs_10_ = f32[2,512,1024]{2,1,0:T(8,128)S(1)} custom-call(s32[51]{0:T(128)S(1)} %copy-done.5, bf16[1024,512]{1,0:T(8,128)(2,1)S(1)} %shard_map.122.refs_0_, bf16[512,512]{1,0:T(8,128)(2,1)S(1)} %collective-permute-done.30.refs_1_, bf16[2,4,64,1024]{3,2,1,0:T(8,128)(2,1)S(1)} %shard_map.120.refs_2_, ...), custom_call_target="tpu_custom_call" | custom-call | tf_op jit(solution)/shard_map/output_near/pallas_call | solution.py:493
  271.0 5.8 %output_far.1 = bf16[512,2048]{1,0:T(8,128)(2,1)} custom-call(s32[51]{0:T(128)S(1)} %copy-done.5, bf16[1024,512]{1,0:T(8,128)(2,1)S(1)} %collective-permute-done.18.refs_0_, bf16[512,512]{1,0:T(8,128)(2,1)S(1)} %collective-permute-done.19.refs_1_, bf16[2,4,64,1024]{3,2,1,0:T(8,128)(2,1)S(1)} %shard_map.120.refs_2_, ...), custom_call_target="tpu_custom_call" | custom-call | tf_op jit(solution)/shard_map/output_far/pallas_call | solution.py:509
  (120 shorter events, 49.6 us)
Async XLA Ops:
  18.2 49.3 %collective-permute-start.1 = (bf16[512,2048]{1,0:T(8,128)(2,1)}, bf16[512,2048]{1,0:T(8,128)(2,1)}, u32[]{:S(2)}, u32[]{:S(2)}) collective-permute-start(bf16[512,2048]{1,0:T(8,128)(2,1)} %fusion.2.refs_0_), channel_id=1, source_target_pairs={{0,1},{1,0},{2,3},{3,2},{4,5},{5,4},{6,7},{7,6},{8,9},{9,8},{10,11... | collective-permute-start | bytes 6291464 | tf_op jit(solution)/shard_map/ppermute | solution.py:30
  19.1 88.0 %collective-permute-start.9 = (bf16[512,2048]{1,0:T(8,128)(2,1)}, bf16[512,2048]{1,0:T(8,128)(2,1)}, u32[]{:S(2)}, u32[]{:S(2)}) collective-permute-start(bf16[512,2048]{1,0:T(8,128)(2,1)} %fusion.2.refs_0_), channel_id=1, source_target_pairs={{0,2},{2,0},{1,3},{3,1},{4,6},{6,4},{5,7},{7,5},{8,10},{10,8},{9,1... | collective-permute-start | bytes 6291464 | tf_op jit(solution)/shard_map/ppermute | solution.py:30
  26.5 45.3 %collective-permute-start.20 = (bf16[2,64,1024]{2,1,0:T(8,128)(2,1)S(1)}, bf16[2,64,1024]{2,1,0:T(8,128)(2,1)S(1)}, u32[]{:S(2)}, u32[]{:S(2)}) collective-permute-start(bf16[2,64,1024]{2,1,0:T(8,128)(2,1)S(1)} %get-tuple-element.24.refs_0_), channel_id=1, source_target_pairs={{0,4},{4,8},{8,12},{12,0},{1,5},{5,9},{9,13},{13,1},{2,6},{6,10},{... | collective-permute-start | bytes 786440 | tf_op jit(solution)/shard_map/ppermute | solution.py:34
  27.9 47.0 %collective-permute-start.21 = (bf16[2,64,1024]{2,1,0:T(8,128)(2,1)S(1)}, bf16[2,64,1024]{2,1,0:T(8,128)(2,1)S(1)}, u32[]{:S(2)}, u32[]{:S(2)}) collective-permute-start(bf16[2,64,1024]{2,1,0:T(8,128)(2,1)S(1)} %get-tuple-element.24.refs_0_), channel_id=1, source_target_pairs={{0,8},{4,12},{8,0},{12,4},{1,9},{5,13},{9,1},{13,5},{2,10},{6,14},... | collective-permute-start | bytes 786440 | tf_op jit(solution)/shard_map/ppermute | solution.py:34
  31.0 44.2 %collective-permute-start.22 = (bf16[2,64,1024]{2,1,0:T(8,128)(2,1)S(1)}, bf16[2,64,1024]{2,1,0:T(8,128)(2,1)S(1)}, u32[]{:S(2)}, u32[]{:S(2)}) collective-permute-start(bf16[2,64,1024]{2,1,0:T(8,128)(2,1)S(1)} %get-tuple-element.24.refs_0_), channel_id=1, source_target_pairs={{0,12},{4,0},{8,4},{12,8},{1,13},{5,1},{9,5},{13,9},{2,14},{6,2},{... | collective-permute-start | bytes 786440 | tf_op jit(solution)/shard_map/ppermute | solution.py:34
  67.5 55.5 %collective-permute-start.2 = (bf16[512,2048]{1,0:T(8,128)(2,1)}, bf16[512,2048]{1,0:T(8,128)(2,1)}, u32[]{:S(2)}, u32[]{:S(2)}) collective-permute-start(bf16[512,2048]{1,0:T(8,128)(2,1)} %collective-permute-done.1.refs_0_), channel_id=1, source_target_pairs={{0,2},{2,0},{1,3},{3,1},{4,6},{6,4},{5,7},{7,5},{8,10},{10,8},{9,1... | collective-permute-start | bytes 6291464 | tf_op jit(solution)/shard_map/ppermute | solution.py:30
  78.2 14.9 %collective-permute-start.13 = (bf16[4,2,64,512]{3,2,1,0:T(8,128)(2,1)}, bf16[4,2,64,512]{3,2,1,0:T(8,128)(2,1)}, u32[]{:S(2)}, u32[]{:S(2)}) collective-permute-start(bf16[4,2,64,512]{3,2,1,0:T(8,128)(2,1)} %shard_map.116.refs_2_), channel_id=1, source_target_pairs={{0,4},{4,8},{8,12},{12,0},{1,5},{5,9},{9,13},{13,1},{2,6},{6,10},{... | collective-permute-start | bytes 1572872 | tf_op jit(solution)/shard_map/ppermute | solution.py:34
  78.3 26.1 %collective-permute-start.23 = (bf16[2,4,64,1024]{3,2,1,0:T(8,128)(2,1)S(1)}, bf16[2,4,64,1024]{3,2,1,0:T(8,128)(2,1)}, u32[]{:S(2)}, u32[]{:S(2)}) collective-permute-start(bf16[2,4,64,1024]{3,2,1,0:T(8,128)(2,1)S(1)} %shard_map.120.refs_2_), channel_id=1, source_target_pairs={{0,96},{32,0},{64,32},{96,64},{1,97},{33,1},{65,33},{97,65},{2,98}... | collective-permute-start | bytes 3145736 | tf_op jit(solution)/shard_map/ppermute | solution.py:34
  86.3 18.2 %collective-permute-start.14 = (bf16[4,2,64,512]{3,2,1,0:T(8,128)(2,1)}, bf16[4,2,64,512]{3,2,1,0:T(8,128)(2,1)}, u32[]{:S(2)}, u32[]{:S(2)}) collective-permute-start(bf16[4,2,64,512]{3,2,1,0:T(8,128)(2,1)} %shard_map.116.refs_2_), channel_id=1, source_target_pairs={{0,8},{4,12},{8,0},{12,4},{1,9},{5,13},{9,1},{13,5},{2,10},{6,14},... | collective-permute-start | bytes 1572872 | tf_op jit(solution)/shard_map/ppermute | solution.py:34
  93.2 13.9 %collective-permute-start.15 = (bf16[4,2,64,512]{3,2,1,0:T(8,128)(2,1)}, bf16[4,2,64,512]{3,2,1,0:T(8,128)(2,1)}, u32[]{:S(2)}, u32[]{:S(2)}) collective-permute-start(bf16[4,2,64,512]{3,2,1,0:T(8,128)(2,1)} %shard_map.116.refs_2_), channel_id=1, source_target_pairs={{0,12},{4,0},{8,4},{12,8},{1,13},{5,1},{9,5},{13,9},{2,14},{6,2},{... | collective-permute-start | bytes 1572872 | tf_op jit(solution)/shard_map/ppermute | solution.py:34
  104.5 28.1 %collective-permute-start.6 = (bf16[2,4,64,512]{3,2,1,0:T(8,128)(2,1)S(1)}, bf16[2,4,64,512]{3,2,1,0:T(8,128)(2,1)S(1)}, u32[]{:S(2)}, u32[]{:S(2)}) collective-permute-start(bf16[2,4,64,512]{3,2,1,0:T(8,128)(2,1)S(1)} %shard_map.114.refs_2_), channel_id=1, source_target_pairs={{0,32},{32,64},{64,96},{96,0},{1,33},{33,65},{65,97},{97,1},{2,34}... | collective-permute-start | bytes 1572872 | tf_op jit(solution)/shard_map/ppermute | solution.py:34
  104.5 44.8 %collective-permute-start.24 = (bf16[2,4,64,1024]{3,2,1,0:T(8,128)(2,1)}, bf16[2,4,64,1024]{3,2,1,0:T(8,128)(2,1)S(1)}, u32[]{:S(2)}, u32[]{:S(2)}) collective-permute-start(bf16[2,4,64,1024]{3,2,1,0:T(8,128)(2,1)} %collective-permute-done.23.refs_3_), channel_id=1, source_target_pairs={{0,96},{32,0},{64,32},{96,64},{1,97},{33,1},{65,33},{97,65},{2,98}... | collective-permute-start | bytes 3145736 | tf_op jit(solution)/shard_map/ppermute | solution.py:34
  114.3 70.5 %collective-permute-start.16 = (bf16[4,1024,128]{2,1,0:T(8,128)(2,1)S(1)}, bf16[4,1024,128]{2,1,0:T(8,128)(2,1)S(1)}, u32[]{:S(2)}, u32[]{:S(2)}) collective-permute-start(bf16[4,1024,128]{2,1,0:T(8,128)(2,1)S(1)} %get-tuple-element.22.refs_1_.refs_0_), channel_id=1, source_target_pairs={{0,4},{1,5},{2,6},{3,7},{4,8},{5,9},{6,10},{7,11},{8,12},{9,13},{1... | collective-permute-start | bytes 3145736 | tf_op jit(solution)/shard_map/ppermute | solution.py:540
  129.6 55.3 %collective-permute-start.17 = (bf16[4,1024,128]{2,1,0:T(8,128)(2,1)S(1)}, bf16[4,1024,128]{2,1,0:T(8,128)(2,1)S(1)}, u32[]{:S(2)}, u32[]{:S(2)}) collective-permute-start(bf16[4,1024,128]{2,1,0:T(8,128)(2,1)S(1)} %get-tuple-element.23.refs_2_.refs_1_), channel_id=1, source_target_pairs={{0,4},{1,5},{2,6},{3,7},{4,8},{5,9},{6,10},{7,11},{8,12},{9,13},{1... | collective-permute-start | bytes 3145736 | tf_op jit(solution)/shard_map/ppermute | solution.py:540
  132.6 46.5 %collective-permute-start.8 = (bf16[2,4,64,512]{3,2,1,0:T(8,128)(2,1)S(1)}, bf16[2,4,64,512]{3,2,1,0:T(8,128)(2,1)S(1)}, u32[]{:S(2)}, u32[]{:S(2)}) collective-permute-start(bf16[2,4,64,512]{3,2,1,0:T(8,128)(2,1)S(1)} %shard_map.114.refs_2_), channel_id=1, source_target_pairs={{0,96},{32,0},{64,32},{96,64},{1,97},{33,1},{65,33},{97,65},{2,98}... | collective-permute-start | bytes 1572872 | tf_op jit(solution)/shard_map/ppermute | solution.py:34
  145.3 59.5 %collective-permute-start.26 = (bf16[2,4,64,1024]{3,2,1,0:T(8,128)(2,1)S(1)}, bf16[2,4,64,1024]{3,2,1,0:T(8,128)(2,1)S(1)}, u32[]{:S(2)}, u32[]{:S(2)}) collective-permute-start(bf16[2,4,64,1024]{3,2,1,0:T(8,128)(2,1)S(1)} %shard_map.120.refs_2_), channel_id=1, source_target_pairs={{0,2},{2,0},{1,3},{3,1},{4,6},{6,4},{5,7},{7,5},{8,10},{10,8},{9,1... | collective-permute-start | bytes 3145736 | tf_op jit(solution)/shard_map/ppermute | solution.py:30
  149.3 55.5 %collective-permute-start.25 = (bf16[2,4,64,1024]{3,2,1,0:T(8,128)(2,1)S(1)}, bf16[2,4,64,1024]{3,2,1,0:T(8,128)(2,1)S(1)}, u32[]{:S(2)}, u32[]{:S(2)}) collective-permute-start(bf16[2,4,64,1024]{3,2,1,0:T(8,128)(2,1)S(1)} %collective-permute-done.24.refs_4_), channel_id=1, source_target_pairs={{0,96},{32,0},{64,32},{96,64},{1,97},{33,1},{65,33},{97,65},{2,98}... | collective-permute-start | bytes 3145736 | tf_op jit(solution)/shard_map/ppermute | solution.py:34
  197.6 40.0 %collective-permute-start.18 = (bf16[1024,512]{1,0:T(8,128)(2,1)S(1)}, bf16[1024,512]{1,0:T(8,128)(2,1)S(1)}, u32[]{:S(2)}, u32[]{:S(2)}) collective-permute-start(bf16[1024,512]{1,0:T(8,128)(2,1)S(1)} %shard_map.119), channel_id=1, source_target_pairs={{0,1},{1,0},{2,3},{3,2},{4,5},{5,4},{6,7},{7,6},{8,9},{9,8},{10,11... | collective-permute-start | bytes 3145736 | tf_op jit(solution)/shard_map/ppermute | solution.py:30
  204.1 32.6 %collective-permute-start.31 = (bf16[512,512]{1,0:T(8,128)(2,1)S(1)}, bf16[512,512]{1,0:T(8,128)(2,1)S(1)}, u32[]{:S(2)}, u32[]{:S(2)}) collective-permute-start(bf16[512,512]{1,0:T(8,128)(2,1)S(1)} %get-tuple-element.28), channel_id=1, source_target_pairs={{0,1},{1,0},{2,3},{3,2},{4,5},{5,4},{6,7},{7,6},{8,9},{9,8},{10,11... | collective-permute-start | bytes 1572872 | tf_op jit(solution)/shard_map/ppermute | solution.py:38
  204.1 62.4 %collective-permute-start.27 = (bf16[2,4,64,1024]{3,2,1,0:T(8,128)(2,1)}, bf16[2,4,64,1024]{3,2,1,0:T(8,128)(2,1)S(1)}, u32[]{:S(2)}, u32[]{:S(2)}) collective-permute-start(bf16[2,4,64,1024]{3,2,1,0:T(8,128)(2,1)} %collective-permute-done.23.refs_3_), channel_id=1, source_target_pairs={{0,2},{2,0},{1,3},{3,1},{4,6},{6,4},{5,7},{7,5},{8,10},{10,8},{9,1... | collective-permute-start | bytes 3145736 | tf_op jit(solution)/shard_map/ppermute | solution.py:30
  204.7 61.8 %collective-permute-start.28 = (bf16[2,4,64,1024]{3,2,1,0:T(8,128)(2,1)S(1)}, bf16[2,4,64,1024]{3,2,1,0:T(8,128)(2,1)S(1)}, u32[]{:S(2)}, u32[]{:S(2)}) collective-permute-start(bf16[2,4,64,1024]{3,2,1,0:T(8,128)(2,1)S(1)} %collective-permute-done.24.refs_4_), channel_id=1, source_target_pairs={{0,2},{2,0},{1,3},{3,1},{4,6},{6,4},{5,7},{7,5},{8,10},{10,8},{9,1... | collective-permute-start | bytes 3145736 | tf_op jit(solution)/shard_map/ppermute | solution.py:30
  204.8 61.7 %collective-permute-start.29 = (bf16[2,4,64,1024]{3,2,1,0:T(8,128)(2,1)S(1)}, bf16[2,4,64,1024]{3,2,1,0:T(8,128)(2,1)S(1)}, u32[]{:S(2)}, u32[]{:S(2)}) collective-permute-start(bf16[2,4,64,1024]{3,2,1,0:T(8,128)(2,1)S(1)} %collective-permute-done.25.refs_5_), channel_id=1, source_target_pairs={{0,2},{2,0},{1,3},{3,1},{4,6},{6,4},{5,7},{7,5},{8,10},{10,8},{9,1... | collective-permute-start | bytes 3145736 | tf_op jit(solution)/shard_map/ppermute | solution.py:30
  236.7 26.7 %collective-permute-start.32 = (bf16[512,512]{1,0:T(8,128)(2,1)}, bf16[512,512]{1,0:T(8,128)(2,1)S(1)}, u32[]{:S(2)}, u32[]{:S(2)}) collective-permute-start(bf16[512,512]{1,0:T(8,128)(2,1)} %get-tuple-element.29), channel_id=1, source_target_pairs={{0,2},{1,3},{2,0},{3,1},{4,6},{5,7},{6,4},{7,5},{8,10},{9,11},{10,... | collective-permute-start | bytes 1572872 | tf_op jit(solution)/shard_map/ppermute | solution.py:38
  237.6 26.3 %collective-permute-start.33 = (bf16[512,512]{1,0:T(8,128)(2,1)S(1)}, bf16[512,512]{1,0:T(8,128)(2,1)S(1)}, u32[]{:S(2)}, u32[]{:S(2)}) collective-permute-start(bf16[512,512]{1,0:T(8,128)(2,1)S(1)} %get-tuple-element.30), channel_id=1, source_target_pairs={{0,3},{1,2},{2,1},{3,0},{4,7},{5,6},{6,5},{7,4},{8,11},{9,10},{10,... | collective-permute-start | bytes 1572872 | tf_op jit(solution)/shard_map/ppermute | solution.py:38
  (28 other events, 289.4 us)

commit v3 on v2

--- a/solution.py
+++ b/solution.py
@@ -47,8 +47,9 @@
 
 def ring_chain(block, axis):
     pieces = [block]
-    for _ in range(3):
+    for _ in range(2):
         pieces.append(shift(pieces[-1], axis, -1))
+    pieces.append(shift(block, axis, 1))
     return pieces
 
 
@@ -254,33 +255,16 @@
     )(meta, *sides, *parts, *tables)
 
 
-def attend_kernel(pair, meta, *refs):
-    q_ref, own, halo, out_ref, kvt, saved, bias = (
-        refs[0], refs[1:3], refs[3:5], *refs[5:]
-    )
+def attend_pages(pair, mode, meta, q_ref, out_ref, kvt, saved, bias, parts):
     role = meta[0]
-    for p in range(4):
-        block = jnp.bitwise_xor(role, 2 * (p % 2) + p // 2)
-        source = slice((p % 2) * TOK, (p % 2) * TOK + TOK)
-        for at, side in ((0, halo), (4, own)):
-            rows = pl.ds(pl.multiple_of((block + at) * TOK, TOK), TOK)
-            kvt[:, rows, :] = side[p // 2][:, source, :]
-    kvt[:, pl.ds(2 * QTOK, CHUNK), :] = jnp.zeros((4, CHUNK, 128), BF)
-    gap = lax.broadcasted_iota(jnp.int32, (CHUNK, 256), 0) - (
-        lax.broadcasted_iota(jnp.int32, (CHUNK, 256), 1) % PAGE
-    )
-    for i in range(2):
-        bias[i] = jnp.where(gap <= i * PAGE, 0.0, NEG)
     factor = (1.0 / math.sqrt(128)) * math.log2(math.e)
     tall = lax.broadcasted_iota(jnp.int32, (PAGE, 128), 0)
 
     def one_page(index, carry):
         rows = pl.ds(pl.multiple_of(index * PAGE, PAGE), PAGE)
         page = jnp.bitwise_xor(role, 2 * (index // 4) + pair) * 4 + index % 4
-        offset = meta[1 + page]
         live = meta[17 + page]
-        low = QPAGES + page - offset
-        full = offset // 2
+        reach = meta[1 + page]
         stack = [
             jnp.concatenate(
                 [
@@ -292,94 +276,201 @@
             for h in range(2)
         ]
 
-        def scan(chunk, tops, count, masked):
-            base = pl.multiple_of((low + 2 * chunk) * PAGE, PAGE)
-            result = []
-            for h in range(2):
-                scores = lax.dot_general(
-                    kvt[h, pl.ds(base, count * CHUNK), :],
-                    stack[h],
-                    (((1,), (1,)), ((), ())),
-                    preferred_element_type=F32,
-                )
-                if masked:
-                    scores = scores + bias[offset % 2]
-                for i in range(count):
-                    saved[h, chunk + i] = scores[CHUNK * i : CHUNK * i + CHUNK]
-                peak = jnp.max(scores.reshape(count * CHUNK // 8, 8, 256), axis=0)
-                result.append(jnp.maximum(tops[h], peak))
-            return tuple(result)
-
-        tops = (jnp.full((8, 256), NEG, F32),) * 2
-        tops = lax.fori_loop(
-            0, full // 2, lambda i, t: scan(2 * i, t, 2, False), tops
-        )
-        tops = lax.fori_loop(
-            full // 2 * 2, full, lambda i, t: scan(i, t, 1, False), tops
-        )
-        tops = scan(full, tops, 1, True)
-        tops = [jnp.max(top, axis=0, keepdims=True) for top in tops]
-
-        def fold(chunk, state, count):
-            result = []
-            for h in range(2):
-                total, acc = state[h]
-                parts, weights = [], []
-                for i in range(count):
-                    expo = jnp.exp2((saved[h, chunk + i] - tops[h]) * factor)
-                    total = total + jnp.sum(expo.reshape(CHUNK // 8, 8, 256), axis=0)
-                    weights.append(expo.astype(BF))
-                for i in range(2 * count):
-                    at = pl.multiple_of((low + 2 * chunk + i) * PAGE, PAGE)
-                    parts.append(kvt[2 + h, pl.ds(at, PAGE), :])
-                acc = acc + jnp.dot(
-                    jnp.concatenate(parts, axis=1),
-                    jnp.concatenate(weights, axis=0),
-                    preferred_element_type=F32,
-                )
-                result.append((total, acc))
-            return tuple(result)
-
-        state = ((jnp.zeros((8, 256), F32), jnp.zeros((128, 256), F32)),) * 2
-        count = full + 1
-        state = lax.fori_loop(0, count // 2, lambda i, s: fold(2 * i, s, 2), state)
-        state = lax.fori_loop(
-            count // 2 * 2, count, lambda i, s: fold(i, s, 1), state
-        )
-        for h in range(2):
-            total, acc = state[h]
-            value = acc / jnp.sum(total, axis=0, keepdims=True)
-            value = jnp.transpose(value)
+        def run(first, opened, closed, covered, shade, count):
+            def scan(chunk, tops, width, masked):
+                base = pl.multiple_of((first + 2 * chunk) * PAGE, PAGE)
+                result = []
+                for h in range(2):
+                    scores = lax.dot_general(
+                        kvt[h, pl.ds(base, width * CHUNK), :],
+                        stack[h],
+                        (((1,), (1,)), ((), ())),
+                        preferred_element_type=F32,
+                    )
+                    if masked:
+                        scores = scores + bias[shade]
+                    for i in range(width):
+                        saved[h, chunk + i] = scores[CHUNK * i : CHUNK * i + CHUNK]
+                    peak = jnp.max(scores.reshape(width * CHUNK // 8, 8, 256), axis=0)
+                    result.append(jnp.maximum(tops[h], peak))
+                return tuple(result)
+
+            tops = (jnp.full((8, 256), NEG, F32),) * 2
+            twice = (closed - opened) // 2
+            tops = lax.fori_loop(
+                0, twice, lambda i, t: scan(opened + 2 * i, t, 2, False), tops
+            )
+            tops = lax.fori_loop(
+                opened + 2 * twice, closed, lambda i, t: scan(i, t, 1, False), tops
+            )
+            tops = scan(covered, tops, 1, True)
+            tops = [jnp.max(top, axis=0, keepdims=True) for top in tops]
+
+            def fold(chunk, state, width):
+                result = []
+                for h in range(2):
+                    total, acc = state[h]
+                    pieces, weights = [], []
+                    for i in range(width):
+                        expo = jnp.exp2((saved[h, chunk + i] - tops[h]) * factor)
+                        total = total + jnp.sum(
+                            expo.reshape(CHUNK // 8, 8, 256), axis=0
+                        )
+                        weights.append(expo.astype(BF))
+                    for i in range(2 * width):
+                        at = pl.multiple_of((first + 2 * chunk + i) * PAGE, PAGE)
+                        pieces.append(kvt[2 + h, pl.ds(at, PAGE), :])
+                    acc = acc + jnp.dot(
+                        jnp.concatenate(pieces, axis=1),
+                        jnp.concatenate(weights, axis=0),
+                        preferred_element_type=F32,
+                    )
+                    result.append((total, acc))
+                return tuple(result)
+
+            state = ((jnp.zeros((8, 256), F32), jnp.zeros((128, 256), F32)),) * 2
+            state = lax.fori_loop(0, count // 2, lambda i, s: fold(2 * i, s, 2), state)
+            state = lax.fori_loop(
+                count // 2 * 2, count, lambda i, s: fold(i, s, 1), state
+            )
+            return [
+                (tops[h], jnp.sum(state[h][0], axis=0, keepdims=True), state[h][1])
+                for h in range(2)
+            ]
+
+        def finish(h, total, acc):
+            value = jnp.transpose(acc / total)
             for g in range(2):
                 part = value[128 * g : 128 * g + 128]
                 part = jnp.where(tall < live, part, 0.0)
                 at_lane = 256 * h + 128 * g
                 out_ref[rows, at_lane : at_lane + 128] = part.astype(BF)
+
+        if mode == "halo":
+            pages = jnp.maximum(reach - page, 0)
+            count = (pages + 1) // 2
+            peaks, totals, sums = parts
+
+            @pl.when(count > 0)
+            def _():
+                result = run(QPAGES - 2 * count, 1, count, 0, 2 + pages % 2, count)
+                for h in range(2):
+                    top, total, acc = result[h]
+                    before = peaks[index, h][:1]
+                    higher = jnp.maximum(top, before)
+                    fade = jnp.exp2((top - higher) * factor)
+                    keep = jnp.exp2((before - higher) * factor)
+                    total = total * fade + totals[index, h][:1] * keep
+                    acc = acc * fade + sums[index, h] * keep
+                    finish(h, total, acc)
+
+            @pl.when(count == 0)
+            def _():
+                for h in range(2):
+                    finish(h, totals[index, h][:1], sums[index, h])
+
+            return carry
+
+        offset = jnp.minimum(reach, page) if mode == "own" else reach
+        full = offset // 2
+        result = run(QPAGES + page - offset, 0, full, full, offset % 2, full + 1)
+        for h in range(2):
+            top, total, acc = result[h]
+            if mode == "own":
+                peaks, totals, sums = parts
+                peaks[index, h] = jnp.broadcast_to(top, (8, 256))
+                totals[index, h] = jnp.broadcast_to(total, (8, 256))
+                sums[index, h] = acc
+            else:
+                finish(h, total, acc)
         return carry
 
     lax.fori_loop(0, 8, one_page, 0)
 
 
-def attend(meta, queries, own, halo, pair):
+def fill_pages(role, sides, kvt):
+    for p in range(4):
+        block = jnp.bitwise_xor(role, 2 * (p % 2) + p // 2)
+        source = slice((p % 2) * TOK, (p % 2) * TOK + TOK)
+        for at, side in sides:
+            rows = pl.ds(pl.multiple_of((block + at) * TOK, TOK), TOK)
+            kvt[:, rows, :] = side[p // 2][:, source, :]
+
+
+def fill_bias(bias):
+    key = lax.broadcasted_iota(jnp.int32, (CHUNK, 256), 0)
+    gap = key - lax.broadcasted_iota(jnp.int32, (CHUNK, 256), 1) % PAGE
+    for i in range(2):
+        bias[i] = jnp.where(gap <= i * PAGE, 0.0, NEG)
+    bias[2] = jnp.zeros((CHUNK, 256), F32)
+    bias[3] = jnp.where(key < PAGE, NEG, 0.0)
+
+
+def whole_kernel(pair, meta, q_ref, own0, own1, halo0, halo1, out_ref, kvt, saved, bias):
+    fill_pages(meta[0], ((0, (halo0, halo1)), (4, (own0, own1))), kvt)
+    kvt[:, pl.ds(2 * QTOK, CHUNK), :] = jnp.zeros((4, CHUNK, 128), BF)
+    fill_bias(bias)
+    attend_pages(pair, "all", meta, q_ref, out_ref, kvt, saved, bias, None)
+
+
+def own_kernel(pair, meta, q_ref, own0, own1, peaks, totals, sums, kvt, saved, bias):
+    fill_pages(meta[0], ((4, (own0, own1)),), kvt)
+    kvt[:, pl.ds(2 * QTOK, CHUNK), :] = jnp.zeros((4, CHUNK, 128), BF)
+    fill_bias(bias)
+    parts = (peaks, totals, sums)
+    attend_pages(pair, "own", meta, q_ref, None, kvt, saved, bias, parts)
+
+
+def halo_kernel(pair, meta, q_ref, halo0, halo1, peaks, totals, sums, out_ref, *scratch):
+    kvt, saved, bias = scratch
+    fill_pages(meta[0], ((0, (halo0, halo1)),), kvt)
+    fill_bias(bias)
+    parts = (peaks, totals, sums)
+    attend_pages(pair, "halo", meta, q_ref, out_ref, kvt, saved, bias, parts)
+
+
+def attend_call(kernel, pair, meta, operands, shapes):
     return pl.pallas_call(
-        functools.partial(attend_kernel, pair),
+        functools.partial(kernel, pair),
         grid_spec=pltpu.PrefetchScalarGridSpec(
             num_scalar_prefetch=1,
             grid=(),
-            in_specs=[INSIDE] * 5,
-            out_specs=INSIDE,
+            in_specs=[INSIDE] * len(operands),
+            out_specs=[INSIDE] * len(shapes),
             scratch_shapes=[
                 pltpu.VMEM((4, 2 * QTOK + CHUNK, 128), BF),
                 pltpu.VMEM((2, 9, CHUNK, 256), F32),
-                pltpu.VMEM((2, CHUNK, 256), F32),
+                pltpu.VMEM((4, CHUNK, 256), F32),
             ],
         ),
-        out_shape=jax.ShapeDtypeStruct((2 * TOK, 512), BF),
+        out_shape=shapes,
         compiler_params=pltpu.CompilerParams(vmem_limit_bytes=40 << 20),
         cost_estimate=pl.CostEstimate(
-            flops=4 << 30, transcendentals=4 << 20, bytes_accessed=6 << 20
-        ),
-    )(meta, queries, *own, *halo)
+            flops=2 << 30, transcendentals=2 << 20, bytes_accessed=6 << 20
+        ),
+    )(meta, *operands)
+
+
+ROWS = [jax.ShapeDtypeStruct((2 * TOK, 512), BF)]
+STATE = [
+    jax.ShapeDtypeStruct((8, 2, 8, 256), F32),
+    jax.ShapeDtypeStruct((8, 2, 8, 256), F32),
+    jax.ShapeDtypeStruct((8, 2, 128, 256), F32),
+]
+
+
+def attend(meta, queries, own, halo, pair):
+    operands = (queries, *own, *halo)
+    return attend_call(whole_kernel, pair, meta, operands, ROWS)[0]
+
+
+def attend_own(meta, queries, own, pair):
+    return attend_call(own_kernel, pair, meta, (queries, *own), STATE)
+
+
+def attend_halo(meta, queries, halo, parts, pair):
+    operands = (queries, *halo, *parts)
+    return attend_call(halo_kernel, pair, meta, operands, ROWS)[0]
 
 
 def pack_kernel(meta, *refs):
@@ -592,7 +683,8 @@
     for flip in (1, 2, 3):
         pages.append(to_role(packed[flip], flip))
 
-    far = attend(meta, queries[1], keys, halo, 1)
+    parts = attend_own(meta, queries[1], keys, 1)
+    far = attend_halo(meta, queries[1], halo, parts, 1)
     far = swap(far, "zh")
     near = attend(meta, queries[0], keys, halo, 0)
     o_parts = list(o_parts)

time: 277 us -> 301 us (1.087)
  starting transfers between devices: 82.1 us -> 89.1 us
  local copies, waits for them, and re-layouts: 4.67 us -> 11.6 us
  waiting for transfers between devices: 104 us -> 110 us
  other arithmetic: 9.55 us -> 13.6 us
    ppermute x18, starting transfers between devices: 48.4 us -> 64.5 us  [shift(): lax.ppermute(block, axis, [(i, (i + distance) % 4) for i in range(4)])]
    ppermute x11, waiting for transfers between devices: 34.1 us -> 46.7 us  [swap(): return lax.ppermute(block, axis, [(0, 1), (1, 0)])]
    unnamed x34 -> x62, local copies, waits for them, and re-layouts: 3.23 us -> 10.2 us
    ppermute x18, waiting for transfers between devices: 34.5 us -> 27.8 us  [shift(): lax.ppermute(block, axis, [(i, (i + distance) % 4) for i in range(4)])]
    ppermute x2, starting transfers between devices: 10.5 us -> 4.02 us  [previous_quad(): return lax.ppermute(block, names, route)]
    pallas_call x2 -> x3, Pallas kernels: 29.6 us -> 31.3 us  [attend_call(): pl.pallas_call(functools.partial(kernel, pair), grid_spec=pltpu.PrefetchS...]
  transfers between devices with their start and end apart: 35 -> 35, of which waited for: 12 -> 10; matrix products, arithmetic and copies ran while one was open for 4% -> 5% of each run, Pallas kernels for 25% -> 23%
where the time goes in v3:
time: 301 us
  waiting for transfers between devices  110 us (37%)
  starting transfers between devices  89.1 us (30%)
  Pallas kernels  74.9 us (25%)
  other arithmetic  13.6 us (5%)
  local copies, waits for them, and re-layouts  11.6 us (4%)
    ppermute x18, starting transfers between devices, shift(): lax.ppermute(block, axis, [(i, (i + distance) % 4) for i in range(4)])  64.5 us
    ppermute x11, waiting for transfers between devices, swap(): return lax.ppermute(block, axis, [(0, 1), (1, 0)])  46.7 us
    ppermute x3, waiting for transfers between devices, to_role(): return lax.ppermute(block, QUAD, [(i, i ^ flip) for i in range(4)])  31.9 us
    pallas_call x3, Pallas kernels, attend_call(): pl.pallas_call(functools.partial(kernel, pair), grid_spec=pltpu.PrefetchS...  31.3 us
    ppermute x18, waiting for transfers between devices, shift(): lax.ppermute(block, axis, [(i, (i + distance) % 4) for i in range(4)])  27.8 us
    pallas_call x4, Pallas kernels, project(): pl.pallas_call(functools.partial(project_kernel, store), grid_spec=pltpu....  24 us
    ppermute x11, starting transfers between devices, swap(): return lax.ppermute(block, axis, [(0, 1), (1, 0)])  11.1 us
    unnamed x62, local copies, waits for them, and re-layouts  10.2 us
  transfers between devices with their start and end apart: 35, of which 10 were waited for; matrix products, arithmetic and copies ran while one was open for 5% of the time, Pallas kernels for 23%

profile of v3, /device:TPU:57, one launch (start us, length us, event | category | flops | bytes accessed | tf_op | source)
XLA Modules:
  0.0 300.8 jit_solution(3250756098383495602)
XLA Ops:
  4.6 5.7 %all-to-all-start = ((bf16[8,16,2048]{2,1,0:T(8,128)(2,1)}), bf16[8,16,2048]{2,1,0:T(8,128)(2,1)S(1)}, u32[]{:S(2)}, u32[]{:S(2)}) async-start(bf16[8,16,2048]{2,1,0:T(8,128)(2,1)} %shard_map.112), calls=%async_computation | async-start | bytes 1048576 | tf_op jit(solution)/shard_map/all_to_all | solution.py:643
  14.3 4.0 %all-to-all-done = bf16[8,16,2048]{2,1,0:T(8,128)(2,1)S(1)} async-done(((bf16[8,16,2048]{2,1,0:T(8,128)(2,1)}), bf16[8,16,2048]{2,1,0:T(8,128)(2,1)S(1)}, u32[]{:S(2)}, u32[]{:S(2)}) %all-to-all-start) | async-done | bytes 524320 | tf_op jit(solution)/shard_map/all_to_all | solution.py:643
  20.8 46.7 %collective-permute-done.1.refs_0_ = bf16[512,2048]{1,0:T(8,128)(2,1)} collective-permute-done((bf16[512,2048]{1,0:T(8,128)(2,1)}, bf16[512,2048]{1,0:T(8,128)(2,1)}, u32[]{:S(2)}, u32[]{:S(2)}) %collective-permute-start.1) | collective-permute-done | bytes 2097184 | tf_op jit(solution)/shard_map/ppermute | solution.py:30
  68.1 5.5 %fusion.3 = (f32[2048,64]{1,0:T(8,128)}, f32[2048,64]{1,0:T(8,128)}, f32[2048,64]{1,0:T(8,128)S(1)}) fusion(f32[64]{0:T(128)S(1)} %multiply_power_fusion, f32[2048]{0:T(1024)S(1)} %convert_bitcast_fusion), kind=kLoop, calls=%fused_computation.9 | loop fusion | flops 262144 | bytes 1581312 | tf_op jit(solution)/shard_map/neg | solution.py:152
  87.2 3.5 %collective-permute-done.11.refs_2_ = bf16[2,64,512]{2,1,0:T(8,128)(2,1)S(1)} collective-permute-done((bf16[2,64,512]{2,1,0:T(8,128)(2,1)S(1)}, bf16[2,64,512]{2,1,0:T(8,128)(2,1)S(1)}, u32[]{:S(2)}, u32[]{:S(2)}) %collective-permute-start.11) | collective-permute-done | bytes 131104 | tf_op jit(solution)/shard_map/ppermute | solution.py:34
  103.4 4.0 %collective-permute-start.15 = (bf16[4,2,64,512]{3,2,1,0:T(8,128)(2,1)S(1)}, bf16[4,2,64,512]{3,2,1,0:T(8,128)(2,1)}, u32[]{:S(2)}, u32[]{:S(2)}) collective-permute-start(bf16[4,2,64,512]{3,2,1,0:T(8,128)(2,1)S(1)} %shard_map.116.refs_2_), channel_id=1, source_target_pairs={{0,12},{4,0},{8,4},{12,8},{1,13},{5,1},{9,5},{13,9},{2,14},{6,2},{... | collective-permute-start | bytes 1572872 | tf_op jit(solution)/shard_map/ppermute | solution.py:34
  116.3 3.3 %collective-permute-start.6 = (bf16[2,4,64,512]{3,2,1,0:T(8,128)(2,1)S(1)}, bf16[2,4,64,512]{3,2,1,0:T(8,128)(2,1)S(1)}, u32[]{:S(2)}, u32[]{:S(2)}) collective-permute-start(bf16[2,4,64,512]{3,2,1,0:T(8,128)(2,1)S(1)} %shard_map.114.refs_2_), channel_id=1, source_target_pairs={{0,32},{32,64},{64,96},{96,0},{1,33},{33,65},{65,97},{97,1},{2,34}... | collective-permute-start | bytes 1572872 | tf_op jit(solution)/shard_map/ppermute | solution.py:34
  121.0 6.3 %collective-permute-start.23 = (bf16[2,4,64,1024]{3,2,1,0:T(8,128)(2,1)S(1)}, bf16[2,4,64,1024]{3,2,1,0:T(8,128)(2,1)S(1)}, u32[]{:S(2)}, u32[]{:S(2)}) collective-permute-start(bf16[2,4,64,1024]{3,2,1,0:T(8,128)(2,1)S(1)} %shard_map.121.refs_2_), channel_id=1, source_target_pairs={{0,96},{32,0},{64,32},{96,64},{1,97},{33,1},{65,33},{97,65},{2,98}... | collective-permute-start | bytes 3145736 | tf_op jit(solution)/shard_map/ppermute | solution.py:34
  127.3 6.2 %shard_map.117 = (bf16[4,1024,128]{2,1,0:T(8,128)(2,1)S(1)}, bf16[2,1024,128]{2,1,0:T(8,128)(2,1)S(1)}) custom-call(s32[51]{0:T(128)S(1)} %copy-done.18, bf16[512,2048]{1,0:T(8,128)(2,1)} %fusion.2.refs_0_, bf16[512,2048]{1,0:T(8,128)(2,1)} %collective-permute-done.9.refs_1_, bf16[4,2,64,512]{3,2,1,0:T(8,128)(2,1)S(1)} %shard_map.116.refs_2_, ...), custom_call_target="tpu_custom_call" | custom-call | flops 2147483648 | bytes 8388608 | tf_op jit(solution)/shard_map/pallas_call | solution.py:239
  135.7 6.2 %shard_map.118 = (bf16[4,1024,128]{2,1,0:T(8,128)(2,1)S(1)}, bf16[2,1024,128]{2,1,0:T(8,128)(2,1)S(1)}) custom-call(s32[51]{0:T(128)S(1)} %copy-done.20, bf16[512,2048]{1,0:T(8,128)(2,1)} %collective-permute-done.1.refs_0_, bf16[512,2048]{1,0:T(8,128)(2,1)} %collective-permute-done.2.refs_1_, bf16[4,2,64,512]{3,2,1,0:T(8,128)(2,1)S(1)} %shard_map.116.refs_2_, ...), custom_call_target="tpu_custom_call" | custom-call | flops 2147483648 | bytes 8388608 | tf_op jit(solution)/shard_map/pallas_call | solution.py:239
  143.9 3.8 %collective-permute-start.7 = (bf16[2,4,64,512]{3,2,1,0:T(8,128)(2,1)S(1)}, bf16[2,4,64,512]{3,2,1,0:T(8,128)(2,1)S(1)}, u32[]{:S(2)}, u32[]{:S(2)}) collective-permute-start(bf16[2,4,64,512]{3,2,1,0:T(8,128)(2,1)S(1)} %shard_map.114.refs_2_), channel_id=1, source_target_pairs={{0,64},{32,96},{64,0},{96,32},{1,65},{33,97},{65,1},{97,33},{2,66}... | collective-permute-start | bytes 1572872 | tf_op jit(solution)/shard_map/ppermute | solution.py:34
  147.6 13.8 %collective-permute-done.7.refs_4_ = bf16[2,4,64,512]{3,2,1,0:T(8,128)(2,1)S(1)} collective-permute-done((bf16[2,4,64,512]{3,2,1,0:T(8,128)(2,1)S(1)}, bf16[2,4,64,512]{3,2,1,0:T(8,128)(2,1)S(1)}, u32[]{:S(2)}, u32[]{:S(2)}) %collective-permute-start.7) | collective-permute-done | bytes 524320 | tf_op jit(solution)/shard_map/ppermute | solution.py:34
  161.4 38.5 %collective-permute-start.25 = (bf16[2,4,64,1024]{3,2,1,0:T(8,128)(2,1)S(1)}, bf16[2,4,64,1024]{3,2,1,0:T(8,128)(2,1)S(1)}, u32[]{:S(2)}, u32[]{:S(2)}) collective-permute-start(bf16[2,4,64,1024]{3,2,1,0:T(8,128)(2,1)S(1)} %shard_map.121.refs_2_), channel_id=1, source_target_pairs={{0,32},{32,64},{64,96},{96,0},{1,33},{33,65},{65,97},{97,1},{2,34}... | collective-permute-start | bytes 3145736 | tf_op jit(solution)/shard_map/ppermute | solution.py:34
  200.7 5.8 %shard_map.115.q_ref = bf16[1024,512]{1,0:T(8,128)(2,1)S(1)} custom-call(s32[51]{0:T(128)S(1)} %copy-done.18, bf16[512,2048]{1,0:T(8,128)(2,1)} %collective-permute-done.1.refs_0_, bf16[512,2048]{1,0:T(8,128)(2,1)} %collective-permute-done.2.refs_1_, bf16[2,4,64,512]{3,2,1,0:T(8,128)(2,1)S(1)} %shard_map.114.refs_2_, ...), custom_call_target="tpu_custom_call" | custom-call | flops 2147483648 | bytes 8388608 | tf_op jit(solution)/shard_map/pallas_call | solution.py:239
  206.5 10.2 %shard_map.119 = (f32[8,2,8,256]{3,2,1,0:T(8,128)S(1)}, f32[8,2,8,256]{3,2,1,0:T(8,128)S(1)}, f32[8,2,128,256]{3,2,1,0:T(8,128)S(1)}) custom-call(s32[51]{0:T(128)S(1)} %copy-done.18, bf16[1024,512]{1,0:T(8,128)(2,1)S(1)} %shard_map.115.q_ref, bf16[4,1024,128]{2,1,0:T(8,128)(2,1)S(1)} %get-tuple-element.25.own0.refs_0_, ...), custom_call_target="tpu_custom_call" | custom-call | flops 2147483648 | bytes 6291456 | tf_op jit(solution)/shard_map/pallas_call | solution.py:433
  216.8 4.1 %shard_map.120 = bf16[1024,512]{1,0:T(8,128)(2,1)S(1)} custom-call(s32[51]{0:T(128)S(1)} %copy-done.18, bf16[1024,512]{1,0:T(8,128)(2,1)S(1)} %shard_map.115.q_ref, bf16[4,1024,128]{2,1,0:T(8,128)(2,1)S(1)} %collective-permute-done.16.halo0, bf16[4,1024,128]{2,1,0:T(8,128)(2,1)S(1)} %collective-permute-done.17.halo1, ...), custom_call_target="tpu_custom_call" | custom-call | flops 2147483648 | bytes 6291456 | tf_op jit(solution)/shard_map/pallas_call | solution.py:433
  220.9 6.1 %collective-permute-start.18 = (bf16[1024,512]{1,0:T(8,128)(2,1)S(1)}, bf16[1024,512]{1,0:T(8,128)(2,1)S(1)}, u32[]{:S(2)}, u32[]{:S(2)}) collective-permute-start(bf16[1024,512]{1,0:T(8,128)(2,1)S(1)} %shard_map.120), channel_id=1, source_target_pairs={{0,1},{1,0},{2,3},{3,2},{4,5},{5,4},{6,7},{7,6},{8,9},{9,8},{10,11... | collective-permute-start | bytes 3145736 | tf_op jit(solution)/shard_map/ppermute | solution.py:30
  229.9 31.9 %collective-permute-done.31.refs_1_ = bf16[512,512]{1,0:T(8,128)(2,1)S(1)} collective-permute-done((bf16[512,512]{1,0:T(8,128)(2,1)S(1)}, bf16[512,512]{1,0:T(8,128)(2,1)S(1)}, u32[]{:S(2)}, u32[]{:S(2)}) %collective-permute-start.31) | collective-permute-done | bytes 524320 | tf_op jit(solution)/shard_map/ppermute | solution.py:38
  262.5 3.2 %collective-permute-start.33 = (bf16[512,512]{1,0:T(8,128)(2,1)}, bf16[512,512]{1,0:T(8,128)(2,1)}, u32[]{:S(2)}, u32[]{:S(2)}) collective-permute-start(bf16[512,512]{1,0:T(8,128)(2,1)} %get-tuple-element.36), channel_id=1, source_target_pairs={{0,3},{1,2},{2,1},{3,0},{4,7},{5,6},{6,5},{7,4},{8,11},{9,10},{10,... | collective-permute-start | bytes 1572872 | tf_op jit(solution)/shard_map/ppermute | solution.py:38
  265.6 5.8 %shard_map.122.q_ref = bf16[1024,512]{1,0:T(8,128)(2,1)S(1)} custom-call(s32[51]{0:T(128)S(1)} %copy-done.18, bf16[512,2048]{1,0:T(8,128)(2,1)} %fusion.2.refs_0_, bf16[512,2048]{1,0:T(8,128)(2,1)} %collective-permute-done.9.refs_1_, bf16[2,4,64,512]{3,2,1,0:T(8,128)(2,1)S(1)} %shard_map.114.refs_2_, ...), custom_call_target="tpu_custom_call" | custom-call | flops 2147483648 | bytes 8388608 | tf_op jit(solution)/shard_map/pallas_call | solution.py:239
  271.5 17.0 %shard_map.123.refs_0_ = bf16[1024,512]{1,0:T(8,128)(2,1)S(1)} custom-call(s32[51]{0:T(128)S(1)} %copy-done.18, bf16[1024,512]{1,0:T(8,128)(2,1)S(1)} %shard_map.122.q_ref, bf16[4,1024,128]{2,1,0:T(8,128)(2,1)S(1)} %copy-done.1, bf16[4,1024,128]{2,1,0:T(8,128)(2,1)S(1)} %copy-done.3, bf16[4,1024,128]{2,1,0:T(8,128)(2,1)S(1)} %copy-done.22, ...), custom_call_target="tpu_custom_call" | custom-call | flops 2147483648 | bytes 6291456 | tf_op jit(solution)/shard_map/pallas_call | solution.py:433
  289.3 3.6 %unpack_pages.1 = (bf16[512,1024]{1,0:T(8,128)(2,1)}, bf16[512,1024]{1,0:T(8,128)(2,1)}) custom-call(s32[51]{0:T(128)S(1)} %copy-done.18, bf16[512,512]{1,0:T(8,128)(2,1)S(1)} %get-tuple-element.33.refs_0_, bf16[512,512]{1,0:T(8,128)(2,1)S(1)} %collective-permute-done.31.refs_1_, bf16[512,512]{1,0:T(8,128)(2,1)} %collective-permute-done.32.refs_2_, ...), custom_call_target="tpu_custom_call" | custom-call | tf_op jit(solution)/shard_map/unpack_pages/pallas_call | solution.py:528
  292.9 3.3 %output_near.1.refs_10_ = f32[2,512,1024]{2,1,0:T(8,128)S(1)} custom-call(s32[51]{0:T(128)S(1)} %copy-done.18, bf16[1024,512]{1,0:T(8,128)(2,1)S(1)} %shard_map.123.refs_0_, bf16[512,512]{1,0:T(8,128)(2,1)S(1)} %collective-permute-done.30.refs_1_, bf16[2,4,64,1024]{3,2,1,0:T(8,128)(2,1)S(1)} %shard_map.121.refs_2_, ...), custom_call_target="tpu_custom_call" | custom-call | tf_op jit(solution)/shard_map/output_near/pallas_call | solution.py:584
  296.2 4.6 %output_far.1 = bf16[512,2048]{1,0:T(8,128)(2,1)} custom-call(s32[51]{0:T(128)S(1)} %copy-done.18, bf16[1024,512]{1,0:T(8,128)(2,1)S(1)} %collective-permute-done.18.refs_0_, bf16[512,512]{1,0:T(8,128)(2,1)S(1)} %collective-permute-done.19.refs_1_, bf16[2,4,64,1024]{3,2,1,0:T(8,128)(2,1)S(1)} %shard_map.121.refs_2_, ...), custom_call_target="tpu_custom_call" | custom-call | tf_op jit(solution)/shard_map/output_far/pallas_call | solution.py:600
  (149 shorter events, 56.6 us)
Async XLA Ops:
  4.6 13.7 %all-to-all-start = ((bf16[8,16,2048]{2,1,0:T(8,128)(2,1)}), bf16[8,16,2048]{2,1,0:T(8,128)(2,1)S(1)}, u32[]{:S(2)}, u32[]{:S(2)}) async-start(bf16[8,16,2048]{2,1,0:T(8,128)(2,1)} %shard_map.112), calls=%async_computation | async-start | bytes 1048576 | tf_op jit(solution)/shard_map/all_to_all | solution.py:643
  18.2 49.3 %collective-permute-start.1 = (bf16[512,2048]{1,0:T(8,128)(2,1)}, bf16[512,2048]{1,0:T(8,128)(2,1)}, u32[]{:S(2)}, u32[]{:S(2)}) collective-permute-start(bf16[512,2048]{1,0:T(8,128)(2,1)} %fusion.2.refs_0_), channel_id=1, source_target_pairs={{0,1},{1,0},{2,3},{3,2},{4,5},{5,4},{6,7},{7,6},{8,9},{9,8},{10,11... | collective-permute-start | bytes 6291464 | tf_op jit(solution)/shard_map/ppermute | solution.py:30
  19.1 108.2 %collective-permute-start.9 = (bf16[512,2048]{1,0:T(8,128)(2,1)}, bf16[512,2048]{1,0:T(8,128)(2,1)}, u32[]{:S(2)}, u32[]{:S(2)}) collective-permute-start(bf16[512,2048]{1,0:T(8,128)(2,1)} %fusion.2.refs_0_), channel_id=1, source_target_pairs={{0,2},{2,0},{1,3},{3,1},{4,6},{6,4},{5,7},{7,5},{8,10},{10,8},{9,1... | collective-permute-start | bytes 6291464 | tf_op jit(solution)/shard_map/ppermute | solution.py:30
  20.4 57.5 %collective-permute-start = (s32[8]{0:T(128)S(1)}, s32[8]{0:T(128)S(1)}, u32[]{:S(2)}, u32[]{:S(2)}) collective-permute-start(s32[8]{0:T(128)S(1)} %copy-done.27), channel_id=1, source_target_pairs={{0,2},{2,0},{1,3},{3,1},{4,6},{6,4},{5,7},{7,5},{8,10},{10,8},{9,1... | collective-permute-start | bytes 104 | tf_op jit(solution)/shard_map/ppermute | solution.py:30
  67.5 68.2 %collective-permute-start.2 = (bf16[512,2048]{1,0:T(8,128)(2,1)}, bf16[512,2048]{1,0:T(8,128)(2,1)}, u32[]{:S(2)}, u32[]{:S(2)}) collective-permute-start(bf16[512,2048]{1,0:T(8,128)(2,1)} %collective-permute-done.1.refs_0_), channel_id=1, source_target_pairs={{0,2},{2,0},{1,3},{3,1},{4,6},{6,4},{5,7},{7,5},{8,10},{10,8},{9,1... | collective-permute-start | bytes 6291464 | tf_op jit(solution)/shard_map/ppermute | solution.py:30
  98.7 17.6 %collective-permute-start.13 = (bf16[4,2,64,512]{3,2,1,0:T(8,128)(2,1)S(1)}, bf16[4,2,64,512]{3,2,1,0:T(8,128)(2,1)S(1)}, u32[]{:S(2)}, u32[]{:S(2)}) collective-permute-start(bf16[4,2,64,512]{3,2,1,0:T(8,128)(2,1)S(1)} %shard_map.116.refs_2_), channel_id=1, source_target_pairs={{0,4},{4,8},{8,12},{12,0},{1,5},{5,9},{9,13},{13,1},{2,6},{6,10},{... | collective-permute-start | bytes 1572872 | tf_op jit(solution)/shard_map/ppermute | solution.py:34
  100.2 20.9 %collective-permute-start.14 = (bf16[4,2,64,512]{3,2,1,0:T(8,128)(2,1)S(1)}, bf16[4,2,64,512]{3,2,1,0:T(8,128)(2,1)}, u32[]{:S(2)}, u32[]{:S(2)}) collective-permute-start(bf16[4,2,64,512]{3,2,1,0:T(8,128)(2,1)S(1)} %shard_map.116.refs_2_), channel_id=1, source_target_pairs={{0,8},{4,12},{8,0},{12,4},{1,9},{5,13},{9,1},{13,5},{2,10},{6,14},... | collective-permute-start | bytes 1572872 | tf_op jit(solution)/shard_map/ppermute | solution.py:34
  103.4 23.9 %collective-permute-start.15 = (bf16[4,2,64,512]{3,2,1,0:T(8,128)(2,1)S(1)}, bf16[4,2,64,512]{3,2,1,0:T(8,128)(2,1)}, u32[]{:S(2)}, u32[]{:S(2)}) collective-permute-start(bf16[4,2,64,512]{3,2,1,0:T(8,128)(2,1)S(1)} %shard_map.116.refs_2_), channel_id=1, source_target_pairs={{0,12},{4,0},{8,4},{12,8},{1,13},{5,1},{9,5},{13,9},{2,14},{6,2},{... | collective-permute-start | bytes 1572872 | tf_op jit(solution)/shard_map/ppermute | solution.py:34
  116.3 31.3 %collective-permute-start.6 = (bf16[2,4,64,512]{3,2,1,0:T(8,128)(2,1)S(1)}, bf16[2,4,64,512]{3,2,1,0:T(8,128)(2,1)S(1)}, u32[]{:S(2)}, u32[]{:S(2)}) collective-permute-start(bf16[2,4,64,512]{3,2,1,0:T(8,128)(2,1)S(1)} %shard_map.114.refs_2_), channel_id=1, source_target_pairs={{0,32},{32,64},{64,96},{96,0},{1,33},{33,65},{65,97},{97,1},{2,34}... | collective-permute-start | bytes 1572872 | tf_op jit(solution)/shard_map/ppermute | solution.py:34
  121.0 79.7 %collective-permute-start.23 = (bf16[2,4,64,1024]{3,2,1,0:T(8,128)(2,1)S(1)}, bf16[2,4,64,1024]{3,2,1,0:T(8,128)(2,1)S(1)}, u32[]{:S(2)}, u32[]{:S(2)}) collective-permute-start(bf16[2,4,64,1024]{3,2,1,0:T(8,128)(2,1)S(1)} %shard_map.121.refs_2_), channel_id=1, source_target_pairs={{0,96},{32,0},{64,32},{96,64},{1,97},{33,1},{65,33},{97,65},{2,98}... | collective-permute-start | bytes 3145736 | tf_op jit(solution)/shard_map/ppermute | solution.py:34
  133.6 83.2 %collective-permute-start.16 = (bf16[4,1024,128]{2,1,0:T(8,128)(2,1)S(1)}, bf16[4,1024,128]{2,1,0:T(8,128)(2,1)S(1)}, u32[]{:S(2)}, u32[]{:S(2)}) collective-permute-start(bf16[4,1024,128]{2,1,0:T(8,128)(2,1)S(1)} %get-tuple-element.25.own0.refs_0_), channel_id=1, source_target_pairs={{0,4},{1,5},{2,6},{3,7},{4,8},{5,9},{6,10},{7,11},{8,12},{9,13},{1... | collective-permute-start | bytes 3145736 | tf_op jit(solution)/shard_map/ppermute | solution.py:631
  141.9 74.9 %collective-permute-start.17 = (bf16[4,1024,128]{2,1,0:T(8,128)(2,1)S(1)}, bf16[4,1024,128]{2,1,0:T(8,128)(2,1)S(1)}, u32[]{:S(2)}, u32[]{:S(2)}) collective-permute-start(bf16[4,1024,128]{2,1,0:T(8,128)(2,1)S(1)} %get-tuple-element.26.own1.refs_1_), channel_id=1, source_target_pairs={{0,4},{1,5},{2,6},{3,7},{4,8},{5,9},{6,10},{7,11},{8,12},{9,13},{1... | collective-permute-start | bytes 3145736 | tf_op jit(solution)/shard_map/ppermute | solution.py:631
  143.9 17.6 %collective-permute-start.7 = (bf16[2,4,64,512]{3,2,1,0:T(8,128)(2,1)S(1)}, bf16[2,4,64,512]{3,2,1,0:T(8,128)(2,1)S(1)}, u32[]{:S(2)}, u32[]{:S(2)}) collective-permute-start(bf16[2,4,64,512]{3,2,1,0:T(8,128)(2,1)S(1)} %shard_map.114.refs_2_), channel_id=1, source_target_pairs={{0,64},{32,96},{64,0},{96,32},{1,65},{33,97},{65,1},{97,33},{2,66}... | collective-permute-start | bytes 1572872 | tf_op jit(solution)/shard_map/ppermute | solution.py:34
  147.6 52.3 %collective-permute-start.8 = (bf16[2,4,64,512]{3,2,1,0:T(8,128)(2,1)S(1)}, bf16[2,4,64,512]{3,2,1,0:T(8,128)(2,1)S(1)}, u32[]{:S(2)}, u32[]{:S(2)}) collective-permute-start(bf16[2,4,64,512]{3,2,1,0:T(8,128)(2,1)S(1)} %shard_map.114.refs_2_), channel_id=1, source_target_pairs={{0,96},{32,0},{64,32},{96,64},{1,97},{33,1},{65,33},{97,65},{2,98}... | collective-permute-start | bytes 1572872 | tf_op jit(solution)/shard_map/ppermute | solution.py:34
  161.4 67.7 %collective-permute-start.25 = (bf16[2,4,64,1024]{3,2,1,0:T(8,128)(2,1)S(1)}, bf16[2,4,64,1024]{3,2,1,0:T(8,128)(2,1)S(1)}, u32[]{:S(2)}, u32[]{:S(2)}) collective-permute-start(bf16[2,4,64,1024]{3,2,1,0:T(8,128)(2,1)S(1)} %shard_map.121.refs_2_), channel_id=1, source_target_pairs={{0,32},{32,64},{64,96},{96,0},{1,33},{33,65},{65,97},{97,1},{2,34}... | collective-permute-start | bytes 3145736 | tf_op jit(solution)/shard_map/ppermute | solution.py:34
  200.0 29.5 %collective-permute-start.26 = (bf16[2,4,64,1024]{3,2,1,0:T(8,128)(2,1)S(1)}, bf16[2,4,64,1024]{3,2,1,0:T(8,128)(2,1)S(1)}, u32[]{:S(2)}, u32[]{:S(2)}) collective-permute-start(bf16[2,4,64,1024]{3,2,1,0:T(8,128)(2,1)S(1)} %shard_map.121.refs_2_), channel_id=1, source_target_pairs={{0,2},{2,0},{1,3},{3,1},{4,6},{6,4},{5,7},{7,5},{8,10},{10,8},{9,1... | collective-permute-start | bytes 3145736 | tf_op jit(solution)/shard_map/ppermute | solution.py:30
  200.7 29.0 %collective-permute-start.24 = (bf16[2,4,64,1024]{3,2,1,0:T(8,128)(2,1)S(1)}, bf16[2,4,64,1024]{3,2,1,0:T(8,128)(2,1)S(1)}, u32[]{:S(2)}, u32[]{:S(2)}) collective-permute-start(bf16[2,4,64,1024]{3,2,1,0:T(8,128)(2,1)S(1)} %collective-permute-done.23.refs_3_), channel_id=1, source_target_pairs={{0,96},{32,0},{64,32},{96,64},{1,97},{33,1},{65,33},{97,65},{2,98}... | collective-permute-start | bytes 3145736 | tf_op jit(solution)/shard_map/ppermute | solution.py:34
  220.9 41.5 %collective-permute-start.18 = (bf16[1024,512]{1,0:T(8,128)(2,1)S(1)}, bf16[1024,512]{1,0:T(8,128)(2,1)S(1)}, u32[]{:S(2)}, u32[]{:S(2)}) collective-permute-start(bf16[1024,512]{1,0:T(8,128)(2,1)S(1)} %shard_map.120), channel_id=1, source_target_pairs={{0,1},{1,0},{2,3},{3,2},{4,5},{5,4},{6,7},{7,6},{8,9},{9,8},{10,11... | collective-permute-start | bytes 3145736 | tf_op jit(solution)/shard_map/ppermute | solution.py:30
  229.1 32.8 %collective-permute-start.31 = (bf16[512,512]{1,0:T(8,128)(2,1)S(1)}, bf16[512,512]{1,0:T(8,128)(2,1)S(1)}, u32[]{:S(2)}, u32[]{:S(2)}) collective-permute-start(bf16[512,512]{1,0:T(8,128)(2,1)S(1)} %get-tuple-element.34), channel_id=1, source_target_pairs={{0,1},{1,0},{2,3},{3,2},{4,5},{5,4},{6,7},{7,6},{8,9},{9,8},{10,11... | collective-permute-start | bytes 1572872 | tf_op jit(solution)/shard_map/ppermute | solution.py:38
  229.2 63.7 %collective-permute-start.27 = (bf16[2,4,64,1024]{3,2,1,0:T(8,128)(2,1)S(1)}, bf16[2,4,64,1024]{3,2,1,0:T(8,128)(2,1)S(1)}, u32[]{:S(2)}, u32[]{:S(2)}) collective-permute-start(bf16[2,4,64,1024]{3,2,1,0:T(8,128)(2,1)S(1)} %collective-permute-done.23.refs_3_), channel_id=1, source_target_pairs={{0,2},{2,0},{1,3},{3,1},{4,6},{6,4},{5,7},{7,5},{8,10},{10,8},{9,1... | collective-permute-start | bytes 3145736 | tf_op jit(solution)/shard_map/ppermute | solution.py:30
  229.4 63.4 %collective-permute-start.29 = (bf16[2,4,64,1024]{3,2,1,0:T(8,128)(2,1)S(1)}, bf16[2,4,64,1024]{3,2,1,0:T(8,128)(2,1)S(1)}, u32[]{:S(2)}, u32[]{:S(2)}) collective-permute-start(bf16[2,4,64,1024]{3,2,1,0:T(8,128)(2,1)S(1)} %collective-permute-done.25.refs_5_), channel_id=1, source_target_pairs={{0,2},{2,0},{1,3},{3,1},{4,6},{6,4},{5,7},{7,5},{8,10},{10,8},{9,1... | collective-permute-start | bytes 3145736 | tf_op jit(solution)/shard_map/ppermute | solution.py:30
  229.7 63.2 %collective-permute-start.28 = (bf16[2,4,64,1024]{3,2,1,0:T(8,128)(2,1)S(1)}, bf16[2,4,64,1024]{3,2,1,0:T(8,128)(2,1)S(1)}, u32[]{:S(2)}, u32[]{:S(2)}) collective-permute-start(bf16[2,4,64,1024]{3,2,1,0:T(8,128)(2,1)S(1)} %collective-permute-done.24.refs_4_), channel_id=1, source_target_pairs={{0,2},{2,0},{1,3},{3,1},{4,6},{6,4},{5,7},{7,5},{8,10},{10,8},{9,1... | collective-permute-start | bytes 3145736 | tf_op jit(solution)/shard_map/ppermute | solution.py:30
  261.9 26.7 %collective-permute-start.32 = (bf16[512,512]{1,0:T(8,128)(2,1)}, bf16[512,512]{1,0:T(8,128)(2,1)}, u32[]{:S(2)}, u32[]{:S(2)}) collective-permute-start(bf16[512,512]{1,0:T(8,128)(2,1)} %get-tuple-element.35), channel_id=1, source_target_pairs={{0,2},{1,3},{2,0},{3,1},{4,6},{5,7},{6,4},{7,5},{8,10},{9,11},{10,... | collective-permute-start | bytes 1572872 | tf_op jit(solution)/shard_map/ppermute | solution.py:38
  262.5 26.7 %collective-permute-start.33 = (bf16[512,512]{1,0:T(8,128)(2,1)}, bf16[512,512]{1,0:T(8,128)(2,1)}, u32[]{:S(2)}, u32[]{:S(2)}) collective-permute-start(bf16[512,512]{1,0:T(8,128)(2,1)} %get-tuple-element.36), channel_id=1, source_target_pairs={{0,3},{1,2},{2,1},{3,0},{4,7},{5,6},{6,5},{7,4},{8,11},{9,10},{10,... | collective-permute-start | bytes 1572872 | tf_op jit(solution)/shard_map/ppermute | solution.py:38
  (42 other events, 414.0 us)

commit v4 on v3

--- a/solution.py
+++ b/solution.py
@@ -241,7 +241,7 @@
         grid_spec=pltpu.PrefetchScalarGridSpec(
             num_scalar_prefetch=1,
             grid=(2,),
-            in_specs=[pl.BlockSpec((tile, DEPTH), lambda i, m: (0, 0))] * 2
+            in_specs=[INSIDE] * 2
             + [INSIDE] * 4
             + [pl.BlockSpec((tile, 128), table)] * 2,
             out_specs=out_specs,
@@ -639,7 +639,20 @@
 
     here = jnp.stack([role, y, x]).astype(jnp.int32)
 
-    slices = small(slices_kernel, here, (w_qk, w_v, w_o), [(8, 16, 2048)])[0]
+    slices = pl.pallas_call(
+        slices_kernel,
+        grid_spec=pltpu.PrefetchScalarGridSpec(
+            num_scalar_prefetch=1,
+            grid=(1,),
+            in_specs=[
+                pl.BlockSpec(block.shape, lambda i, m: (0, 0))
+                for block in (w_qk, w_v, w_o)
+            ],
+            out_specs=INSIDE,
+        ),
+        out_shape=jax.ShapeDtypeStruct((8, 16, 2048), BF),
+        name="role_slices",
+    )(here, w_qk, w_v, w_o)
     level = lax.all_to_all(
         slices, ("zl", "c", "zh"), split_axis=0, concat_axis=0, tiled=True
     ).reshape(2, 64, 2048)

time: 301 us -> 300 us (level)
    unnamed x62 -> x58, local copies, waits for them, and re-layouts: 10.2 us -> 7.68 us
where the time goes in v4:
time: 300 us
  waiting for transfers between devices  111 us (37%)
  starting transfers between devices  89.1 us (30%)
  Pallas kernels  76 us (25%)
  other arithmetic  14 us (5%)
  local copies, waits for them, and re-layouts  9.04 us (3%)
    ppermute x18, starting transfers between devices, shift(): lax.ppermute(block, axis, [(i, (i + distance) % 4) for i in range(4)])  64.4 us
    ppermute x11, waiting for transfers between devices, swap(): return lax.ppermute(block, axis, [(0, 1), (1, 0)])  46.7 us
    ppermute x3, waiting for transfers between devices, to_role(): return lax.ppermute(block, QUAD, [(i, i ^ flip) for i in range(4)])  32 us
    pallas_call x3, Pallas kernels, attend_call(): pl.pallas_call(functools.partial(kernel, pair), grid_spec=pltpu.PrefetchS...  31.2 us
    ppermute x18, waiting for transfers between devices, shift(): lax.ppermute(block, axis, [(i, (i + distance) % 4) for i in range(4)])  28 us
    pallas_call x4, Pallas kernels, project(): pl.pallas_call(functools.partial(project_kernel, store), grid_spec=pltpu....  24 us
    ppermute x11, starting transfers between devices, swap(): return lax.ppermute(block, axis, [(0, 1), (1, 0)])  11.2 us
    unnamed x58, local copies, waits for them, and re-layouts  7.68 us
  transfers between devices with their start and end apart: 35, of which 10 were waited for; matrix products, arithmetic and copies ran while one was open for 5% of the time, Pallas kernels for 23%

profile of v4, /device:TPU:57, one launch (start us, length us, event | category | flops | bytes accessed | tf_op | source)
XLA Modules:
  0.0 299.9 jit_solution(17403935150099732028)
XLA Ops:
  3.8 5.7 %all-to-all-start = ((bf16[8,16,2048]{2,1,0:T(8,128)(2,1)}), bf16[8,16,2048]{2,1,0:T(8,128)(2,1)S(1)}, u32[]{:S(2)}, u32[]{:S(2)}) async-start(bf16[8,16,2048]{2,1,0:T(8,128)(2,1)} %role_slices.1), calls=%async_computation | async-start | bytes 1048576 | tf_op jit(solution)/shard_map/all_to_all | solution.py:656
  13.5 4.0 %all-to-all-done = bf16[8,16,2048]{2,1,0:T(8,128)(2,1)S(1)} async-done(((bf16[8,16,2048]{2,1,0:T(8,128)(2,1)}), bf16[8,16,2048]{2,1,0:T(8,128)(2,1)S(1)}, u32[]{:S(2)}, u32[]{:S(2)}) %all-to-all-start) | async-done | bytes 524320 | tf_op jit(solution)/shard_map/all_to_all | solution.py:656
  20.0 46.7 %collective-permute-done.1.refs_0_ = bf16[512,2048]{1,0:T(8,128)(2,1)} collective-permute-done((bf16[512,2048]{1,0:T(8,128)(2,1)}, bf16[512,2048]{1,0:T(8,128)(2,1)}, u32[]{:S(2)}, u32[]{:S(2)}) %collective-permute-start.1) | collective-permute-done | bytes 2097184 | tf_op jit(solution)/shard_map/ppermute | solution.py:30
  67.3 5.5 %fusion.3 = (f32[2048,64]{1,0:T(8,128)}, f32[2048,64]{1,0:T(8,128)}, f32[2048,64]{1,0:T(8,128)S(1)}) fusion(f32[64]{0:T(128)S(1)} %multiply_power_fusion, f32[2048]{0:T(1024)S(1)} %convert_bitcast_fusion), kind=kLoop, calls=%fused_computation.9 | loop fusion | flops 262144 | bytes 1581312 | tf_op jit(solution)/shard_map/neg | solution.py:152
  86.3 3.5 %collective-permute-done.11.refs_2_ = bf16[2,64,512]{2,1,0:T(8,128)(2,1)S(1)} collective-permute-done((bf16[2,64,512]{2,1,0:T(8,128)(2,1)S(1)}, bf16[2,64,512]{2,1,0:T(8,128)(2,1)S(1)}, u32[]{:S(2)}, u32[]{:S(2)}) %collective-permute-start.11) | collective-permute-done | bytes 131104 | tf_op jit(solution)/shard_map/ppermute | solution.py:34
  102.6 4.0 %collective-permute-start.15 = (bf16[4,2,64,512]{3,2,1,0:T(8,128)(2,1)S(1)}, bf16[4,2,64,512]{3,2,1,0:T(8,128)(2,1)}, u32[]{:S(2)}, u32[]{:S(2)}) collective-permute-start(bf16[4,2,64,512]{3,2,1,0:T(8,128)(2,1)S(1)} %shard_map.115.refs_2_), channel_id=1, source_target_pairs={{0,12},{4,0},{8,4},{12,8},{1,13},{5,1},{9,5},{13,9},{2,14},{6,2},{... | collective-permute-start | bytes 1572872 | tf_op jit(solution)/shard_map/ppermute | solution.py:34
  115.4 3.2 %collective-permute-start.6 = (bf16[2,4,64,512]{3,2,1,0:T(8,128)(2,1)S(1)}, bf16[2,4,64,512]{3,2,1,0:T(8,128)(2,1)S(1)}, u32[]{:S(2)}, u32[]{:S(2)}) collective-permute-start(bf16[2,4,64,512]{3,2,1,0:T(8,128)(2,1)S(1)} %shard_map.113.refs_2_), channel_id=1, source_target_pairs={{0,32},{32,64},{64,96},{96,0},{1,33},{33,65},{65,97},{97,1},{2,34}... | collective-permute-start | bytes 1572872 | tf_op jit(solution)/shard_map/ppermute | solution.py:34
  120.2 6.3 %collective-permute-start.23 = (bf16[2,4,64,1024]{3,2,1,0:T(8,128)(2,1)S(1)}, bf16[2,4,64,1024]{3,2,1,0:T(8,128)(2,1)S(1)}, u32[]{:S(2)}, u32[]{:S(2)}) collective-permute-start(bf16[2,4,64,1024]{3,2,1,0:T(8,128)(2,1)S(1)} %shard_map.120.refs_2_), channel_id=1, source_target_pairs={{0,96},{32,0},{64,32},{96,64},{1,97},{33,1},{65,33},{97,65},{2,98}... | collective-permute-start | bytes 3145736 | tf_op jit(solution)/shard_map/ppermute | solution.py:34
  126.5 6.2 %shard_map.116 = (bf16[4,1024,128]{2,1,0:T(8,128)(2,1)S(1)}, bf16[2,1024,128]{2,1,0:T(8,128)(2,1)S(1)}) custom-call(s32[51]{0:T(128)S(1)} %copy-done.16, bf16[512,2048]{1,0:T(8,128)(2,1)} %fusion.2.refs_0_, bf16[512,2048]{1,0:T(8,128)(2,1)} %collective-permute-done.9.refs_1_, bf16[4,2,64,512]{3,2,1,0:T(8,128)(2,1)S(1)} %shard_map.115.refs_2_, ...), custom_call_target="tpu_custom_call" | custom-call | flops 2147483648 | bytes 8388608 | tf_op jit(solution)/shard_map/pallas_call | solution.py:239
  134.8 6.2 %shard_map.117 = (bf16[4,1024,128]{2,1,0:T(8,128)(2,1)S(1)}, bf16[2,1024,128]{2,1,0:T(8,128)(2,1)S(1)}) custom-call(s32[51]{0:T(128)S(1)} %copy-done.18, bf16[512,2048]{1,0:T(8,128)(2,1)} %collective-permute-done.1.refs_0_, bf16[512,2048]{1,0:T(8,128)(2,1)} %collective-permute-done.2.refs_1_, bf16[4,2,64,512]{3,2,1,0:T(8,128)(2,1)S(1)} %shard_map.115.refs_2_, ...), custom_call_target="tpu_custom_call" | custom-call | flops 2147483648 | bytes 8388608 | tf_op jit(solution)/shard_map/pallas_call | solution.py:239
  143.0 3.8 %collective-permute-start.7 = (bf16[2,4,64,512]{3,2,1,0:T(8,128)(2,1)S(1)}, bf16[2,4,64,512]{3,2,1,0:T(8,128)(2,1)S(1)}, u32[]{:S(2)}, u32[]{:S(2)}) collective-permute-start(bf16[2,4,64,512]{3,2,1,0:T(8,128)(2,1)S(1)} %shard_map.113.refs_2_), channel_id=1, source_target_pairs={{0,64},{32,96},{64,0},{96,32},{1,65},{33,97},{65,1},{97,33},{2,66}... | collective-permute-start | bytes 1572872 | tf_op jit(solution)/shard_map/ppermute | solution.py:34
  146.8 13.8 %collective-permute-done.7.refs_4_ = bf16[2,4,64,512]{3,2,1,0:T(8,128)(2,1)S(1)} collective-permute-done((bf16[2,4,64,512]{3,2,1,0:T(8,128)(2,1)S(1)}, bf16[2,4,64,512]{3,2,1,0:T(8,128)(2,1)S(1)}, u32[]{:S(2)}, u32[]{:S(2)}) %collective-permute-start.7) | collective-permute-done | bytes 524320 | tf_op jit(solution)/shard_map/ppermute | solution.py:34
  160.6 38.5 %collective-permute-start.25 = (bf16[2,4,64,1024]{3,2,1,0:T(8,128)(2,1)S(1)}, bf16[2,4,64,1024]{3,2,1,0:T(8,128)(2,1)S(1)}, u32[]{:S(2)}, u32[]{:S(2)}) collective-permute-start(bf16[2,4,64,1024]{3,2,1,0:T(8,128)(2,1)S(1)} %shard_map.120.refs_2_), channel_id=1, source_target_pairs={{0,32},{32,64},{64,96},{96,0},{1,33},{33,65},{65,97},{97,1},{2,34}... | collective-permute-start | bytes 3145736 | tf_op jit(solution)/shard_map/ppermute | solution.py:34
  199.9 5.8 %shard_map.114.q_ref = bf16[1024,512]{1,0:T(8,128)(2,1)S(1)} custom-call(s32[51]{0:T(128)S(1)} %copy-done.16, bf16[512,2048]{1,0:T(8,128)(2,1)} %collective-permute-done.1.refs_0_, bf16[512,2048]{1,0:T(8,128)(2,1)} %collective-permute-done.2.refs_1_, bf16[2,4,64,512]{3,2,1,0:T(8,128)(2,1)S(1)} %shard_map.113.refs_2_, ...), custom_call_target="tpu_custom_call" | custom-call | flops 2147483648 | bytes 8388608 | tf_op jit(solution)/shard_map/pallas_call | solution.py:239
  205.7 10.2 %shard_map.118 = (f32[8,2,8,256]{3,2,1,0:T(8,128)S(1)}, f32[8,2,8,256]{3,2,1,0:T(8,128)S(1)}, f32[8,2,128,256]{3,2,1,0:T(8,128)S(1)}) custom-call(s32[51]{0:T(128)S(1)} %copy-done.16, bf16[1024,512]{1,0:T(8,128)(2,1)S(1)} %shard_map.114.q_ref, bf16[4,1024,128]{2,1,0:T(8,128)(2,1)S(1)} %get-tuple-element.25.own0.refs_0_, ...), custom_call_target="tpu_custom_call" | custom-call | flops 2147483648 | bytes 6291456 | tf_op jit(solution)/shard_map/pallas_call | solution.py:433
  215.9 4.1 %shard_map.119 = bf16[1024,512]{1,0:T(8,128)(2,1)S(1)} custom-call(s32[51]{0:T(128)S(1)} %copy-done.16, bf16[1024,512]{1,0:T(8,128)(2,1)S(1)} %shard_map.114.q_ref, bf16[4,1024,128]{2,1,0:T(8,128)(2,1)S(1)} %collective-permute-done.16.halo0, bf16[4,1024,128]{2,1,0:T(8,128)(2,1)S(1)} %collective-permute-done.17.halo1, ...), custom_call_target="tpu_custom_call" | custom-call | flops 2147483648 | bytes 6291456 | tf_op jit(solution)/shard_map/pallas_call | solution.py:433
  220.0 6.2 %collective-permute-start.18 = (bf16[1024,512]{1,0:T(8,128)(2,1)S(1)}, bf16[1024,512]{1,0:T(8,128)(2,1)S(1)}, u32[]{:S(2)}, u32[]{:S(2)}) collective-permute-start(bf16[1024,512]{1,0:T(8,128)(2,1)S(1)} %shard_map.119), channel_id=1, source_target_pairs={{0,1},{1,0},{2,3},{3,2},{4,5},{5,4},{6,7},{7,6},{8,9},{9,8},{10,11... | collective-permute-start | bytes 3145736 | tf_op jit(solution)/shard_map/ppermute | solution.py:30
  229.1 31.9 %collective-permute-done.31.refs_1_ = bf16[512,512]{1,0:T(8,128)(2,1)S(1)} collective-permute-done((bf16[512,512]{1,0:T(8,128)(2,1)S(1)}, bf16[512,512]{1,0:T(8,128)(2,1)S(1)}, u32[]{:S(2)}, u32[]{:S(2)}) %collective-permute-start.31) | collective-permute-done | bytes 524320 | tf_op jit(solution)/shard_map/ppermute | solution.py:38
  261.6 3.2 %collective-permute-start.33 = (bf16[512,512]{1,0:T(8,128)(2,1)}, bf16[512,512]{1,0:T(8,128)(2,1)}, u32[]{:S(2)}, u32[]{:S(2)}) collective-permute-start(bf16[512,512]{1,0:T(8,128)(2,1)} %get-tuple-element.36), channel_id=1, source_target_pairs={{0,3},{1,2},{2,1},{3,0},{4,7},{5,6},{6,5},{7,4},{8,11},{9,10},{10,... | collective-permute-start | bytes 1572872 | tf_op jit(solution)/shard_map/ppermute | solution.py:38
  264.8 5.8 %shard_map.121.q_ref = bf16[1024,512]{1,0:T(8,128)(2,1)S(1)} custom-call(s32[51]{0:T(128)S(1)} %copy-done.16, bf16[512,2048]{1,0:T(8,128)(2,1)} %fusion.2.refs_0_, bf16[512,2048]{1,0:T(8,128)(2,1)} %collective-permute-done.9.refs_1_, bf16[2,4,64,512]{3,2,1,0:T(8,128)(2,1)S(1)} %shard_map.113.refs_2_, ...), custom_call_target="tpu_custom_call" | custom-call | flops 2147483648 | bytes 8388608 | tf_op jit(solution)/shard_map/pallas_call | solution.py:239
  270.6 17.0 %shard_map.122.refs_0_ = bf16[1024,512]{1,0:T(8,128)(2,1)S(1)} custom-call(s32[51]{0:T(128)S(1)} %copy-done.16, bf16[1024,512]{1,0:T(8,128)(2,1)S(1)} %shard_map.121.q_ref, bf16[4,1024,128]{2,1,0:T(8,128)(2,1)S(1)} %copy-done.1, bf16[4,1024,128]{2,1,0:T(8,128)(2,1)S(1)} %copy-done.3, bf16[4,1024,128]{2,1,0:T(8,128)(2,1)S(1)} %copy-done.20, ...), custom_call_target="tpu_custom_call" | custom-call | flops 2147483648 | bytes 6291456 | tf_op jit(solution)/shard_map/pallas_call | solution.py:433
  288.4 3.6 %unpack_pages.1 = (bf16[512,1024]{1,0:T(8,128)(2,1)}, bf16[512,1024]{1,0:T(8,128)(2,1)}) custom-call(s32[51]{0:T(128)S(1)} %copy-done.16, bf16[512,512]{1,0:T(8,128)(2,1)S(1)} %get-tuple-element.33.refs_0_, bf16[512,512]{1,0:T(8,128)(2,1)S(1)} %collective-permute-done.31.refs_1_, bf16[512,512]{1,0:T(8,128)(2,1)} %collective-permute-done.32.refs_2_, ...), custom_call_target="tpu_custom_call" | custom-call | tf_op jit(solution)/shard_map/unpack_pages/pallas_call | solution.py:528
  292.0 3.3 %output_near.1.refs_10_ = f32[2,512,1024]{2,1,0:T(8,128)S(1)} custom-call(s32[51]{0:T(128)S(1)} %copy-done.16, bf16[1024,512]{1,0:T(8,128)(2,1)S(1)} %shard_map.122.refs_0_, bf16[512,512]{1,0:T(8,128)(2,1)S(1)} %collective-permute-done.30.refs_1_, bf16[2,4,64,1024]{3,2,1,0:T(8,128)(2,1)S(1)} %shard_map.120.refs_2_, ...), custom_call_target="tpu_custom_call" | custom-call | tf_op jit(solution)/shard_map/output_near/pallas_call | solution.py:584
  295.4 4.6 %output_far.1 = bf16[512,2048]{1,0:T(8,128)(2,1)} custom-call(s32[51]{0:T(128)S(1)} %copy-done.16, bf16[1024,512]{1,0:T(8,128)(2,1)S(1)} %collective-permute-done.18.refs_0_, bf16[512,512]{1,0:T(8,128)(2,1)S(1)} %collective-permute-done.19.refs_1_, bf16[2,4,64,1024]{3,2,1,0:T(8,128)(2,1)S(1)} %shard_map.120.refs_2_, ...), custom_call_target="tpu_custom_call" | custom-call | tf_op jit(solution)/shard_map/output_far/pallas_call | solution.py:600
  (145 shorter events, 55.7 us)
Async XLA Ops:
  3.8 13.7 %all-to-all-start = ((bf16[8,16,2048]{2,1,0:T(8,128)(2,1)}), bf16[8,16,2048]{2,1,0:T(8,128)(2,1)S(1)}, u32[]{:S(2)}, u32[]{:S(2)}) async-start(bf16[8,16,2048]{2,1,0:T(8,128)(2,1)} %role_slices.1), calls=%async_computation | async-start | bytes 1048576 | tf_op jit(solution)/shard_map/all_to_all | solution.py:656
  17.4 49.3 %collective-permute-start.1 = (bf16[512,2048]{1,0:T(8,128)(2,1)}, bf16[512,2048]{1,0:T(8,128)(2,1)}, u32[]{:S(2)}, u32[]{:S(2)}) collective-permute-start(bf16[512,2048]{1,0:T(8,128)(2,1)} %fusion.2.refs_0_), channel_id=1, source_target_pairs={{0,1},{1,0},{2,3},{3,2},{4,5},{5,4},{6,7},{7,6},{8,9},{9,8},{10,11... | collective-permute-start | bytes 6291464 | tf_op jit(solution)/shard_map/ppermute | solution.py:30
  18.4 108.1 %collective-permute-start.9 = (bf16[512,2048]{1,0:T(8,128)(2,1)}, bf16[512,2048]{1,0:T(8,128)(2,1)}, u32[]{:S(2)}, u32[]{:S(2)}) collective-permute-start(bf16[512,2048]{1,0:T(8,128)(2,1)} %fusion.2.refs_0_), channel_id=1, source_target_pairs={{0,2},{2,0},{1,3},{3,1},{4,6},{6,4},{5,7},{7,5},{8,10},{10,8},{9,1... | collective-permute-start | bytes 6291464 | tf_op jit(solution)/shard_map/ppermute | solution.py:30
  19.6 57.5 %collective-permute-start = (s32[8]{0:T(128)S(1)}, s32[8]{0:T(128)S(1)}, u32[]{:S(2)}, u32[]{:S(2)}) collective-permute-start(s32[8]{0:T(128)S(1)} %copy-done.25), channel_id=1, source_target_pairs={{0,2},{2,0},{1,3},{3,1},{4,6},{6,4},{5,7},{7,5},{8,10},{10,8},{9,1... | collective-permute-start | bytes 104 | tf_op jit(solution)/shard_map/ppermute | solution.py:30
  66.7 68.1 %collective-permute-start.2 = (bf16[512,2048]{1,0:T(8,128)(2,1)}, bf16[512,2048]{1,0:T(8,128)(2,1)}, u32[]{:S(2)}, u32[]{:S(2)}) collective-permute-start(bf16[512,2048]{1,0:T(8,128)(2,1)} %collective-permute-done.1.refs_0_), channel_id=1, source_target_pairs={{0,2},{2,0},{1,3},{3,1},{4,6},{6,4},{5,7},{7,5},{8,10},{10,8},{9,1... | collective-permute-start | bytes 6291464 | tf_op jit(solution)/shard_map/ppermute | solution.py:30
  97.9 17.6 %collective-permute-start.13 = (bf16[4,2,64,512]{3,2,1,0:T(8,128)(2,1)S(1)}, bf16[4,2,64,512]{3,2,1,0:T(8,128)(2,1)S(1)}, u32[]{:S(2)}, u32[]{:S(2)}) collective-permute-start(bf16[4,2,64,512]{3,2,1,0:T(8,128)(2,1)S(1)} %shard_map.115.refs_2_), channel_id=1, source_target_pairs={{0,4},{4,8},{8,12},{12,0},{1,5},{5,9},{9,13},{13,1},{2,6},{6,10},{... | collective-permute-start | bytes 1572872 | tf_op jit(solution)/shard_map/ppermute | solution.py:34
  99.3 20.9 %collective-permute-start.14 = (bf16[4,2,64,512]{3,2,1,0:T(8,128)(2,1)S(1)}, bf16[4,2,64,512]{3,2,1,0:T(8,128)(2,1)}, u32[]{:S(2)}, u32[]{:S(2)}) collective-permute-start(bf16[4,2,64,512]{3,2,1,0:T(8,128)(2,1)S(1)} %shard_map.115.refs_2_), channel_id=1, source_target_pairs={{0,8},{4,12},{8,0},{12,4},{1,9},{5,13},{9,1},{13,5},{2,10},{6,14},... | collective-permute-start | bytes 1572872 | tf_op jit(solution)/shard_map/ppermute | solution.py:34
  102.6 23.8 %collective-permute-start.15 = (bf16[4,2,64,512]{3,2,1,0:T(8,128)(2,1)S(1)}, bf16[4,2,64,512]{3,2,1,0:T(8,128)(2,1)}, u32[]{:S(2)}, u32[]{:S(2)}) collective-permute-start(bf16[4,2,64,512]{3,2,1,0:T(8,128)(2,1)S(1)} %shard_map.115.refs_2_), channel_id=1, source_target_pairs={{0,12},{4,0},{8,4},{12,8},{1,13},{5,1},{9,5},{13,9},{2,14},{6,2},{... | collective-permute-start | bytes 1572872 | tf_op jit(solution)/shard_map/ppermute | solution.py:34
  115.4 31.3 %collective-permute-start.6 = (bf16[2,4,64,512]{3,2,1,0:T(8,128)(2,1)S(1)}, bf16[2,4,64,512]{3,2,1,0:T(8,128)(2,1)S(1)}, u32[]{:S(2)}, u32[]{:S(2)}) collective-permute-start(bf16[2,4,64,512]{3,2,1,0:T(8,128)(2,1)S(1)} %shard_map.113.refs_2_), channel_id=1, source_target_pairs={{0,32},{32,64},{64,96},{96,0},{1,33},{33,65},{65,97},{97,1},{2,34}... | collective-permute-start | bytes 1572872 | tf_op jit(solution)/shard_map/ppermute | solution.py:34
  120.2 79.7 %collective-permute-start.23 = (bf16[2,4,64,1024]{3,2,1,0:T(8,128)(2,1)S(1)}, bf16[2,4,64,1024]{3,2,1,0:T(8,128)(2,1)S(1)}, u32[]{:S(2)}, u32[]{:S(2)}) collective-permute-start(bf16[2,4,64,1024]{3,2,1,0:T(8,128)(2,1)S(1)} %shard_map.120.refs_2_), channel_id=1, source_target_pairs={{0,96},{32,0},{64,32},{96,64},{1,97},{33,1},{65,33},{97,65},{2,98}... | collective-permute-start | bytes 3145736 | tf_op jit(solution)/shard_map/ppermute | solution.py:34
  132.7 83.2 %collective-permute-start.16 = (bf16[4,1024,128]{2,1,0:T(8,128)(2,1)S(1)}, bf16[4,1024,128]{2,1,0:T(8,128)(2,1)S(1)}, u32[]{:S(2)}, u32[]{:S(2)}) collective-permute-start(bf16[4,1024,128]{2,1,0:T(8,128)(2,1)S(1)} %get-tuple-element.25.own0.refs_0_), channel_id=1, source_target_pairs={{0,4},{1,5},{2,6},{3,7},{4,8},{5,9},{6,10},{7,11},{8,12},{9,13},{1... | collective-permute-start | bytes 3145736 | tf_op jit(solution)/shard_map/ppermute | solution.py:631
  141.0 74.8 %collective-permute-start.17 = (bf16[4,1024,128]{2,1,0:T(8,128)(2,1)S(1)}, bf16[4,1024,128]{2,1,0:T(8,128)(2,1)S(1)}, u32[]{:S(2)}, u32[]{:S(2)}) collective-permute-start(bf16[4,1024,128]{2,1,0:T(8,128)(2,1)S(1)} %get-tuple-element.26.own1.refs_1_), channel_id=1, source_target_pairs={{0,4},{1,5},{2,6},{3,7},{4,8},{5,9},{6,10},{7,11},{8,12},{9,13},{1... | collective-permute-start | bytes 3145736 | tf_op jit(solution)/shard_map/ppermute | solution.py:631
  143.0 17.6 %collective-permute-start.7 = (bf16[2,4,64,512]{3,2,1,0:T(8,128)(2,1)S(1)}, bf16[2,4,64,512]{3,2,1,0:T(8,128)(2,1)S(1)}, u32[]{:S(2)}, u32[]{:S(2)}) collective-permute-start(bf16[2,4,64,512]{3,2,1,0:T(8,128)(2,1)S(1)} %shard_map.113.refs_2_), channel_id=1, source_target_pairs={{0,64},{32,96},{64,0},{96,32},{1,65},{33,97},{65,1},{97,33},{2,66}... | collective-permute-start | bytes 1572872 | tf_op jit(solution)/shard_map/ppermute | solution.py:34
  146.8 52.3 %collective-permute-start.8 = (bf16[2,4,64,512]{3,2,1,0:T(8,128)(2,1)S(1)}, bf16[2,4,64,512]{3,2,1,0:T(8,128)(2,1)S(1)}, u32[]{:S(2)}, u32[]{:S(2)}) collective-permute-start(bf16[2,4,64,512]{3,2,1,0:T(8,128)(2,1)S(1)} %shard_map.113.refs_2_), channel_id=1, source_target_pairs={{0,96},{32,0},{64,32},{96,64},{1,97},{33,1},{65,33},{97,65},{2,98}... | collective-permute-start | bytes 1572872 | tf_op jit(solution)/shard_map/ppermute | solution.py:34
  160.6 67.7 %collective-permute-start.25 = (bf16[2,4,64,1024]{3,2,1,0:T(8,128)(2,1)S(1)}, bf16[2,4,64,1024]{3,2,1,0:T(8,128)(2,1)S(1)}, u32[]{:S(2)}, u32[]{:S(2)}) collective-permute-start(bf16[2,4,64,1024]{3,2,1,0:T(8,128)(2,1)S(1)} %shard_map.120.refs_2_), channel_id=1, source_target_pairs={{0,32},{32,64},{64,96},{96,0},{1,33},{33,65},{65,97},{97,1},{2,34}... | collective-permute-start | bytes 3145736 | tf_op jit(solution)/shard_map/ppermute | solution.py:34
  199.1 29.5 %collective-permute-start.26 = (bf16[2,4,64,1024]{3,2,1,0:T(8,128)(2,1)S(1)}, bf16[2,4,64,1024]{3,2,1,0:T(8,128)(2,1)S(1)}, u32[]{:S(2)}, u32[]{:S(2)}) collective-permute-start(bf16[2,4,64,1024]{3,2,1,0:T(8,128)(2,1)S(1)} %shard_map.120.refs_2_), channel_id=1, source_target_pairs={{0,2},{2,0},{1,3},{3,1},{4,6},{6,4},{5,7},{7,5},{8,10},{10,8},{9,1... | collective-permute-start | bytes 3145736 | tf_op jit(solution)/shard_map/ppermute | solution.py:30
  199.9 29.0 %collective-permute-start.24 = (bf16[2,4,64,1024]{3,2,1,0:T(8,128)(2,1)S(1)}, bf16[2,4,64,1024]{3,2,1,0:T(8,128)(2,1)S(1)}, u32[]{:S(2)}, u32[]{:S(2)}) collective-permute-start(bf16[2,4,64,1024]{3,2,1,0:T(8,128)(2,1)S(1)} %collective-permute-done.23.refs_3_), channel_id=1, source_target_pairs={{0,96},{32,0},{64,32},{96,64},{1,97},{33,1},{65,33},{97,65},{2,98}... | collective-permute-start | bytes 3145736 | tf_op jit(solution)/shard_map/ppermute | solution.py:34
  220.0 41.6 %collective-permute-start.18 = (bf16[1024,512]{1,0:T(8,128)(2,1)S(1)}, bf16[1024,512]{1,0:T(8,128)(2,1)S(1)}, u32[]{:S(2)}, u32[]{:S(2)}) collective-permute-start(bf16[1024,512]{1,0:T(8,128)(2,1)S(1)} %shard_map.119), channel_id=1, source_target_pairs={{0,1},{1,0},{2,3},{3,2},{4,5},{5,4},{6,7},{7,6},{8,9},{9,8},{10,11... | collective-permute-start | bytes 3145736 | tf_op jit(solution)/shard_map/ppermute | solution.py:30
  228.3 32.8 %collective-permute-start.31 = (bf16[512,512]{1,0:T(8,128)(2,1)S(1)}, bf16[512,512]{1,0:T(8,128)(2,1)S(1)}, u32[]{:S(2)}, u32[]{:S(2)}) collective-permute-start(bf16[512,512]{1,0:T(8,128)(2,1)S(1)} %get-tuple-element.34), channel_id=1, source_target_pairs={{0,1},{1,0},{2,3},{3,2},{4,5},{5,4},{6,7},{7,6},{8,9},{9,8},{10,11... | collective-permute-start | bytes 1572872 | tf_op jit(solution)/shard_map/ppermute | solution.py:38
  228.3 63.7 %collective-permute-start.27 = (bf16[2,4,64,1024]{3,2,1,0:T(8,128)(2,1)S(1)}, bf16[2,4,64,1024]{3,2,1,0:T(8,128)(2,1)S(1)}, u32[]{:S(2)}, u32[]{:S(2)}) collective-permute-start(bf16[2,4,64,1024]{3,2,1,0:T(8,128)(2,1)S(1)} %collective-permute-done.23.refs_3_), channel_id=1, source_target_pairs={{0,2},{2,0},{1,3},{3,1},{4,6},{6,4},{5,7},{7,5},{8,10},{10,8},{9,1... | collective-permute-start | bytes 3145736 | tf_op jit(solution)/shard_map/ppermute | solution.py:30
  228.6 63.5 %collective-permute-start.29 = (bf16[2,4,64,1024]{3,2,1,0:T(8,128)(2,1)S(1)}, bf16[2,4,64,1024]{3,2,1,0:T(8,128)(2,1)S(1)}, u32[]{:S(2)}, u32[]{:S(2)}) collective-permute-start(bf16[2,4,64,1024]{3,2,1,0:T(8,128)(2,1)S(1)} %collective-permute-done.25.refs_5_), channel_id=1, source_target_pairs={{0,2},{2,0},{1,3},{3,1},{4,6},{6,4},{5,7},{7,5},{8,10},{10,8},{9,1... | collective-permute-start | bytes 3145736 | tf_op jit(solution)/shard_map/ppermute | solution.py:30
  228.8 63.2 %collective-permute-start.28 = (bf16[2,4,64,1024]{3,2,1,0:T(8,128)(2,1)S(1)}, bf16[2,4,64,1024]{3,2,1,0:T(8,128)(2,1)S(1)}, u32[]{:S(2)}, u32[]{:S(2)}) collective-permute-start(bf16[2,4,64,1024]{3,2,1,0:T(8,128)(2,1)S(1)} %collective-permute-done.24.refs_4_), channel_id=1, source_target_pairs={{0,2},{2,0},{1,3},{3,1},{4,6},{6,4},{5,7},{7,5},{8,10},{10,8},{9,1... | collective-permute-start | bytes 3145736 | tf_op jit(solution)/shard_map/ppermute | solution.py:30
  261.0 26.7 %collective-permute-start.32 = (bf16[512,512]{1,0:T(8,128)(2,1)}, bf16[512,512]{1,0:T(8,128)(2,1)}, u32[]{:S(2)}, u32[]{:S(2)}) collective-permute-start(bf16[512,512]{1,0:T(8,128)(2,1)} %get-tuple-element.35), channel_id=1, source_target_pairs={{0,2},{1,3},{2,0},{3,1},{4,6},{5,7},{6,4},{7,5},{8,10},{9,11},{10,... | collective-permute-start | bytes 1572872 | tf_op jit(solution)/shard_map/ppermute | solution.py:38
  261.6 26.7 %collective-permute-start.33 = (bf16[512,512]{1,0:T(8,128)(2,1)}, bf16[512,512]{1,0:T(8,128)(2,1)}, u32[]{:S(2)}, u32[]{:S(2)}) collective-permute-start(bf16[512,512]{1,0:T(8,128)(2,1)} %get-tuple-element.36), channel_id=1, source_target_pairs={{0,3},{1,2},{2,1},{3,0},{4,7},{5,6},{6,5},{7,4},{8,11},{9,10},{10,... | collective-permute-start | bytes 1572872 | tf_op jit(solution)/shard_map/ppermute | solution.py:38
  (40 other events, 471.8 us)
